TPU v7x, 128 devices: a whole 4x4x4 slice. The times are simulated.
128 devices in a mesh: section: 4 (over y_lo, core), seq: 32 (over y_hi, z, x).
Axes of the slice: x: 4, y: 4 (y_hi: 2, y_lo: 2; y = y_hi * 2 + y_lo), z: 4, core: 2. Of those that a mesh axis runs over, the one named last changes fastest.
Arguments:
- context: bfloat16 [8192, 8192], P('seq'), may hold values from -24 to 24, as said below
- memory: bfloat16 [2048, 8192], P('seq'), may hold values from -24 to 24, as said below
- query_weight: bfloat16 [8192, 4096], P(None, 'section'), may hold values from -0.0625 to 0.0625
- key_weight: bfloat16 [8192, 512], P('seq', 'section'), may hold values from -0.0625 to 0.0625
- value_weight: bfloat16 [8192, 512], P('seq', 'section'), may hold values from -0.0625 to 0.0625
- query_down_map: bfloat16 [8192, 128], replicated, may hold values from -0.0625 to 0.0625
- query_up_map: bfloat16 [128, 4096], P(None, 'section'), may hold values from -0.5 to 0.5
- value_down_map: bfloat16 [8192, 128], P('seq'), may hold values from -0.0625 to 0.0625
- value_up_map: bfloat16 [128, 512], P(None, 'section'), may hold values from -0.5 to 0.5
- output_weight: bfloat16 [4096, 8192], P('section', 'seq'), may hold values from -1 to 1
- decoder_gain: float32 [8192], P('seq'), may hold values from 0.25 to 1.75
- document_slots: int32 [8], replicated, may hold values from 1 to 1088, 2048 in all
- normed_gradient: bfloat16 [2048, 8192], P('section', 'seq'), may hold values from -6 to 6
Outputs:
- normed: bfloat16 [2048, 8192], P('section', 'seq')
- grad_qa: float32 [8192, 128], P(('section', 'seq'))
- grad_va: float32 [8192, 128], P(('section', 'seq'))
- query_up_gradient: float32 [128, 4096], P(None, 'section')
- value_up_gradient: float32 [128, 512], P(None, 'section')
Inputs may be any that keep to these rules, and one draw needn't show every extreme that they name: `context`: values of the normed inputs lie in this range. `memory`: values of the normed inputs lie in this range. Documents lie end to end in order; document d has document_slots[d] memory slots and 4 document_slots[d] context tokens; the counts sum to 2048.
All inputs are finite; a program needn't handle non-finite values.
Results may differ from a plain program's by a relative error of at most 0.014.
The roundings to bfloat16 on the way count: a program that leaves them out, or rounds other values in their place, can miss the bound.
Values may be sent and summed in bfloat16 or wider, within the bound.
A program may use at most 192 MiB of HBM per device.

v0:
```python
import jax
import jax.numpy as jnp
from jax import lax
from jax.sharding import PartitionSpec as P

MODEL_DIM = 8192


adapter_scale = 0.25
epsilon = 1e-05
mask_fill = -1e30


def side_by_side(arrays, axis, dim, along):
    both = jnp.concatenate(arrays, axis=along)
    filled, at, finished = (lax.all_gather(both, axis, axis=dim, tiled=True), 0, [])
    for a in arrays:
        finished.append(lax.slice_in_dim(filled, at, at + a.shape[along], axis=along))
        at += a.shape[along]
    return tuple(finished)


def split_up(value, dim, count):
    shape = value.shape
    pieces = value.reshape(*shape[:dim], count, shape[dim] // count, *shape[dim + 1 :])
    return jnp.moveaxis(pieces, dim, 0)


def summed_on_arrival(value, axis, dim):
    count = lax.axis_size(axis)
    pieces = lax.all_to_all(split_up(value, dim, count), axis, 0, 0, tiled=True)
    return jnp.sum(pieces, axis=0)


def sent_to_all(value, axis):
    count = lax.axis_size(axis)
    return lax.all_to_all(
        jnp.broadcast_to(value[None], (count, *value.shape)), axis, 0, 0, tiled=True
    )


def of_everyone(value, axis):
    everything = sent_to_all(value, axis)
    return jnp.sum(everything, axis=0)


def in_one(arrays, axis):
    flat, at, finished = (jnp.concatenate([a.reshape(-1) for a in arrays]), 0, [])
    subtotal = of_everyone(flat, axis)
    for a in arrays:
        finished.append(subtotal[at : at + a.size].reshape(a.shape))
        at += a.size
    return tuple(finished)


def in_order(pieces, dim):
    shape = list(pieces.shape[1:])
    shape[dim] *= pieces.shape[0]
    return jnp.moveaxis(pieces, 0, dim).reshape(shape)


def gather_directly(value, axis, dim):
    return in_order(sent_to_all(value, axis), dim)


def rows_for(lines, count):
    spare = -lines.shape[0] % count
    if not spare:
        return lines
    return jnp.concatenate([lines, jnp.zeros((spare, *lines.shape[1:]), lines.dtype)])


def nested_sum(value, axes):
    own = summed_on_arrival(rows_for(value, lax.axis_size(axes)), axes, 0)
    whole = gather_directly(own, axes, 0)
    return whole[: len(value)].reshape(value.shape)


def in_one_2(arrays, axis):
    flat, at, finished = (jnp.concatenate([a.reshape(-1) for a in arrays]), 0, [])
    subtotal = nested_sum(flat, axis)
    for a in arrays:
        finished.append(subtotal[at : at + a.size].reshape(a.shape))
        at += a.size
    return tuple(finished)


def sent_together(arrays, axis, dim, along):
    widths = [a.shape[along] for a in arrays]
    both = jnp.concatenate(arrays, axis=along)
    filled = lax.psum_scatter(both, axis, scatter_dimension=dim, tiled=True)
    return tuple(jnp.split(filled, [sum(widths[:k]) for k in range(1, len(widths))], axis=along))


def doc_index(units, doc_ends):
    return jnp.sum((units[:, None] >= doc_ends[None, :]).astype(jnp.int32), axis=1)


def leading_contract(left, right):
    return lax.dot_general(
        left, right, (((0,), (0,)), ((), ())), preferred_element_type=jnp.float32
    )


def trailing_contract(left, right):
    return lax.dot_general(
        left, right, (((1,), (1,)), ((), ())), preferred_element_type=jnp.float32
    )


def body(
    context,
    memory,
    query_weight,
    key_weight,
    value_weight,
    query_down_map,
    query_up_map,
    value_down_map,
    value_up_map,
    output_weight,
    decoder_gain,
    document_slots,
    normed_gradient,
):
    tok_dev = context.shape[0]
    slot_dev = memory.shape[0]
    keys_dev = tok_dev + slot_dev
    seq_size = lax.axis_size("seq")
    seq_index = lax.axis_index("seq")
    section_extent = lax.axis_size("section")
    head_dim = key_weight.shape[1]
    group_heads = query_weight.shape[1] // head_dim
    every_row = jnp.concatenate([context, memory], axis=0)
    key_portion, value_fragment, adapter_portion = side_by_side(
        (key_weight, value_weight, value_down_map), "seq", 0, 1
    )
    combined_rows = jnp.concatenate([key_portion, value_fragment, adapter_portion], axis=1)
    projected = jnp.dot(every_row, combined_rows, preferred_element_type=jnp.float32)
    query_reduced = jnp.dot(memory, query_down_map, preferred_element_type=jnp.float32).astype(
        jnp.bfloat16
    )
    value_reduced = projected[:, 2 * head_dim :].astype(jnp.bfloat16)
    query_rows_out = (
        jnp.dot(memory, query_weight, preferred_element_type=jnp.float32)
        + adapter_scale * jnp.dot(query_reduced, query_up_map, preferred_element_type=jnp.float32)
    ).astype(jnp.bfloat16)
    keys_local = projected[:, :head_dim].astype(jnp.bfloat16)
    values_local = (
        projected[:, head_dim : 2 * head_dim]
        + adapter_scale * jnp.dot(value_reduced, value_up_map, preferred_element_type=jnp.float32)
    ).astype(jnp.bfloat16)
    keys_all, value_rows_all = side_by_side((keys_local, values_local), "seq", 0, 1)
    key_rank = jnp.arange(seq_size * keys_dev, dtype=jnp.int32)
    key_owner = key_rank // keys_dev
    owner_valid = jnp.ones(key_rank.shape, dtype=bool)
    doc_ends = jnp.cumsum(document_slots)
    offset = key_rank % keys_dev
    is_context = offset < tok_dev
    key_unit = jnp.where(
        is_context, (key_owner * tok_dev + offset) // 4, key_owner * slot_dev + offset - tok_dev
    )
    key_doc = doc_index(key_unit, doc_ends)
    slot_unit = seq_index * slot_dev + jnp.arange(slot_dev, dtype=jnp.int32)
    row_unit = jnp.repeat(slot_unit, group_heads)
    row_doc = doc_index(row_unit, doc_ends)
    allowed = (
        (key_doc[None, :] == row_doc[:, None])
        & (is_context[None, :] | (key_unit[None, :] <= row_unit[:, None]))
        & owner_valid[None, :]
    )
    score_scale = head_dim ** (-0.5)
    query_rows = query_rows_out.reshape(slot_dev * group_heads, head_dim)
    scores = jnp.where(allowed, trailing_contract(query_rows, keys_all) * score_scale, mask_fill)
    row_top = jnp.max(scores, axis=1, keepdims=True)
    exponent = jnp.exp(scores - row_top)
    probability = exponent / jnp.sum(exponent, axis=1, keepdims=True)
    prob_low = probability.astype(jnp.bfloat16)
    attended = (
        jnp.dot(prob_low, value_rows_all, preferred_element_type=jnp.float32)
        .reshape(slot_dev, group_heads * head_dim)
        .astype(jnp.bfloat16)
    )
    slots_all = lax.all_gather(attended, "seq", axis=0, tiled=True)
    hidden = summed_on_arrival(
        jnp.dot(slots_all, output_weight, preferred_element_type=jnp.float32), "section", 0
    )
    total_slots = slot_dev * seq_size
    weighted = total_slots ** (-0.5) * normed_gradient.astype(jnp.float32) * decoder_gain[None, :]
    square_sum, cross_sum = in_one(
        (jnp.sum(hidden * hidden, axis=1), jnp.sum(weighted * hidden, axis=1)), "seq"
    )
    inv_rms = lax.rsqrt(square_sum / MODEL_DIM + epsilon)
    normed = (hidden * inv_rms[:, None] * decoder_gain[None, :]).astype(jnp.bfloat16)
    d_hidden = (
        inv_rms[:, None] * weighted - hidden * (inv_rms**3 * cross_sum / MODEL_DIM)[:, None]
    ).astype(jnp.bfloat16)
    grads_all = gather_directly(d_hidden, "section", 0)
    d_attended = lax.psum_scatter(
        trailing_contract(grads_all, output_weight), "seq", scatter_dimension=0, tiled=True
    ).astype(jnp.bfloat16)
    grad_rows_local = d_attended.reshape(slot_dev * group_heads, head_dim)
    d_probs = trailing_contract(grad_rows_local, value_rows_all)
    center = jnp.sum(probability * d_probs, axis=1, keepdims=True)
    d_scores = (probability * (d_probs - center)).astype(jnp.bfloat16)
    query_gradient = (
        (score_scale * jnp.dot(d_scores, keys_all, preferred_element_type=jnp.float32))
        .reshape(slot_dev, group_heads * head_dim)
        .astype(jnp.bfloat16)
    )
    value_gradient = lax.psum_scatter(
        leading_contract(prob_low, grad_rows_local), "seq", scatter_dimension=0, tiled=True
    ).astype(jnp.bfloat16)
    query_up_portion = adapter_scale * leading_contract(query_reduced, query_gradient)
    value_up_portion = adapter_scale * leading_contract(value_reduced, value_gradient)
    query_up_gradient, value_up_gradient = in_one_2((query_up_portion, value_up_portion), "seq")
    query_portion = adapter_scale * trailing_contract(query_gradient, query_up_map)
    value_portion = adapter_scale * trailing_contract(value_gradient, value_up_map)
    query_backward, value_backward = in_one((query_portion, value_portion), "section")
    query_backward = query_backward.astype(jnp.bfloat16)
    value_backward = value_backward.astype(jnp.bfloat16)
    model_width = memory.shape[1]
    section_columns = model_width // section_extent
    section_index = lax.axis_index("section")
    memory_cols = lax.dynamic_slice_in_dim(
        memory, section_index * section_columns, section_columns, 1
    )
    row_cols = lax.dynamic_slice_in_dim(
        every_row, section_index * section_columns, section_columns, 1
    )
    grad_qa, grad_va = sent_together(
        (leading_contract(memory_cols, query_backward), leading_contract(row_cols, value_backward)),
        "seq",
        0,
        1,
    )
    return (normed, grad_qa, grad_va, query_up_gradient, value_up_gradient)


def solution(mesh):
    in_specs = (
        P("seq", None),
        P("seq", None),
        P(None, "section"),
        P("seq", "section"),
        P("seq", "section"),
        P(),
        P(None, "section"),
        P("seq", None),
        P(None, "section"),
        P("section", "seq"),
        P("seq"),
        P(),
        P("section", "seq"),
    )
    out_specs = (
        P("section", "seq"),
        P(("section", "seq"), None),
        P(("section", "seq"), None),
        P(None, "section"),
        P(None, "section"),
    )
    return jax.shard_map(body, mesh=mesh, in_specs=in_specs, out_specs=out_specs, check_vma=False)
```

profile of v0, /device:TPU:0, one launch (start us, length us, event | category | flops | bytes accessed | tf_op | source)
XLA Modules:
  0.0 1001.2 jit_solution(3964902990142431977)
XLA Ops:
  7.2 1.8 pad_maximum_fusion.2
  9.1 4.6 constant_dynamic-update-slice_fusion.1
  14.8 91.6 %all-gather.4.cloned.1.call-done = bf16[8192,384]{1,0:T(8,128)(2,1)} async-done(((bf16[256,384]{1,0:T(8,128)(2,1)}), bf16[8192,384]{1,0:T(8,128)(2,1)}) %all-gather.4.cloned.1.call-update) | async-done | bytes 6291472 | tf_op jit(solution)/shard_map/all_gather | solution.py:16
  106.4 6.7 fusion.58
  115.8 8.8 fusion.16
  125.2 73.6 %all-gather.6.cloned.1.call-done = bf16[10240,256]{1,0:T(8,128)(2,1)} async-done(((bf16[320,256]{1,0:T(8,128)(2,1)}), bf16[10240,256]{1,0:T(8,128)(2,1)}) %all-gather.6.cloned.1.call-update) | async-done | bytes 5242896 | tf_op jit(solution)/shard_map/all_gather | solution.py:16
  198.8 9.3 fusion.59
  208.1 3.7 fusion.1
  211.8 7.8 fusion
  219.5 10.6 %fusion.17 = bf16[512,128]{1,0:T(8,128)(2,1)S(1)} fusion(bf16[10240,256]{1,0:T(8,128)(2,1)} %all-gather.6.cloned.1.call-done, f32[512,10240]{1,0:T(8,128)} %fusion), kind=kOutput, calls=%fused_computation.25 | convolution fusion | flops 1347485696 | bytes 23724032 | tf_op jit(solution)/shard_map/dot_general | solution.py:180
  230.9 78.1 %all-gather.8.cloned.1.call-done = bf16[2048,1024]{1,0:T(8,128)(2,1)} async-done(((bf16[64,1024]{1,0:T(8,128)(2,1)}), bf16[2048,1024]{1,0:T(8,128)(2,1)}) %all-gather.8.cloned.1.call-update) | async-done | bytes 4194320 | tf_op jit(solution)/shard_map/all_gather | solution.py:184
  309.1 4.8 fusion.60
  313.8 3.7 all-to-all-start
  317.7 25.6 %all-to-all-done = f32[4,512,256]{2,1,0:T(8,128)S(1)} async-done(((f32[4,512,256]{2,1,0:T(8,128)}), f32[4,512,256]{2,1,0:T(8,128)S(1)}, u32[]{:S(2)}, u32[]{:S(2)}) %all-to-all-start) | async-done | bytes 2097184 | tf_op jit(solution)/shard_map/all_to_all | solution.py:31
  345.6 15.3 %all_to_all.37 = f32[32,1,1024]{2,1,0:T(1,128)S(1)} all-to-all(f32[32,1,1024]{2,1,0:T(1,128)S(1)} %broadcast_in_dim.16), channel_id=1, replica_groups=mesh['section'=4,'seq'=32] {'seq'}, dimensions={0} | all-to-all | bytes 262144 | tf_op jit(solution)/shard_map/all_to_all | solution.py:37
  361.0 1.9 subtract_convert_fusion
  363.0 16.9 %all_to_all.38 = bf16[4,512,256]{2,1,0:T(8,128)(2,1)S(1)} all-to-all(bf16[4,512,256]{2,1,0:T(8,128)(2,1)S(1)} %broadcast_in_dim.17), channel_id=1, replica_groups=mesh['section'=4,'seq'=32] {'section'}, dimensions={0} | all-to-all | bytes 2097152 | tf_op jit(solution)/shard_map/all_to_all | solution.py:37
  379.9 5.6 fusion.61
  385.6 198.2 %reduce-scatter.6.cloned.1.call-done = f32[64,1024]{1,0:T(8,128)} async-done(((f32[2048,1024]{1,0:T(8,128)}), f32[64,1024]{1,0:T(8,128)}) %reduce-scatter.6.cloned.1.call-update) | async-done | bytes 262160 | tf_op jit(solution)/shard_map/reduce_scatter | solution.py:199
  584.8 12.1 %fusion.4 = f32[10240,128]{1,0:T(8,128)} fusion(bf16[512,128]{1,0:T(8,128)(2,1)S(1)} %reshape.208, f32[512,10240]{1,0:T(8,128)} %fusion), kind=kOutput, calls=%fused_computation.8 | convolution fusion | flops 1347420160 | bytes 26345472 | tf_op jit(solution)/shard_map/dot_general | solution.py:100
  597.0 14.6 %multiply_reduce_fusion = (f32[512]{0:T(512)S(1)}, f32[512,10240]{1,0:T(8,128)}) fusion(f32[512,10240]{1,0:T(8,128)} %fusion, bf16[512,128]{1,0:T(8,128)(2,1)S(1)} %reshape.208, bf16[10240,256]{1,0:T(8,128)(2,1)} %all-gather.6.cloned.1.call-done), kind=kOutput, calls=%fused_computation.1 | convolution fusion | flops 1352662528 | bytes 44697600 | tf_op jit(solution)/shard_map/dot_general | solution.py:106
  611.6 16.9 %fusion.27 = bf16[512,128]{1,0:T(8,128)(2,1)S(1)} fusion(bf16[10240,256]{1,0:T(8,128)(2,1)} %all-gather.6.cloned.1.call-done, f32[512,10240]{1,0:T(8,128)} %fusion, f32[512,10240]{1,0:T(8,128)} %get-tuple-element.43, f32[512]{0:T(512)S(1)} %get-tuple-element.42), kind=kOutput, calls=%fused_computation.31 | convolution fusion | flops 1358036992 | bytes 44697600 | tf_op jit(solution)/shard_map/dot_general | solution.py:207
  628.8 158.1 %reduce-scatter.8.cloned.1.call-done = f32[320,128]{1,0:T(8,128)} async-done(((f32[10240,128]{1,0:T(8,128)}), f32[320,128]{1,0:T(8,128)}) %reduce-scatter.8.cloned.1.call-update) | async-done | bytes 163856 | tf_op jit(solution)/shard_map/reduce_scatter | solution.py:211
  789.3 3.5 all-to-all-start.3
  792.9 11.6 %all-to-all-done.3 = f32[4,1,49152]{2,1,0:T(1,128)S(1)} async-done(((f32[4,1,49152]{2,1,0:T(1,128)}), f32[4,1,49152]{2,1,0:T(1,128)S(1)}, u32[]{:S(2)}, u32[]{:S(2)}) %all-to-all-start.3) | async-done | bytes 786464 | tf_op jit(solution)/shard_map/all_to_all | solution.py:37
  805.4 1.8 fusion.13
  807.7 1.9 copy.31
  811.3 18.5 %all_to_all.39 = f32[32,1,4608]{2,1,0:T(1,128)} all-to-all(f32[32,1,4608]{2,1,0:T(1,128)S(1)} %bitcast.45), channel_id=1, replica_groups=mesh['section'=4,'seq'=32] {'seq'}, dimensions={0} | all-to-all | bytes 1179648 | tf_op jit(solution)/shard_map/all_to_all | solution.py:31
  829.8 1.4 reduce_sum.99
  831.5 17.2 %all_to_all.40 = f32[32,1,4608]{2,1,0:T(1,128)S(1)} all-to-all(f32[32,1,4608]{2,1,0:T(1,128)S(1)} %broadcast_in_dim.19), channel_id=1, replica_groups=mesh['section'=4,'seq'=32] {'seq'}, dimensions={0} | all-to-all | bytes 1179648 | tf_op jit(solution)/shard_map/all_to_all | solution.py:37
  849.3 2.3 reduce.3
  853.7 139.2 %reduce-scatter.10.cloned.1.call-done = f32[64,256]{1,0:T(8,128)} async-done(((f32[2048,256]{1,0:T(8,128)}), f32[64,256]{1,0:T(8,128)}) %reduce-scatter.10.cloned.1.call-update) | async-done | bytes 65552
  (79 shorter events, 19.0 us)
Async XLA Ops:
  7.2 107.9 %copy-start = (bf16[8192,128]{1,0:T(8,128)(2,1)S(1)}, bf16[8192,128]{1,0:T(8,128)(2,1)}, u32[]{:S(2)}) copy-start(bf16[8192,128]{1,0:T(8,128)(2,1)} %param.18) | copy-start | bytes 6291460
  7.2 6.5 copy-start.2
  7.2 99.2 %all-gather.4.cloned.1.call-start = ((), (), s32[]{:S(2)}) async-start(), calls=%async_computation.9 | async-start | bytes 6488064 | tf_op jit(solution)/shard_map/all_gather | solution.py:16
  9.1 189.7 %all-gather.6.cloned.1.call-start = ((), (), s32[]{:S(2)}) async-start(), calls=%async_computation.10 | async-start | bytes 5406720 | tf_op jit(solution)/shard_map/all_gather | solution.py:16
  14.8 99.0 %copy-start.9 = (bf16[128,128]{1,0:T(8,128)(2,1)S(1)}, bf16[128,128]{1,0:T(8,128)(2,1)}, u32[]{:S(2)}) copy-start(bf16[128,128]{1,0:T(8,128)(2,1)} %param.21) | copy-start | bytes 98308
  14.8 100.8 %copy-start.4 = (bf16[128,1024]{1,0:T(8,128)(2,1)S(1)}, bf16[128,1024]{1,0:T(8,128)(2,1)}, u32[]{:S(2)}) copy-start(bf16[128,1024]{1,0:T(8,128)(2,1)} %param.19) | copy-start | bytes 786436
  113.1 0.7 copy-start.8
  114.6 194.4 %all-gather.8.cloned.1.call-start = ((), (), s32[]{:S(2)}) async-start(), calls=%async_computation.11 | async-start | bytes 4325376 | tf_op jit(solution)/shard_map/all_gather | solution.py:184
  115.8 8.9 copy-start.11
  219.5 89.5 %copy-start.7 = (bf16[1024,256]{1,0:T(8,128)(2,1)S(1)}, bf16[1024,256]{1,0:T(8,128)(2,1)}, u32[]{:S(2)}) copy-start(bf16[1024,256]{1,0:T(8,128)(2,1)} %param.22) | copy-start | bytes 1572868
  230.9 86.7 %copy-start.10 = (f32[256]{0:T(256)S(1)}, f32[256]{0:T(256)}, u32[]{:S(2)}) copy-start(f32[256]{0:T(256)} %param.23) | copy-start | bytes 3076
  313.8 30.4 %copy-start.3 = (bf16[512,256]{1,0:T(8,128)(2,1)S(1)}, bf16[512,256]{1,0:T(8,128)(2,1)}, u32[]{:S(2)}) copy-start(bf16[512,256]{1,0:T(8,128)(2,1)} %param.25) | copy-start | bytes 786436
  313.8 29.4 %all-to-all-start = ((f32[4,512,256]{2,1,0:T(8,128)}), f32[4,512,256]{2,1,0:T(8,128)S(1)}, u32[]{:S(2)}, u32[]{:S(2)}) async-start(f32[4,512,256]{2,1,0:T(8,128)} %bitcast.46), calls=%async_computation | async-start | bytes 4194304 | tf_op jit(solution)/shard_map/all_to_all | solution.py:31
  317.6 266.2 %reduce-scatter.6.cloned.1.call-start = ((), (), s32[]{:S(2)}) async-start(), calls=%async_computation.12 | async-start | bytes 8650752 | tf_op jit(solution)/shard_map/reduce_scatter | solution.py:199
  385.5 401.4 %reduce-scatter.8.cloned.1.call-start = ((), (), s32[]{:S(2)}) async-start(), calls=%async_computation.13 | async-start | bytes 5406720 | tf_op jit(solution)/shard_map/reduce_scatter | solution.py:211
  611.6 17.0 %copy-start.5 = (bf16[128,1024]{1,0:T(8,128)(2,1)S(1)}, bf16[128,1024]{1,0:T(8,128)(2,1)}, u32[]{:S(2)}) copy-start(bf16[128,1024]{1,0:T(8,128)(2,1)} %param.19) | copy-start | bytes 786436
  789.3 15.1 %all-to-all-start.3 = ((f32[4,1,49152]{2,1,0:T(1,128)}), f32[4,1,49152]{2,1,0:T(1,128)S(1)}, u32[]{:S(2)}, u32[]{:S(2)}) async-start(f32[4,1,49152]{2,1,0:T(1,128)} %broadcast_in_dim.18), calls=%async_computation.5 | async-start | bytes 1572864 | tf_op jit(solution)/shard_map/all_to_all | solution.py:37
  792.8 200.1 %reduce-scatter.10.cloned.1.call-start = ((), (), s32[]{:S(2)}) async-start(), calls=%async_computation.14 | async-start | bytes 2162688
  807.6 2.4 copy-start.6
  809.6 184.7 %copy-start.1 = (bf16[8192,128]{1,0:T(8,128)(2,1)S(1)}, bf16[8192,128]{1,0:T(8,128)(2,1)}, u32[]{:S(2)}) copy-start(bf16[8192,128]{1,0:T(8,128)(2,1)} %param.18) | copy-start | bytes 6291460
Sparse Core Ops, SparseCore 0:
  11.7 94.6 all-gather.3
  114.8 83.9 all-gather.5
  231.0 77.9 all-gather.7
  385.6 198.0 reduce-scatter.5
  597.1 189.8 reduce-scatter.7
  809.7 183.1 reduce-scatter.9
where the time goes:
time: 1000 us
  waiting for transfers between devices  776 us (78%)
  matrix products  95.3 us (10%)
  blocking collectives  67.8 us (7%)
  other arithmetic  24.6 us (2%)
  local copies, waits for them, and re-layouts  15.3 us (2%)
  between operations  14.5 us (1%)
    reduce_scatter x1, waiting for transfers between devices, body(): lax.psum_scatter(trailing_contract(grads_all, output_weight), 'seq', scat...  198 us
    all_gather x2, waiting for transfers between devices, side_by_side(): lax.all_gather(both, axis, axis=dim, tiled=True)  165 us
    reduce_scatter x1, waiting for transfers between devices, body(): lax.psum_scatter(leading_contract(prob_low, grad_rows_local), 'seq', scat...  158 us
    unnamed x7, waiting for transfers between devices  139 us
    all_gather x1, waiting for transfers between devices, body(): slots_all = lax.all_gather(attended, 'seq', axis=0, tiled=True)  78.1 us
    all_to_all x3, blocking collectives, sent_to_all(): lax.all_to_all(jnp.broadcast_to(value[None], (count, *value.shape)), axis...  49.4 us
    dot_general x5, matrix products, trailing_contract(): lax.dot_general(left, right, (((1,), (1,)), ((), ())), preferred_element_...  30.8 us
    all_to_all x1, waiting for transfers between devices, summed_on_arrival(): pieces = lax.all_to_all(split_up(value, dim, count), axis, 0, 0, tiled=True)  25.6 us
  transfers between devices with their start and end apart: 8, of which 8 were waited for; matrix products, arithmetic and copies ran while one was open for 6% of the time, Pallas kernels for 0%

commit v1 on v0

v1 whole, which is shorter than its diff:
```python
import functools

import jax
import jax.numpy as jnp
from jax import lax
from jax.experimental import pallas as pl
from jax.experimental.pallas import tpu as pltpu
from jax.sharding import PartitionSpec as P

MODEL_DIM = 8192
HEADS_HERE = 8
HD = 128
ROWS = 512
GROUP = 2

adapter_scale = 0.25
epsilon = 1e-05
mask_fill = -1e30
score_scale = HD ** (-0.5)
exp2_scale = score_scale * 1.4426950408889634

MESH = pl.DeviceIdType.MESH
ANY = pl.BlockSpec(memory_space=pl.ANY)
VMEM = pl.BlockSpec(memory_space=pltpu.VMEM)

SIZES = {"y": 2, "z": 4, "x": 4}
AXES = "yzx"


def seq_coords():
    me = lax.axis_index("seq")
    return [me // 16, (me // 4) % 4, me % 4]


def peer(section, me, axis, step):
    at = list(me)
    k = AXES.index(axis)
    at[k] = lax.rem(at[k] + step, SIZES[axis])
    return (section, at[0] * 16 + at[1] * 4 + at[2])


def greet(devices):
    barrier = pltpu.get_barrier_semaphore()
    for device in devices:
        pl.semaphore_signal(barrier, inc=1, device_id=device, device_id_type=MESH)
    pl.semaphore_wait(barrier, len(devices))


def axis_peers(section, me):
    return [peer(section, me, a, d) for a in AXES for d in range(1, SIZES[a])]


def gather_kernel(pieces, x_ref, o_ref, send, recv, local):
    section = lax.axis_index("section")
    me = seq_coords()
    greet(axis_peers(section, me))
    own = pltpu.make_async_copy(x_ref, o_ref.at[tuple(me)], local)
    own.start()
    copies, latest = [], {}
    for phase in range(3):
        for i, (lo, size, order) in enumerate(pieces):
            if phase:
                for copy in latest[i]:
                    copy.wait_recv()
                if phase == 1 and i == 0:
                    own.wait()
            held = [slice(None) if a in order[:phase] else me[AXES.index(a)] for a in AXES]
            region = o_ref.at[tuple(held) + (pl.ds(lo, size),)]
            source = region if phase else x_ref.at[pl.ds(lo, size)]
            latest[i] = []
            for d in range(1, SIZES[order[phase]]):
                at = (i * 3 + phase) * 3 + d - 1
                copy = pltpu.make_async_remote_copy(
                    src_ref=source,
                    dst_ref=region,
                    send_sem=send.at[at],
                    recv_sem=recv.at[at],
                    device_id=peer(section, me, order[phase], d),
                    device_id_type=MESH,
                )
                copy.start()
                latest[i].append(copy)
            copies += latest[i]
    for i in range(len(pieces)):
        for copy in latest[i]:
            copy.wait_recv()
    for copy in copies:
        copy.wait_send()


def cut(rows, orders):
    step = 16
    units = rows // step
    base, extra = divmod(units, len(orders))
    pieces, at = [], 0
    for i, order in enumerate(orders):
        size = (base + (1 if i < extra else 0)) * step
        if size:
            pieces.append((at, size, order))
        at += size
    return pieces


def seq_gather(x, collective_id, name):
    rows, cols = x.shape
    pieces = cut(rows, ("xzy", "zyx", "yxz"))
    n = 9 * len(pieces)
    return pl.pallas_call(
        functools.partial(gather_kernel, pieces),
        out_shape=jax.ShapeDtypeStruct((2, 4, 4, rows, cols), x.dtype),
        in_specs=[ANY],
        out_specs=ANY,
        scratch_shapes=[
            pltpu.SemaphoreType.DMA((n,)),
            pltpu.SemaphoreType.DMA((n,)),
            pltpu.SemaphoreType.DMA,
        ],
        compiler_params=pltpu.CompilerParams(
            collective_id=collective_id, has_side_effects=True, vmem_limit_bytes=1 << 20
        ),
        name=name,
    )(x).reshape(32, rows, cols)


def scatter_kernel(pieces, x_ref, o_ref, send, recv, *bufs):
    section = lax.axis_index("section")
    me = seq_coords()
    greet(axis_peers(section, me))
    arrived = [bufs[3 * i : 3 * i + 3] for i in range(len(pieces))]
    partial = [bufs[3 * len(pieces) + 2 * i :][:2] for i in range(len(pieces))]
    copies, latest = [], {}

    def source(phase, i):
        lo, size, order = pieces[i]
        if phase == 0:
            return x_ref, (pl.ds(lo, size),)
        return partial[i][phase - 1], ()

    def block(phase, i, coord):
        lo, size, order = pieces[i]
        left = [a for a in AXES if a not in order[:phase]]
        ref, tail = source(phase, i)
        return ref.at[tuple(coord if a == order[phase] else slice(None) for a in left) + tail]

    def launch(phase, i):
        order = pieces[i][2]
        axis = order[phase]
        latest[i] = []
        for d in range(1, SIZES[axis]):
            at = (i * 3 + phase) * 3 + d - 1
            coord = lax.rem(me[AXES.index(axis)] + d, SIZES[axis])
            copy = pltpu.make_async_remote_copy(
                src_ref=block(phase, i, coord),
                dst_ref=arrived[i][phase].at[d - 1],
                send_sem=send.at[at],
                recv_sem=recv.at[at],
                device_id=peer(section, me, axis, d),
                device_id_type=MESH,
            )
            copy.start()
            latest[i].append(copy)
        copies.extend(latest[i])

    def total(phase, i):
        lo, size, order = pieces[i]
        axis = order[phase]
        for copy in latest[i]:
            copy.wait_recv()
        mine = block(phase, i, me[AXES.index(axis)])
        inbox = arrived[i][phase]
        left = [SIZES[a] for a in AXES if a not in order[: phase + 1]]
        count = 1
        for extent in left:
            count *= extent

        def add(k, carry):
            at = (k // left[1], k % left[1]) if len(left) == 2 else ((k,) if left else ())
            whole = mine[at].astype(jnp.float32) if at else mine[...].astype(jnp.float32)
            for d in range(SIZES[axis] - 1):
                whole = whole + inbox[(d,) + at].astype(jnp.float32)
            if phase == 2:
                o_ref[pl.ds(lo, size), :] = whole.astype(o_ref.dtype)
            else:
                partial[i][phase][at] = whole.astype(jnp.bfloat16)
            return carry

        if count == 1:
            add(0, 0)
        else:
            lax.fori_loop(0, count, add, 0)

    for i in range(len(pieces)):
        launch(0, i)
    for phase in range(3):
        for i in range(len(pieces)):
            total(phase, i)
            if phase < 2:
                launch(phase + 1, i)
    for copy in copies:
        copy.wait_send()


def seq_scatter(x, out_dtype, collective_id, name):
    _, rows, cols = x.shape
    pieces = cut(rows, ("yzx", "xyz", "zxy"))
    n = 9 * len(pieces)
    inboxes, partials = [], []
    for lo, size, order in pieces:
        for phase in range(3):
            left = [SIZES[a] for a in AXES if a not in order[: phase + 1]]
            inboxes.append(pltpu.VMEM((SIZES[order[phase]] - 1, *left, size, cols), jnp.bfloat16))
            if phase < 2:
                partials.append(pltpu.VMEM((*left, size, cols), jnp.bfloat16))
    return pl.pallas_call(
        functools.partial(scatter_kernel, pieces),
        out_shape=jax.ShapeDtypeStruct((rows, cols), out_dtype),
        in_specs=[VMEM],
        out_specs=VMEM,
        scratch_shapes=[
            pltpu.SemaphoreType.DMA((n,)),
            pltpu.SemaphoreType.DMA((n,)),
            *inboxes,
            *partials,
        ],
        compiler_params=pltpu.CompilerParams(
            collective_id=collective_id, has_side_effects=True, vmem_limit_bytes=40 << 20
        ),
        name=name,
    )(x.reshape(2, 4, 4, rows, cols))


def exchange_kernel(axis, count, apart, x_ref, o_ref, send, recv, local):
    me = lax.axis_index(axis)
    others = [lax.rem(me + d, count) for d in range(1, count)]
    device = lambda k: (
        (lax.axis_index("section"), k) if axis == "seq" else (k, lax.axis_index("seq"))
    )
    greet([device(k) for k in others])
    own = pltpu.make_async_copy(x_ref.at[me] if apart else x_ref, o_ref.at[me], local)
    own.start()
    copies = []
    for d, k in enumerate(others):
        copy = pltpu.make_async_remote_copy(
            src_ref=x_ref.at[k] if apart else x_ref,
            dst_ref=o_ref.at[me],
            send_sem=send.at[d],
            recv_sem=recv.at[d],
            device_id=device(k),
            device_id_type=MESH,
        )
        copy.start()
        copies.append(copy)
    own.wait()
    for copy in copies:
        copy.wait()


def exchange(x, axis, count, apart, collective_id, name):
    shape = x.shape[1:] if apart else x.shape
    return pl.pallas_call(
        functools.partial(exchange_kernel, axis, count, apart),
        out_shape=jax.ShapeDtypeStruct((count, *shape), x.dtype),
        in_specs=[ANY],
        out_specs=ANY,
        scratch_shapes=[
            pltpu.SemaphoreType.DMA((count - 1,)),
            pltpu.SemaphoreType.DMA((count - 1,)),
            pltpu.SemaphoreType.DMA,
        ],
        compiler_params=pltpu.CompilerParams(
            collective_id=collective_id, has_side_effects=True, vmem_limit_bytes=1 << 20
        ),
        name=name,
    )(x)


def contract(left, right, l, r):
    return lax.dot_general(
        left, right, (((l,), (r,)), ((), ())), preferred_element_type=jnp.float32
    )


def head_rows(ref):
    return jnp.concatenate([ref[:, h * HD : (h + 1) * HD] for h in range(HEADS_HERE)], axis=0)


def key_block(kv_ref, g, cols, context_rows):
    slots = kv_ref.shape[1] - context_rows
    context = kv_ref[pl.ds(g * GROUP, GROUP), :context_rows, cols]
    memory = kv_ref[pl.ds(g * GROUP, GROUP), context_rows:, cols]
    return jnp.concatenate(
        [context.reshape(GROUP * context_rows, HD), memory.reshape(GROUP * slots, HD)], axis=0
    )


def seen(g, rows_ref, context_rows, slots):
    token = g * (GROUP * context_rows) + lax.broadcasted_iota(
        jnp.int32, (GROUP * context_rows, ROWS), 0
    )
    slot = g * (GROUP * slots) + lax.broadcasted_iota(jnp.int32, (GROUP * slots, ROWS), 0)
    context = (token >= rows_ref[0:1, :]) & (token < rows_ref[1:2, :])
    memory = (slot >= rows_ref[2:3, :]) & (slot <= rows_ref[3:4, :])
    return context, memory


def attend_kernel(context_rows, span, rows_ref, q_ref, kv_ref, o_ref, ot_ref, top_ref, mass_ref):
    slots = kv_ref.shape[1] - context_rows
    edge = GROUP * context_rows
    q = head_rows(q_ref)
    ot_ref[...] = jnp.zeros_like(ot_ref)
    top_ref[...] = jnp.full_like(top_ref, mask_fill)
    mass_ref[...] = jnp.zeros_like(mass_ref)

    def step(g, carry):
        scores = contract(key_block(kv_ref, g, slice(0, HD), context_rows), q, 1, 1)
        context, memory = seen(g, rows_ref, context_rows, slots)
        scores = jnp.concatenate(
            [
                jnp.where(context, scores[:edge], mask_fill),
                jnp.where(memory, scores[edge:], mask_fill),
            ],
            axis=0,
        )
        before = top_ref[0:1, :]
        top = jnp.maximum(before, jnp.max(scores, axis=0, keepdims=True))
        keep = jnp.exp2((before - top) * exp2_scale)
        weight = jnp.exp2((scores - top) * exp2_scale)
        top_ref[0:1, :] = top
        mass_ref[0:1, :] = mass_ref[0:1, :] * keep + jnp.sum(weight, axis=0, keepdims=True)
        values = key_block(kv_ref, g, slice(HD, 2 * HD), context_rows)
        ot_ref[...] = ot_ref[...] * keep + contract(values, weight.astype(jnp.bfloat16), 0, 0)
        return carry

    lax.fori_loop(span[0], span[1], step, 0)
    ot_ref[...] = ot_ref[...] / mass_ref[0:1, :]
    rows = jnp.transpose(ot_ref[...]).astype(jnp.bfloat16)
    here = q_ref.shape[0]
    for h in range(HEADS_HERE):
        o_ref[:, h * HD : (h + 1) * HD] = rows[h * here : (h + 1) * here]


def backward_kernel(
    context_rows, span, rows_ref, q_ref, g_ref, kv_ref, ot_ref, top_ref, mass_ref, dq_ref, dv_ref, acc
):
    slots = kv_ref.shape[1] - context_rows
    edge = GROUP * context_rows
    q = head_rows(q_ref)
    grad = head_rows(g_ref)
    center = jnp.sum(jnp.transpose(grad.astype(jnp.float32)) * ot_ref[...], axis=0, keepdims=True)
    top = top_ref[0:1, :]
    share = 1.0 / mass_ref[0:1, :]
    acc[...] = jnp.zeros_like(acc)
    dv_ref[...] = jnp.zeros_like(dv_ref)

    def step(g, carry):
        keys = key_block(kv_ref, g, slice(0, HD), context_rows)
        scores = contract(keys, q, 1, 1)
        context, memory = seen(g, rows_ref, context_rows, slots)
        probs = jnp.exp2((scores - top) * exp2_scale) * share
        probs = jnp.concatenate(
            [jnp.where(context, probs[:edge], 0.0), jnp.where(memory, probs[edge:], 0.0)], axis=0
        )
        values = key_block(kv_ref, g, slice(HD, 2 * HD), context_rows)
        d_probs = contract(values, grad, 1, 1)
        d_scores = (probs * (d_probs - center)).astype(jnp.bfloat16)
        d_values = contract(probs.astype(jnp.bfloat16), grad, 1, 0).astype(jnp.bfloat16)
        dv_ref[pl.ds(g * GROUP, GROUP), :context_rows, :] = d_values[:edge].reshape(
            GROUP, context_rows, HD
        )
        dv_ref[pl.ds(g * GROUP, GROUP), context_rows:, :] = d_values[edge:].reshape(
            GROUP, slots, HD
        )
        acc[...] += contract(keys, d_scores, 0, 0)
        return carry

    lax.fori_loop(span[0], span[1], step, 0)
    rows = jnp.transpose(acc[...] * score_scale).astype(jnp.bfloat16)
    here = q_ref.shape[0]
    for h in range(HEADS_HERE):
        dq_ref[:, h * HD : (h + 1) * HD] = rows[h * here : (h + 1) * here]


SMEM = pl.BlockSpec(memory_space=pltpu.SMEM)
BIG = pltpu.CompilerParams(vmem_limit_bytes=48 << 20)


def attend(span, rows, q, kv, context_rows):
    f32 = jnp.float32
    return pl.pallas_call(
        functools.partial(attend_kernel, context_rows),
        out_shape=(
            jax.ShapeDtypeStruct(q.shape, jnp.bfloat16),
            jax.ShapeDtypeStruct((HD, ROWS), f32),
            jax.ShapeDtypeStruct((8, ROWS), f32),
            jax.ShapeDtypeStruct((8, ROWS), f32),
        ),
        in_specs=[SMEM, VMEM, VMEM, VMEM],
        out_specs=(VMEM, VMEM, VMEM, VMEM),
        compiler_params=BIG,
        name="attend",
    )(span, rows, q, kv)


def attend_backward(span, rows, q, grad, kv, ot, top, mass, context_rows):
    return pl.pallas_call(
        functools.partial(backward_kernel, context_rows),
        out_shape=(
            jax.ShapeDtypeStruct(q.shape, jnp.bfloat16),
            jax.ShapeDtypeStruct((*kv.shape[:2], HD), jnp.bfloat16),
        ),
        in_specs=[SMEM] + [VMEM] * 7,
        out_specs=(VMEM, VMEM),
        scratch_shapes=[pltpu.VMEM((HD, ROWS), jnp.float32)],
        compiler_params=BIG,
        name="attend_backward",
    )(span, rows, q, grad, kv, ot, top, mass)


def row_bounds(document_slots, first, slot_dev, seq_size):
    docs = document_slots.shape[0]
    order = jnp.arange(docs, dtype=jnp.int32)
    ends = jnp.sum(jnp.where(order[None, :] <= order[:, None], document_slots[None, :], 0), axis=1)
    slot = first + jnp.arange(slot_dev, dtype=jnp.int32)
    passed = ends[None, :] <= slot[:, None]
    low = jnp.max(jnp.where(passed, ends[None, :], 0), axis=1)
    high = jnp.min(jnp.where(passed, slot_dev * seq_size, ends[None, :]), axis=1)
    one = jnp.stack([4 * low, 4 * high, low, slot] + [slot] * 4).astype(jnp.int32)
    unit = GROUP * slot_dev
    span = jnp.stack([jnp.min(low) // unit, (jnp.max(high) + unit - 1) // unit])
    return span.astype(jnp.int32), jnp.tile(one, (1, HEADS_HERE))


def body(
    context,
    memory,
    query_weight,
    key_weight,
    value_weight,
    query_down_map,
    query_up_map,
    value_down_map,
    value_up_map,
    output_weight,
    decoder_gain,
    document_slots,
    normed_gradient,
):
    bf16, f32 = jnp.bfloat16, jnp.float32
    tok_dev = context.shape[0]
    slot_dev = memory.shape[0]
    seq_size = lax.axis_size("seq")
    seq_index = lax.axis_index("seq")
    section_extent = lax.axis_size("section")
    section_index = lax.axis_index("section")
    every_row = jnp.concatenate([context, memory], axis=0)
    weights = seq_gather(
        jnp.concatenate([key_weight, value_weight, value_down_map], axis=1), 1, "gather_weights"
    ).reshape(MODEL_DIM, 3 * HD)
    projected = jnp.dot(every_row, weights, preferred_element_type=f32)
    query_low = jnp.dot(memory, query_down_map, preferred_element_type=f32).astype(bf16)
    value_low = projected[:, 2 * HD :].astype(bf16)
    queries = (
        jnp.dot(memory, query_weight, preferred_element_type=f32)
        + adapter_scale * jnp.dot(query_low, query_up_map, preferred_element_type=f32)
    ).astype(bf16)
    keys = projected[:, :HD].astype(bf16)
    values = (
        projected[:, HD : 2 * HD]
        + adapter_scale * jnp.dot(value_low, value_up_map, preferred_element_type=f32)
    ).astype(bf16)
    kv = seq_gather(jnp.concatenate([keys, values], axis=1), 2, "gather_keys")
    span, rows = row_bounds(document_slots, seq_index * slot_dev, slot_dev, seq_size)
    attended, ot, top, mass = attend(span, rows, queries, kv, tok_dev)
    slots_all = seq_gather(attended, 3, "gather_attended").reshape(seq_size * slot_dev, -1)
    hidden_part = jnp.dot(slots_all, output_weight, preferred_element_type=f32).astype(bf16)
    pieces = exchange(
        hidden_part.reshape(section_extent, -1, hidden_part.shape[1]),
        "section", 4, True, 4, "sum_hidden",
    )
    hidden = jnp.sum(pieces.astype(f32), axis=0)
    total_slots = slot_dev * seq_size
    weighted = total_slots ** (-0.5) * normed_gradient.astype(f32) * decoder_gain[None, :]
    stats = jnp.stack([jnp.sum(hidden * hidden, axis=1), jnp.sum(weighted * hidden, axis=1)])
    stats = jnp.sum(
        exchange(stats.reshape(8, 128), "seq", 32, False, 5, "sum_stats"), axis=0
    ).reshape(2, -1)
    square_sum, cross_sum = stats[0], stats[1]
    inv_rms = lax.rsqrt(square_sum / MODEL_DIM + epsilon)
    normed = (hidden * inv_rms[:, None] * decoder_gain[None, :]).astype(bf16)
    d_hidden = (
        inv_rms[:, None] * weighted - hidden * (inv_rms**3 * cross_sum / MODEL_DIM)[:, None]
    ).astype(bf16)
    grads_all = exchange(d_hidden, "section", 4, False, 6, "gather_grads").reshape(
        total_slots, -1
    )
    d_part = contract(grads_all, output_weight, 1, 1).astype(bf16)
    d_attended = seq_scatter(
        d_part.reshape(seq_size, slot_dev, -1), bf16, 7, "scatter_attended"
    )
    d_queries, dv_part = attend_backward(
        span, rows, queries, d_attended, kv, ot, top, mass, tok_dev
    )
    d_values = seq_scatter(dv_part, bf16, 8, "scatter_values")
    query_up_part = adapter_scale * contract(query_low, d_queries, 0, 0)
    value_up_part = adapter_scale * contract(value_low, d_values, 0, 0)
    query_part = adapter_scale * contract(d_queries, query_up_map, 1, 1)
    value_part = adapter_scale * contract(d_values, value_up_map, 1, 1)
    backs = jnp.sum(
        exchange(
            jnp.concatenate([query_part, value_part], axis=0), "section", 4, False, 9, "sum_backs"
        ),
        axis=0,
    ).astype(bf16)
    width = memory.shape[1] // section_extent
    memory_cols = lax.dynamic_slice_in_dim(memory, section_index * width, width, 1)
    row_cols = lax.dynamic_slice_in_dim(every_row, section_index * width, width, 1)
    down_parts = [
        contract(memory_cols, backs[:slot_dev], 0, 0),
        contract(row_cols, backs[slot_dev:], 0, 0),
    ]
    ups = jnp.concatenate([query_up_part, value_up_part], axis=1)
    lanes = ups.shape[1] // 128
    ups = jnp.moveaxis(ups.reshape(128, lanes, 128), 1, 0).reshape(seq_size, -1, 128)
    up_rows = ups.shape[1]
    final_parts = jnp.concatenate(
        [part.reshape(seq_size, -1, 128).astype(bf16) for part in down_parts]
        + [jnp.pad(ups.astype(bf16), ((0, 0), (0, -up_rows % 16), (0, 0)))],
        axis=1,
    )
    final = seq_scatter(final_parts, f32, 10, "scatter_final")
    down_rows = MODEL_DIM // section_extent // seq_size
    grad_qa, grad_va = final[:down_rows], final[down_rows : 2 * down_rows]
    ups = exchange(final[2 * down_rows :], "seq", 32, False, 11, "gather_ups")[:, :up_rows]
    ups = jnp.moveaxis(ups.reshape(lanes, 128, 128), 0, 1).reshape(128, lanes * 128)
    split = query_up_part.shape[1]
    return (normed, grad_qa, grad_va, ups[:, :split], ups[:, split:])


def solution(mesh):
    in_specs = (
        P("seq", None),
        P("seq", None),
        P(None, "section"),
        P("seq", "section"),
        P("seq", "section"),
        P(),
        P(None, "section"),
        P("seq", None),
        P(None, "section"),
        P("section", "seq"),
        P("seq"),
        P(),
        P("section", "seq"),
    )
    out_specs = (
        P("section", "seq"),
        P(("section", "seq"), None),
        P(("section", "seq"), None),
        P(None, "section"),
        P(None, "section"),
    )
    return jax.shard_map(body, mesh=mesh, in_specs=in_specs, out_specs=out_specs, check_vma=False)
```

time: 1000 us -> 361 us (0.36)
  waiting for transfers between devices: 776 us -> 0 us
  Pallas kernels: 0 us -> 319 us
  matrix products: 95.3 us -> 21.6 us
  blocking collectives: 67.8 us -> 0 us
  other arithmetic: 24.6 us -> 5.51 us
  between operations: 14.5 us -> 4.39 us
    reduce_scatter x2 -> x0, waiting for transfers between devices: 356 us -> none  [the longest x1 198 us: body(): lax.psum_scatter(trailing_contract(grads_all, output_weight), 'seq', scat...]
    pallas_call x0 -> x13, Pallas kernels: none -> 319 us  [the longest x3 142 us: seq_gather(): pl.pallas_call(functools.partial(gather_kernel, pieces), out_shape=jax.Sh...]
    all_gather x3 -> x0, waiting for transfers between devices: 243 us -> none  [the longest x2 165 us: side_by_side(): lax.all_gather(both, axis, axis=dim, tiled=True)]
    unnamed x7 -> x0, waiting for transfers between devices: 139 us -> none
    dot_general x18 -> x13, matrix products: 95.3 us -> 21.6 us  [the longest x1 8.94 us: body(): jnp.dot(memory, query_weight, preferred_element_type=f32)]
    all_to_all x4 -> x0, blocking collectives: 67.8 us -> none  [the longest x3 49.4 us: sent_to_all(): lax.all_to_all(jnp.broadcast_to(value[None], (count, *value.shape)), axis...]
    all_to_all x2 -> x0, waiting for transfers between devices: 37.2 us -> none  [the longest x1 25.6 us: summed_on_arrival(): pieces = lax.all_to_all(split_up(value, dim, count), axis, 0, 0, tiled=True)]
  transfers between devices with their start and end apart: 8 -> 0, of which waited for: 8 -> 0; matrix products, arithmetic and copies ran while one was open for 6% -> 0% of each run, Pallas kernels for 0% -> 0%
where the time goes in v1:
time: 361 us; the launch traced here: 360 us
  Pallas kernels  319 us (88%)
  matrix products  21.6 us (6%)
  local copies, waits for them, and re-layouts  9.53 us (3%)
  other arithmetic  5.51 us (2%)
  between operations  4.39 us (1%)
    pallas_call x3, Pallas kernels, seq_gather(): pl.pallas_call(functools.partial(gather_kernel, pieces), out_shape=jax.Sh...  142 us
    pallas_call x3, Pallas kernels, seq_scatter(): pl.pallas_call(functools.partial(scatter_kernel, pieces), out_shape=jax.S...  105 us
    pallas_call x5, Pallas kernels, exchange(): pl.pallas_call(functools.partial(exchange_kernel, axis, count, apart), ou...  66.5 us
    dot_general x1, matrix products, body(): jnp.dot(memory, query_weight, preferred_element_type=f32)  8.94 us

profile of v1, /device:TPU:0, one launch (start us, length us, event | category | flops | bytes accessed | tf_op | source)
XLA Modules:
  0.0 360.2 jit_solution(16310104271896285274)
XLA Ops:
  0.7 0.9 select_reduce_fusion
  1.7 0.6 reduce_min.18
  4.9 0.6 multiply_bitcast_fusion
  6.3 0.7 broadcast_multiply_fusion
  7.0 1.7 convolution_convert_fusion.4
  8.8 0.9 pad_maximum_fusion.1.x_ref
  9.8 1.1 convolution_multiply_fusion.1
  10.9 8.9 %fusion.4.q_ref = bf16[64,1024]{1,0:T(8,128)(2,1)S(1)} fusion(f32[64,1024]{1,0:T(8,128)S(1)} %convolution_multiply_fusion.1, bf16[64,8192]{1,0:T(8,128)(2,1)S(1)} %copy-done.3, bf16[8192,1024]{1,0:T(8,128)(2,1)} %param.15), kind=kOutput, calls=%fused_computation.13 | convolution fusion | flops 1073872896 | bytes 18219008 | tf_op jit(solution)/shard_map/dot_general | solution.py:463
  20.4 52.6 %gather_weights.1 = bf16[2,4,4,256,384]{4,3,2,1,0:T(8,128)(2,1)S(1)} custom-call(bf16[256,384]{1,0:T(8,128)(2,1)S(1)} %pad_maximum_fusion.1.x_ref), custom_call_target="tpu_custom_call" | custom-call | tf_op jit(solution)/shard_map/gather_weights/pallas_call | solution.py:108
  73.0 2.9 fusion.20
  76.2 39.8 %gather_keys.1 = bf16[2,4,4,320,256]{4,3,2,1,0:T(8,128)(2,1)S(1)} custom-call(bf16[320,256]{1,0:T(8,128)(2,1)S(1)} %pad_maximum_fusion.3.x_ref), custom_call_target="tpu_custom_call" | custom-call | tf_op jit(solution)/shard_map/gather_keys/pallas_call | solution.py:108
  116.0 1.8 attend.1
  117.8 49.7 %gather_attended.1 = bf16[2,4,4,64,1024]{4,3,2,1,0:T(8,128)(2,1)S(1)} custom-call(bf16[64,1024]{1,0:T(8,128)(2,1)S(1)} %get-tuple-element.11.x_ref), custom_call_target="tpu_custom_call" | custom-call | tf_op jit(solution)/shard_map/gather_attended/pallas_call | solution.py:108
  167.5 1.3 convolution_convert_fusion.1
  168.8 12.7 %sum_hidden.1 = bf16[4,512,256]{2,1,0:T(8,128)(2,1)S(1)} custom-call(bf16[4,512,256]{2,1,0:T(8,128)(2,1)S(1)} %bitcast.57), custom_call_target="tpu_custom_call" | custom-call | tf_op jit(solution)/shard_map/sum_hidden/pallas_call | solution.py:260
  181.9 15.7 %sum_stats.1 = f32[32,8,128]{2,1,0:T(8,128)S(1)} custom-call(f32[8,128]{1,0:T(8,128)S(1)} %reshape.106.x_ref), custom_call_target="tpu_custom_call" | custom-call | tf_op jit(solution)/shard_map/sum_stats/pallas_call | solution.py:260
  197.7 0.9 subtract_convert_fusion
  198.6 12.4 %gather_grads.1 = bf16[4,512,256]{2,1,0:T(8,128)(2,1)S(1)} custom-call(bf16[512,256]{1,0:T(8,128)(2,1)S(1)} %get-tuple-element.31.x_ref), custom_call_target="tpu_custom_call" | custom-call | tf_op jit(solution)/shard_map/gather_grads/pallas_call | solution.py:260
  211.0 2.3 convolution_convert_fusion
  213.4 49.0 %scatter_attended.1.g_ref = bf16[64,1024]{1,0:T(8,128)(2,1)S(1)} custom-call(bf16[2,4,4,64,1024]{4,3,2,1,0:T(8,128)(2,1)S(1)} %bitcast.51), custom_call_target="tpu_custom_call" | custom-call | tf_op jit(solution)/shard_map/scatter_attended/pallas_call | solution.py:214
  262.4 4.0 %attend_backward.1 = (bf16[64,1024]{1,0:T(8,128)(2,1)S(1)}, bf16[32,320,128]{2,1,0:T(8,128)(2,1)S(1)}) custom-call(s32[2]{0:T(128)S(1)} %pad_add_fusion.span, s32[8,512]{1,0:T(8,128)S(1)} %tile.10.rows_ref, bf16[64,1024]{1,0:T(8,128)(2,1)S(1)} %fusion.4.q_ref, bf16[64,1024]{1,0:T(8,128)(2,1)S(1)} %scatter_attended.1.g_ref, bf16[32,320,256]{2,1,0:T(8,128)(2,1)} %bitcast.50, ...), custom_call_target="tpu_custom_call" | custom-call | tf_op jit(solution)/shard_map/attend_backward/pallas_call | solution.py:405
  266.4 35.5 %scatter_values.1 = bf16[320,128]{1,0:T(8,128)(2,1)S(1)} custom-call(bf16[2,4,4,320,128]{4,3,2,1,0:T(8,128)(2,1)S(1)} %bitcast.56), custom_call_target="tpu_custom_call" | custom-call | tf_op jit(solution)/shard_map/scatter_values/pallas_call | solution.py:214
  303.4 9.7 %sum_backs.1 = f32[4,384,128]{2,1,0:T(8,128)S(1)} custom-call(f32[384,128]{1,0:T(8,128)S(1)} %pad_maximum_fusion.2.x_ref), custom_call_target="tpu_custom_call" | custom-call | tf_op jit(solution)/shard_map/sum_backs/pallas_call | solution.py:260
  313.1 1.9 convolution_convert_fusion.2
  315.5 20.4 %scatter_final.1 = f32[176,128]{1,0:T(8,128)S(1)} custom-call(bf16[2,4,4,176,128]{4,3,2,1,0:T(8,128)(2,1)S(1)} %bitcast.54), custom_call_target="tpu_custom_call" | custom-call | tf_op jit(solution)/shard_map/scatter_final/pallas_call | solution.py:214
  336.5 16.0 %gather_ups.1 = f32[32,48,128]{2,1,0:T(8,128)S(1)} custom-call(f32[48,128]{1,0:T(8,128)S(1)} %slice.52.x_ref), custom_call_target="tpu_custom_call" | custom-call | tf_op jit(solution)/shard_map/gather_ups/pallas_call | solution.py:260
  352.5 0.9 slice.53
  353.4 1.9 reshape.110
  355.3 1.3 copy.30
  356.6 0.8 slice.61
  357.5 2.0 copy.31
  359.5 0.7 copy.32
  (56 shorter events, 4.0 us)
Async XLA Ops:
  0.6 6.4 %copy-start = (bf16[8192,128]{1,0:T(8,128)(2,1)S(1)}, bf16[8192,128]{1,0:T(8,128)(2,1)}, u32[]{:S(2)}) copy-start(bf16[8192,128]{1,0:T(8,128)(2,1)} %param.18) | copy-start | bytes 6291460
  0.6 10.2 %copy-start.3 = (bf16[64,8192]{1,0:T(8,128)(2,1)S(1)}, bf16[64,8192]{1,0:T(8,128)(2,1)}, u32[]{:S(2)}) copy-start(bf16[64,8192]{1,0:T(8,128)(2,1)} %param.14) | copy-start | bytes 3145732
  10.9 9.0 %copy-start.5 = (bf16[256,8192]{1,0:T(8,128)(2,1)S(1)}, bf16[256,8192]{1,0:T(8,128)(2,1)}, u32[]{:S(2)}) copy-start(bf16[256,8192]{1,0:T(8,128)(2,1)} %param.13) | copy-start | bytes 12582916
  20.4 55.5 %copy-start.4 = (bf16[320,8192]{1,0:T(8,128)(2,1)}, bf16[320,8192]{1,0:T(8,128)(2,1)S(1)}, u32[]{:S(2)}) copy-start(bf16[320,8192]{1,0:T(8,128)(2,1)S(1)} %constant_dynamic-update-slice_fusion) | copy-start | bytes 15728644
  73.0 3.0 copy-start.9
  116.0 51.5 %copy-start.2 = (bf16[2,4,4,320,256]{4,3,2,1,0:T(8,128)(2,1)}, bf16[2,4,4,320,256]{4,3,2,1,0:T(8,128)(2,1)S(1)}, u32[]{:S(2)}) copy-start(bf16[2,4,4,320,256]{4,3,2,1,0:T(8,128)(2,1)S(1)} %gather_keys.1) | copy-start | bytes 15728644
  116.0 51.5 %copy-start.8 = (bf16[1024,256]{1,0:T(8,128)(2,1)S(1)}, bf16[1024,256]{1,0:T(8,128)(2,1)}, u32[]{:S(2)}) copy-start(bf16[1024,256]{1,0:T(8,128)(2,1)} %param.22) | copy-start | bytes 1572868
  167.5 14.2 %copy-start.6 = (bf16[512,256]{1,0:T(8,128)(2,1)S(1)}, bf16[512,256]{1,0:T(8,128)(2,1)}, u32[]{:S(2)}) copy-start(bf16[512,256]{1,0:T(8,128)(2,1)} %param.25) | copy-start | bytes 786436
  168.8 28.9 %copy-start.10 = (f32[256]{0:T(256)S(1)}, f32[256]{0:T(256)}, u32[]{:S(2)}) copy-start(f32[256]{0:T(256)} %param.23) | copy-start | bytes 3076
  262.4 39.7 %copy-start.7 = (bf16[128,1024]{1,0:T(8,128)(2,1)S(1)}, bf16[128,1024]{1,0:T(8,128)(2,1)}, u32[]{:S(2)}) copy-start(bf16[128,1024]{1,0:T(8,128)(2,1)} %param.19) | copy-start | bytes 786436
  315.5 44.7 %copy-start.1 = (bf16[8192,128]{1,0:T(8,128)(2,1)S(1)}, bf16[8192,128]{1,0:T(8,128)(2,1)}, u32[]{:S(2)}) copy-start(bf16[8192,128]{1,0:T(8,128)(2,1)} %param.18) | copy-start | bytes 6291460

commit v2 on v1

--- a/solution.py
+++ b/solution.py
@@ -22,70 +22,322 @@
 MESH = pl.DeviceIdType.MESH
 ANY = pl.BlockSpec(memory_space=pl.ANY)
 VMEM = pl.BlockSpec(memory_space=pltpu.VMEM)
-
-SIZES = {"y": 2, "z": 4, "x": 4}
-AXES = "yzx"
-
-
-def seq_coords():
-    me = lax.axis_index("seq")
-    return [me // 16, (me // 4) % 4, me % 4]
-
-
-def peer(section, me, axis, step):
-    at = list(me)
-    k = AXES.index(axis)
-    at[k] = lax.rem(at[k] + step, SIZES[axis])
-    return (section, at[0] * 16 + at[1] * 4 + at[2])
-
-
-def greet(devices):
+HBM = pl.BlockSpec(memory_space=pltpu.HBM)
+
+SIZES = {"y": 2, "z": 4, "x": 4, "h": 2, "c": 2}
+PLAIN, PAIRED = "yzx", "yzhc"
+
+
+def coords(axes):
+    seq, section = lax.axis_index("seq"), lax.axis_index("section")
+    here = {"y": seq // 16, "z": (seq // 4) % 4, "x": seq % 4, "m": section // 2, "c": section % 2}
+    here["h"], here["l"] = here["x"] // 2, here["x"] % 2
+    return here
+
+
+def device_at(axes, here):
+    x = here["x"] if "x" in axes else here["h"] * 2 + here["l"]
+    return (here["m"] * 2 + here["c"], here["y"] * 16 + here["z"] * 4 + x)
+
+
+def moved(here, axis, step):
+    return {**here, axis: lax.rem(here[axis] + step, SIZES[axis])}
+
+
+def greet(devices, here=None):
     barrier = pltpu.get_barrier_semaphore()
     for device in devices:
         pl.semaphore_signal(barrier, inc=1, device_id=device, device_id_type=MESH)
-    pl.semaphore_wait(barrier, len(devices))
-
-
-def axis_peers(section, me):
-    return [peer(section, me, a, d) for a in AXES for d in range(1, SIZES[a])]
-
-
-def gather_kernel(pieces, x_ref, o_ref, send, recv, local):
-    section = lax.axis_index("section")
-    me = seq_coords()
-    greet(axis_peers(section, me))
-    own = pltpu.make_async_copy(x_ref, o_ref.at[tuple(me)], local)
+    if here is not None:
+
+        @pl.when(here["c"] != here["l"])
+        def _():
+            pl.semaphore_signal(
+                barrier, inc=1, device_id=swap_device(here), device_id_type=MESH
+            )
+
+    extra = 0 if here is None else lax.rem(here["c"] + here["l"], 2)
+    pl.semaphore_wait(barrier, len(devices) + extra)
+
+
+def swap_device(here):
+    return device_at("h", {**here, "c": here["l"], "l": here["c"]})
+
+
+class Swap:
+    def __init__(self, here, source, target, send, recv, local):
+        self.apart = here["c"] != here["l"]
+        self.there = lambda: pltpu.make_async_remote_copy(
+            src_ref=source,
+            dst_ref=target,
+            send_sem=send,
+            recv_sem=recv,
+            device_id=swap_device(here),
+            device_id_type=MESH,
+        )
+        self.stays = lambda: pltpu.make_async_copy(source, target, local)
+
+    def start(self):
+        @pl.when(self.apart)
+        def _():
+            self.there().start()
+
+        @pl.when(jnp.logical_not(self.apart))
+        def _():
+            self.stays().start()
+
+    def wait(self):
+        @pl.when(self.apart)
+        def _():
+            self.there().wait()
+
+        @pl.when(jnp.logical_not(self.apart))
+        def _():
+            self.stays().wait()
+
+
+def axis_peers(axes, here):
+    return [device_at(axes, moved(here, a, d)) for a in axes for d in range(1, SIZES[a])]
+
+
+def remote(source, target, send, recv, device):
+    copy = pltpu.make_async_remote_copy(
+        src_ref=source,
+        dst_ref=target,
+        send_sem=send,
+        recv_sem=recv,
+        device_id=device,
+        device_id_type=MESH,
+    )
+    copy.start()
+    return copy
+
+
+class Gather:
+    def __init__(self, here, axes, pieces, source, target, sems, base):
+        self.here, self.axes, self.pieces, self.base = here, axes, pieces, base
+        self.source, self.target = source, target
+        self.send, self.recv, self.fore, self.back = sems
+        self.place = tuple(here[a] for a in axes)
+        self.paired = "c" in axes
+        self.partner = device_at(axes, moved(here, "c", 1)) if self.paired else None
+        self.copies, self.latest, self.passed = [], {}, []
+
+    def at(self, phase, i, d):
+        return self.base + (i * 3 + phase) * 3 + d
+
+    def begin(self):
+        if self.paired:
+            own = self.target.at[self.place]
+            sem = self.base + 9 * len(self.pieces)
+            self.passed.append(
+                remote(
+                    own if self.source is None else self.source,
+                    own,
+                    self.fore.at[sem],
+                    self.back.at[sem],
+                    self.partner,
+                )
+            )
+
+    def arrived(self, phase, i):
+        lo, size, order = self.pieces[i]
+        axis = order[phase]
+        for d, copy in enumerate(self.latest[i]):
+            copy.wait_recv()
+            if self.paired:
+                came = {**self.here, axis: lax.rem(self.here[axis] + SIZES[axis] - d - 1, SIZES[axis])}
+                region = self.target.at[
+                    tuple(slice(None) if a in order[:phase] else came[a] for a in self.axes)
+                    + (pl.ds(lo, size),)
+                ]
+                at = self.at(phase, i, d)
+                self.passed.append(
+                    remote(region, region, self.fore.at[at], self.back.at[at], self.partner)
+                )
+
+    def launch(self, phase, i):
+        lo, size, order = self.pieces[i]
+        held = tuple(slice(None) if a in order[:phase] else self.here[a] for a in self.axes)
+        region = self.target.at[held + (pl.ds(lo, size),)]
+        source = region if phase or self.source is None else self.source.at[pl.ds(lo, size)]
+        self.latest[i] = []
+        for d in range(1, SIZES[order[phase]]):
+            at = self.at(phase, i, d - 1)
+            device = device_at(self.axes, moved(self.here, order[phase], d))
+            self.latest[i].append(remote(source, region, self.send.at[at], self.recv.at[at], device))
+        self.copies += self.latest[i]
+
+    def finish(self):
+        for i in range(len(self.pieces)):
+            self.arrived(2, i)
+        for copy in self.passed:
+            copy.wait_recv()
+        for copy in self.copies + self.passed:
+            copy.wait_send()
+
+
+def run_gathers(gathers, owns, between):
+    for gather in gathers:
+        gather.begin()
+    for phase in range(3):
+        for gather in gathers:
+            for i in range(len(gather.pieces)):
+                if phase:
+                    gather.arrived(phase - 1, i)
+                    if phase == 1:
+                        while owns:
+                            owns.pop().wait()
+                gather.launch(phase, i)
+        between(phase)
+    for gather in gathers:
+        gather.finish()
+
+
+def semaphores(count):
+    return [pltpu.SemaphoreType.DMA((count,)) for _ in range(4)]
+
+
+def opening_kernel(
+    pieces, half_pieces, kv_ref, down_ref, memory_ref, weight_ref, wo_ref, ng_ref, gain_ref,
+    kv_all, down_all, acc_ref, wo_out, ng_out, gain_out,
+    send, recv, fore, back, buffer, loads, local, swap_send, swap_recv, swap_local,
+):
+    here = coords(PLAIN)
+    depth = buffer.shape[1]
+    count = weight_ref.shape[0] // depth
+
+    def load(k):
+        return pltpu.make_async_copy(
+            weight_ref.at[pl.ds(k * depth, depth)], buffer.at[k % 3], loads.at[k % 3]
+        )
+
+    for k in range(2):
+        load(k).start()
+    greet(axis_peers(PLAIN + "c", here), here)
+    swaps = [
+        Swap(here, a, b, swap_send.at[i], swap_recv.at[i], swap_local.at[i])
+        for i, (a, b) in enumerate(((wo_ref, wo_out), (ng_ref, ng_out), (gain_ref, gain_out)))
+    ]
+    half = down_ref.shape[0] // 2
+    own_half = down_ref.at[pl.ds(here["c"] * half, half)]
+    sems = (send, recv, fore, back)
+    plain = Gather(here, PLAIN, pieces, kv_ref, kv_all, sems, 0)
+    shared = Gather(
+        here, PLAIN + "c", half_pieces, own_half, down_all, sems, 9 * len(pieces) + 1
+    )
+    owns = [
+        pltpu.make_async_copy(kv_ref, kv_all.at[plain.place], local.at[0]),
+        pltpu.make_async_copy(own_half, down_all.at[shared.place], local.at[1]),
+    ]
+    for own in owns:
+        own.start()
+    acc_ref[...] = jnp.zeros_like(acc_ref)
+
+    def between(phase):
+        if phase == 0:
+            for swap in swaps:
+                swap.start()
+        edges = (0, count // 4, count // 2 + count // 8, count)
+        for k in range(edges[phase], edges[phase + 1]):
+            load(k).wait()
+            if k + 2 < count:
+                load(k + 2).start()
+            acc_ref[...] += jnp.dot(
+                memory_ref[:, k * depth : (k + 1) * depth],
+                buffer[k % 3],
+                preferred_element_type=jnp.float32,
+            )
+
+    run_gathers([plain, shared], owns, between)
+    for swap in swaps:
+        swap.wait()
+
+
+def opening(kv_weight, down, memory, query_weight, output_weight, normed_gradient, gain, collective_id):
+    rows, cols = kv_weight.shape
+    half = down.shape[0] // 2
+    pieces = cut(rows, ("xzy", "zyx", "yxz"))
+    half_pieces = cut(half, ("xzy", "zyx", "yxz"))
+    n = 9 * len(pieces) + 1 + 9 * len(half_pieces) + 1
+    like = lambda a: jax.ShapeDtypeStruct(a.shape, a.dtype)
+    outs = pl.pallas_call(
+        functools.partial(opening_kernel, pieces, half_pieces),
+        out_shape=(
+            jax.ShapeDtypeStruct((2, 4, 4, rows, cols), kv_weight.dtype),
+            jax.ShapeDtypeStruct((2, 4, 4, 2, half, down.shape[1]), down.dtype),
+            jax.ShapeDtypeStruct((memory.shape[0], query_weight.shape[1]), jnp.float32),
+            like(output_weight),
+            like(normed_gradient),
+            like(gain),
+        ),
+        in_specs=[ANY, ANY, VMEM, HBM, ANY, ANY, ANY],
+        out_specs=(ANY, ANY, VMEM, ANY, ANY, ANY),
+        scratch_shapes=semaphores(n)
+        + [
+            pltpu.VMEM((3, 1024, query_weight.shape[1]), jnp.bfloat16),
+            pltpu.SemaphoreType.DMA((3,)),
+            pltpu.SemaphoreType.DMA((2,)),
+            pltpu.SemaphoreType.DMA((3,)),
+            pltpu.SemaphoreType.DMA((3,)),
+            pltpu.SemaphoreType.DMA((3,)),
+        ],
+        compiler_params=pltpu.CompilerParams(
+            collective_id=collective_id, has_side_effects=True, vmem_limit_bytes=52 << 20
+        ),
+        name="opening",
+    )(kv_weight, down, memory, query_weight, output_weight, normed_gradient, gain)
+    return (
+        outs[0].reshape(32 * rows, cols),
+        outs[1].reshape(32 * 2 * half, down.shape[1]),
+        *outs[2:],
+    )
+
+
+def keys_kernel(
+    pieces, x_ref, q_ref, o_ref, q_out, send, recv, fore, back, swap_send, swap_recv, swap_local
+):
+    here = coords(PAIRED)
+    greet(axis_peers(PAIRED, here), here)
+    home = o_ref.at[here["y"], here["z"], here["h"], here["l"]]
+    first = Swap(here, x_ref, home, swap_send.at[0], swap_recv.at[0], swap_local.at[0])
+    second = Swap(here, q_ref, q_out, swap_send.at[1], swap_recv.at[1], swap_local.at[1])
+    first.start()
+    first.wait()
+    gather = Gather(here, PAIRED, pieces, None, o_ref, (send, recv, fore, back), 0)
+    run_gathers([gather], [], lambda phase: second.start() if phase == 0 else None)
+    second.wait()
+
+
+def gather_keys(x, q, collective_id):
+    rows, cols = x.shape
+    pieces = cut(rows, ("hzy", "zyh", "yhz"))
+    n = 9 * len(pieces) + 1
+    sizes = [SIZES[a] for a in PAIRED]
+    kv, q_out = pl.pallas_call(
+        functools.partial(keys_kernel, pieces),
+        out_shape=(
+            jax.ShapeDtypeStruct((*sizes, rows, cols), x.dtype),
+            jax.ShapeDtypeStruct(q.shape, q.dtype),
+        ),
+        in_specs=[ANY, ANY],
+        out_specs=(ANY, ANY),
+        scratch_shapes=semaphores(n) + [pltpu.SemaphoreType.DMA((2,))] * 3,
+        compiler_params=pltpu.CompilerParams(
+            collective_id=collective_id, has_side_effects=True, vmem_limit_bytes=1 << 20
+        ),
+        name="gather_keys",
+    )(x, q)
+    return kv.reshape(32, rows, cols), q_out
+
+
+def gather_kernel(axes, pieces, x_ref, o_ref, send, recv, fore, back, local):
+    here = coords(axes)
+    greet(axis_peers(axes, here))
+    gather = Gather(here, axes, pieces, x_ref, o_ref, (send, recv, fore, back), 0)
+    own = pltpu.make_async_copy(x_ref, o_ref.at[gather.place], local)
     own.start()
-    copies, latest = [], {}
-    for phase in range(3):
-        for i, (lo, size, order) in enumerate(pieces):
-            if phase:
-                for copy in latest[i]:
-                    copy.wait_recv()
-                if phase == 1 and i == 0:
-                    own.wait()
-            held = [slice(None) if a in order[:phase] else me[AXES.index(a)] for a in AXES]
-            region = o_ref.at[tuple(held) + (pl.ds(lo, size),)]
-            source = region if phase else x_ref.at[pl.ds(lo, size)]
-            latest[i] = []
-            for d in range(1, SIZES[order[phase]]):
-                at = (i * 3 + phase) * 3 + d - 1
-                copy = pltpu.make_async_remote_copy(
-                    src_ref=source,
-                    dst_ref=region,
-                    send_sem=send.at[at],
-                    recv_sem=recv.at[at],
-                    device_id=peer(section, me, order[phase], d),
-                    device_id_type=MESH,
-                )
-                copy.start()
-                latest[i].append(copy)
-            copies += latest[i]
-    for i in range(len(pieces)):
-        for copy in latest[i]:
-            copy.wait_recv()
-    for copy in copies:
-        copy.wait_send()
+    run_gathers([gather], [own], lambda phase: None)
 
 
 def cut(rows, orders):
@@ -101,20 +353,17 @@
     return pieces
 
 
-def seq_gather(x, collective_id, name):
+def seq_gather(x, axes, collective_id, name):
     rows, cols = x.shape
-    pieces = cut(rows, ("xzy", "zyx", "yxz"))
+    pieces = cut(rows, ("xzy", "zyx", "yxz") if axes == PLAIN else ("hzy", "zyh", "yhz"))
     n = 9 * len(pieces)
+    sizes = [SIZES[a] for a in axes]
     return pl.pallas_call(
-        functools.partial(gather_kernel, pieces),
-        out_shape=jax.ShapeDtypeStruct((2, 4, 4, rows, cols), x.dtype),
+        functools.partial(gather_kernel, axes, pieces),
+        out_shape=jax.ShapeDtypeStruct((*sizes, rows, cols), x.dtype),
         in_specs=[ANY],
         out_specs=ANY,
-        scratch_shapes=[
-            pltpu.SemaphoreType.DMA((n,)),
-            pltpu.SemaphoreType.DMA((n,)),
-            pltpu.SemaphoreType.DMA,
-        ],
+        scratch_shapes=semaphores(n + 1) + [pltpu.SemaphoreType.DMA],
         compiler_params=pltpu.CompilerParams(
             collective_id=collective_id, has_side_effects=True, vmem_limit_bytes=1 << 20
         ),
@@ -122,66 +371,60 @@
     )(x).reshape(32, rows, cols)
 
 
-def scatter_kernel(pieces, x_ref, o_ref, send, recv, *bufs):
-    section = lax.axis_index("section")
-    me = seq_coords()
-    greet(axis_peers(section, me))
-    arrived = [bufs[3 * i : 3 * i + 3] for i in range(len(pieces))]
-    partial = [bufs[3 * len(pieces) + 2 * i :][:2] for i in range(len(pieces))]
-    copies, latest = [], {}
-
-    def source(phase, i):
-        lo, size, order = pieces[i]
-        if phase == 0:
-            return x_ref, (pl.ds(lo, size),)
-        return partial[i][phase - 1], ()
-
-    def block(phase, i, coord):
-        lo, size, order = pieces[i]
-        left = [a for a in AXES if a not in order[:phase]]
-        ref, tail = source(phase, i)
+class Scatter:
+    def __init__(self, here, axes, pieces, x_ref, o_ref, send, recv, bufs):
+        self.here, self.axes, self.pieces, self.x, self.o = here, axes, pieces, x_ref, o_ref
+        self.send, self.recv, self.depth = send, recv, len(axes)
+        n, depth = len(pieces), len(axes)
+        self.inbox = [bufs[depth * i : depth * (i + 1)] for i in range(n)]
+        self.partial = [bufs[depth * n + (depth - 1) * i :][: depth - 1] for i in range(n)]
+        self.copies, self.latest = [], {}
+
+    def block(self, phase, i, coord):
+        lo, size, order = self.pieces[i]
+        left = [a for a in self.axes if a not in order[:phase]]
+        ref = self.partial[i][phase - 1] if phase else self.x
+        tail = () if phase else (pl.ds(lo, size),)
         return ref.at[tuple(coord if a == order[phase] else slice(None) for a in left) + tail]
 
-    def launch(phase, i):
-        order = pieces[i][2]
+    def launch(self, phase, i):
+        axis = self.pieces[i][2][phase]
+        self.latest[i] = []
+        for d in range(1, SIZES[axis]):
+            at = (i * self.depth + phase) * 3 + d - 1
+            self.latest[i].append(
+                remote(
+                    self.block(phase, i, lax.rem(self.here[axis] + d, SIZES[axis])),
+                    self.inbox[i][phase].at[d - 1],
+                    self.send.at[at],
+                    self.recv.at[at],
+                    device_at(self.axes, moved(self.here, axis, d)),
+                )
+            )
+        self.copies.extend(self.latest[i])
+
+    def total(self, phase, i):
+        lo, size, order = self.pieces[i]
         axis = order[phase]
-        latest[i] = []
-        for d in range(1, SIZES[axis]):
-            at = (i * 3 + phase) * 3 + d - 1
-            coord = lax.rem(me[AXES.index(axis)] + d, SIZES[axis])
-            copy = pltpu.make_async_remote_copy(
-                src_ref=block(phase, i, coord),
-                dst_ref=arrived[i][phase].at[d - 1],
-                send_sem=send.at[at],
-                recv_sem=recv.at[at],
-                device_id=peer(section, me, axis, d),
-                device_id_type=MESH,
-            )
-            copy.start()
-            latest[i].append(copy)
-        copies.extend(latest[i])
-
-    def total(phase, i):
-        lo, size, order = pieces[i]
-        axis = order[phase]
-        for copy in latest[i]:
+        for copy in self.latest[i]:
             copy.wait_recv()
-        mine = block(phase, i, me[AXES.index(axis)])
-        inbox = arrived[i][phase]
-        left = [SIZES[a] for a in AXES if a not in order[: phase + 1]]
+        mine, inbox = self.block(phase, i, self.here[axis]), self.inbox[i][phase]
+        left = [SIZES[a] for a in self.axes if a not in order[: phase + 1]]
         count = 1
         for extent in left:
             count *= extent
 
         def add(k, carry):
-            at = (k // left[1], k % left[1]) if len(left) == 2 else ((k,) if left else ())
+            at = ()
+            for extent in reversed(left):
+                at, k = (k % extent,) + at, k // extent
             whole = mine[at].astype(jnp.float32) if at else mine[...].astype(jnp.float32)
             for d in range(SIZES[axis] - 1):
                 whole = whole + inbox[(d,) + at].astype(jnp.float32)
-            if phase == 2:
-                o_ref[pl.ds(lo, size), :] = whole.astype(o_ref.dtype)
+            if phase == self.depth - 1:
+                self.o[pl.ds(lo, size), :] = whole.astype(self.o.dtype)
             else:
-                partial[i][phase][at] = whole.astype(jnp.bfloat16)
+                self.partial[i][phase][at] = whole.astype(jnp.bfloat16)
             return carry
 
         if count == 1:
@@ -189,76 +432,235 @@
         else:
             lax.fori_loop(0, count, add, 0)
 
-    for i in range(len(pieces)):
-        launch(0, i)
-    for phase in range(3):
-        for i in range(len(pieces)):
-            total(phase, i)
-            if phase < 2:
-                launch(phase + 1, i)
-    for copy in copies:
-        copy.wait_send()
-
-
-def seq_scatter(x, out_dtype, collective_id, name):
-    _, rows, cols = x.shape
-    pieces = cut(rows, ("yzx", "xyz", "zxy"))
-    n = 9 * len(pieces)
+    def run(self):
+        for i in range(len(self.pieces)):
+            self.launch(0, i)
+        for phase in range(self.depth):
+            for i in range(len(self.pieces)):
+                self.total(phase, i)
+                if phase < self.depth - 1:
+                    self.launch(phase + 1, i)
+        for copy in self.copies:
+            copy.wait_send()
+
+
+def scatter_plan(rows, cols, axes):
+    pieces = cut(rows, ("yzx", "xyz", "zxy") if axes == PLAIN else ("cyzh", "chyz", "czhy"))
+    depth = len(axes)
+    n = 3 * depth * len(pieces)
     inboxes, partials = [], []
     for lo, size, order in pieces:
-        for phase in range(3):
-            left = [SIZES[a] for a in AXES if a not in order[: phase + 1]]
+        for phase in range(depth):
+            left = [SIZES[a] for a in axes if a not in order[: phase + 1]]
             inboxes.append(pltpu.VMEM((SIZES[order[phase]] - 1, *left, size, cols), jnp.bfloat16))
-            if phase < 2:
+            if phase < depth - 1:
                 partials.append(pltpu.VMEM((*left, size, cols), jnp.bfloat16))
+    sems = [pltpu.SemaphoreType.DMA((n,)), pltpu.SemaphoreType.DMA((n,))]
+    return pieces, sems, inboxes + partials
+
+
+def scatter_kernel(axes, pieces, x_ref, o_ref, send, recv, *bufs):
+    here = coords(axes)
+    greet(axis_peers(axes, here))
+    Scatter(here, axes, pieces, x_ref, o_ref, send, recv, bufs).run()
+
+
+def split_axes(x, axes):
+    return x.reshape(*[SIZES[a] for a in axes], *x.shape[1:])
+
+
+def seq_scatter(x, axes, out_dtype, collective_id, name):
+    _, rows, cols = x.shape
+    pieces, sems, bufs = scatter_plan(rows, cols, axes)
     return pl.pallas_call(
-        functools.partial(scatter_kernel, pieces),
+        functools.partial(scatter_kernel, axes, pieces),
         out_shape=jax.ShapeDtypeStruct((rows, cols), out_dtype),
         in_specs=[VMEM],
         out_specs=VMEM,
+        scratch_shapes=sems + bufs,
+        compiler_params=pltpu.CompilerParams(
+            collective_id=collective_id, has_side_effects=True, vmem_limit_bytes=40 << 20
+        ),
+        name=name,
+    )(split_axes(x, axes))
+
+
+def values_kernel(
+    pieces, x_ref, dq_ref, o_ref, dq_out, send, recv, swap_send, swap_recv, swap_local, own, *bufs
+):
+    here = coords(PAIRED)
+    greet(axis_peers(PAIRED, here), here)
+    first = Swap(here, dq_ref, dq_out, swap_send.at[0], swap_recv.at[0], swap_local.at[0])
+    second = Swap(here, own, o_ref, swap_send.at[1], swap_recv.at[1], swap_local.at[1])
+    first.start()
+    Scatter(here, PAIRED, pieces, x_ref, own, send, recv, bufs).run()
+    second.start()
+    first.wait()
+    second.wait()
+
+
+def scatter_values(x, d_queries, collective_id):
+    _, rows, cols = x.shape
+    pieces, sems, bufs = scatter_plan(rows, cols, PAIRED)
+    return pl.pallas_call(
+        functools.partial(values_kernel, pieces),
+        out_shape=(
+            jax.ShapeDtypeStruct((rows, cols), jnp.bfloat16),
+            jax.ShapeDtypeStruct(d_queries.shape, d_queries.dtype),
+        ),
+        in_specs=[VMEM, ANY],
+        out_specs=(ANY, ANY),
+        scratch_shapes=sems
+        + [pltpu.SemaphoreType.DMA((2,))] * 3
+        + [pltpu.VMEM((rows, cols), jnp.bfloat16)]
+        + bufs,
+        compiler_params=pltpu.CompilerParams(
+            collective_id=collective_id, has_side_effects=True, vmem_limit_bytes=40 << 20
+        ),
+        name="scatter_values",
+    )(split_axes(x, PAIRED), d_queries)
+
+
+def final_kernel(
+    pieces, spread, down_rows, x_ref, o_ref, up_ref, send, recv, g_send, g_recv, g_fore, g_back, local,
+    *bufs,
+):
+    here = coords(PLAIN)
+    greet(axis_peers(PLAIN, here))
+    Scatter(here, PLAIN, pieces, x_ref, o_ref, send, recv, bufs).run()
+    own = o_ref.at[pl.ds(down_rows, x_ref.shape[-2] - down_rows)]
+    gather = Gather(here, PLAIN, spread, own, up_ref, (g_send, g_recv, g_fore, g_back), 0)
+    copy = pltpu.make_async_copy(own, up_ref.at[gather.place], local)
+    copy.start()
+    run_gathers([gather], [copy], lambda phase: None)
+
+
+def scatter_final(x, down_rows, collective_id):
+    _, rows, cols = x.shape
+    pieces, sems, bufs = scatter_plan(rows, cols, PLAIN)
+    spread = cut(rows - down_rows, ("xzy", "zyx", "yxz"))
+    out, ups = pl.pallas_call(
+        functools.partial(final_kernel, pieces, spread, down_rows),
+        out_shape=(
+            jax.ShapeDtypeStruct((rows, cols), jnp.float32),
+            jax.ShapeDtypeStruct((2, 4, 4, rows - down_rows, cols), jnp.float32),
+        ),
+        in_specs=[VMEM],
+        out_specs=(VMEM, VMEM),
+        scratch_shapes=sems + semaphores(9 * len(spread) + 1) + [pltpu.SemaphoreType.DMA] + bufs,
+        compiler_params=pltpu.CompilerParams(
+            collective_id=collective_id, has_side_effects=True, vmem_limit_bytes=40 << 20
+        ),
+        name="scatter_final",
+    )(split_axes(x, PLAIN))
+    return out[:down_rows], ups.reshape(32, rows - down_rows, cols)
+
+
+def stats_kernel(x_ref, o_ref, near_ref, far_ref, send, recv):
+    here = coords(PAIRED)
+    near = [{**here, "h": (here["h"] + a) % 2, "c": (here["c"] + b) % 2} for a, b in ((0, 1), (1, 0), (1, 1))]
+    far = [
+        {**here, "y": (here["y"] + a) % 2, "z": (here["z"] + b) % 4}
+        for a in range(2)
+        for b in range(4)
+        if a or b
+    ]
+    greet([device_at(PAIRED, place) for place in near + far])
+    total = x_ref[...]
+    o_ref[...] = total
+    at = 0
+    for places, inbox in ((near, near_ref), (far, far_ref)):
+        copies = [
+            remote(o_ref, inbox.at[k], send.at[at + k], recv.at[at + k], device_at(PAIRED, place))
+            for k, place in enumerate(places)
+        ]
+        at += len(places)
+        for copy in copies:
+            copy.wait()
+        for k in range(len(places)):
+            total = total + inbox[k]
+        o_ref[...] = total
+
+
+def sum_stats(x, collective_id):
+    return pl.pallas_call(
+        stats_kernel,
+        out_shape=jax.ShapeDtypeStruct(x.shape, x.dtype),
+        in_specs=[VMEM],
+        out_specs=VMEM,
         scratch_shapes=[
-            pltpu.SemaphoreType.DMA((n,)),
-            pltpu.SemaphoreType.DMA((n,)),
-            *inboxes,
-            *partials,
+            pltpu.VMEM((3, *x.shape), x.dtype),
+            pltpu.VMEM((7, *x.shape), x.dtype),
+            pltpu.SemaphoreType.DMA((10,)),
+            pltpu.SemaphoreType.DMA((10,)),
         ],
         compiler_params=pltpu.CompilerParams(
-            collective_id=collective_id, has_side_effects=True, vmem_limit_bytes=40 << 20
-        ),
-        name=name,
-    )(x.reshape(2, 4, 4, rows, cols))
-
-
-def exchange_kernel(axis, count, apart, x_ref, o_ref, send, recv, local):
-    me = lax.axis_index(axis)
+            collective_id=collective_id, has_side_effects=True, vmem_limit_bytes=4 << 20
+        ),
+        name="sum_stats",
+    )(x)
+
+
+def grads_kernel(x_ref, normed_ref, o_ref, normed_out, send, recv, local, swap_send, swap_recv, swap_local):
+    here = coords(PAIRED)
+    me, device = group_place("paired section", here)
+    others = [lax.rem(me + d, 4) for d in range(1, 4)]
+    greet([device(k) for k in others], here)
+    own = pltpu.make_async_copy(x_ref, o_ref.at[me], local)
+    own.start()
+    copies = [
+        remote(x_ref, o_ref.at[me], send.at[d], recv.at[d], device(k)) for d, k in enumerate(others)
+    ]
+    swap = Swap(here, normed_ref, normed_out, swap_send, swap_recv, swap_local)
+    swap.start()
+    own.wait()
+    for copy in copies:
+        copy.wait()
+    swap.wait()
+
+
+def gather_grads(x, normed, collective_id):
+    return pl.pallas_call(
+        grads_kernel,
+        out_shape=(
+            jax.ShapeDtypeStruct((4, *x.shape), x.dtype),
+            jax.ShapeDtypeStruct(normed.shape, normed.dtype),
+        ),
+        in_specs=[ANY, ANY],
+        out_specs=(ANY, ANY),
+        scratch_shapes=[pltpu.SemaphoreType.DMA((3,))] * 2 + [pltpu.SemaphoreType.DMA] * 4,
+        compiler_params=pltpu.CompilerParams(
+            collective_id=collective_id, has_side_effects=True, vmem_limit_bytes=1 << 20
+        ),
+        name="gather_grads",
+    )(x, normed)
+
+
+def group_place(group, here):
+    if group == "section":
+        return here["m"] * 2 + here["c"], lambda k: device_at("x", {**here, "m": k // 2, "c": k % 2})
+    return here["m"] * 2 + here["l"], lambda k: device_at("h", {**here, "m": k // 2, "l": k % 2})
+
+def exchange_kernel(group, count, apart, x_ref, o_ref, send, recv, local):
+    me, device = group_place(group, coords(PLAIN))
     others = [lax.rem(me + d, count) for d in range(1, count)]
-    device = lambda k: (
-        (lax.axis_index("section"), k) if axis == "seq" else (k, lax.axis_index("seq"))
-    )
     greet([device(k) for k in others])
     own = pltpu.make_async_copy(x_ref.at[me] if apart else x_ref, o_ref.at[me], local)
     own.start()
-    copies = []
-    for d, k in enumerate(others):
-        copy = pltpu.make_async_remote_copy(
-            src_ref=x_ref.at[k] if apart else x_ref,
-            dst_ref=o_ref.at[me],
-            send_sem=send.at[d],
-            recv_sem=recv.at[d],
-            device_id=device(k),
-            device_id_type=MESH,
-        )
-        copy.start()
-        copies.append(copy)
+    copies = [
+        remote(x_ref.at[k] if apart else x_ref, o_ref.at[me], send.at[d], recv.at[d], device(k))
+        for d, k in enumerate(others)
+    ]
     own.wait()
     for copy in copies:
         copy.wait()
 
 
-def exchange(x, axis, count, apart, collective_id, name):
+def exchange(x, group, apart, collective_id, name):
+    count = 4
     shape = x.shape[1:] if apart else x.shape
     return pl.pallas_call(
-        functools.partial(exchange_kernel, axis, count, apart),
+        functools.partial(exchange_kernel, group, count, apart),
         out_shape=jax.ShapeDtypeStruct((count, *shape), x.dtype),
         in_specs=[ANY],
         out_specs=ANY,
@@ -449,66 +851,72 @@
     tok_dev = context.shape[0]
     slot_dev = memory.shape[0]
     seq_size = lax.axis_size("seq")
-    seq_index = lax.axis_index("seq")
+    here = coords(PLAIN)
+    paired_index = here["y"] * 16 + here["z"] * 4 + here["h"] * 2 + here["c"]
     section_extent = lax.axis_size("section")
     section_index = lax.axis_index("section")
     every_row = jnp.concatenate([context, memory], axis=0)
-    weights = seq_gather(
-        jnp.concatenate([key_weight, value_weight, value_down_map], axis=1), 1, "gather_weights"
-    ).reshape(MODEL_DIM, 3 * HD)
-    projected = jnp.dot(every_row, weights, preferred_element_type=f32)
+    kv_weight, down, query_sum, output_weight, normed_gradient, decoder_gain = opening(
+        jnp.concatenate([key_weight, value_weight], axis=1),
+        value_down_map,
+        memory,
+        query_weight,
+        output_weight,
+        normed_gradient,
+        decoder_gain.reshape(-1, 128),
+        1,
+    )
+    decoder_gain = decoder_gain.reshape(-1)
+    projected = jnp.dot(every_row, kv_weight, preferred_element_type=f32)
     query_low = jnp.dot(memory, query_down_map, preferred_element_type=f32).astype(bf16)
-    value_low = projected[:, 2 * HD :].astype(bf16)
+    value_low = jnp.dot(every_row, down, preferred_element_type=f32).astype(bf16)
     queries = (
-        jnp.dot(memory, query_weight, preferred_element_type=f32)
-        + adapter_scale * jnp.dot(query_low, query_up_map, preferred_element_type=f32)
+        query_sum + adapter_scale * jnp.dot(query_low, query_up_map, preferred_element_type=f32)
     ).astype(bf16)
     keys = projected[:, :HD].astype(bf16)
     values = (
         projected[:, HD : 2 * HD]
         + adapter_scale * jnp.dot(value_low, value_up_map, preferred_element_type=f32)
     ).astype(bf16)
-    kv = seq_gather(jnp.concatenate([keys, values], axis=1), 2, "gather_keys")
-    span, rows = row_bounds(document_slots, seq_index * slot_dev, slot_dev, seq_size)
-    attended, ot, top, mass = attend(span, rows, queries, kv, tok_dev)
-    slots_all = seq_gather(attended, 3, "gather_attended").reshape(seq_size * slot_dev, -1)
+    kv, queries_here = gather_keys(jnp.concatenate([keys, values], axis=1), queries, 2)
+    span, rows = row_bounds(document_slots, paired_index * slot_dev, slot_dev, seq_size)
+    attended, ot, top, mass = attend(span, rows, queries_here, kv, tok_dev)
+    slots_all = seq_gather(attended, PAIRED, 3, "gather_attended").reshape(seq_size * slot_dev, -1)
     hidden_part = jnp.dot(slots_all, output_weight, preferred_element_type=f32).astype(bf16)
     pieces = exchange(
         hidden_part.reshape(section_extent, -1, hidden_part.shape[1]),
-        "section", 4, True, 4, "sum_hidden",
+        "paired section", True, 4, "sum_hidden",
     )
     hidden = jnp.sum(pieces.astype(f32), axis=0)
     total_slots = slot_dev * seq_size
     weighted = total_slots ** (-0.5) * normed_gradient.astype(f32) * decoder_gain[None, :]
     stats = jnp.stack([jnp.sum(hidden * hidden, axis=1), jnp.sum(weighted * hidden, axis=1)])
-    stats = jnp.sum(
-        exchange(stats.reshape(8, 128), "seq", 32, False, 5, "sum_stats"), axis=0
-    ).reshape(2, -1)
+    stats = sum_stats(stats.reshape(8, 128), 5).reshape(2, -1)
     square_sum, cross_sum = stats[0], stats[1]
     inv_rms = lax.rsqrt(square_sum / MODEL_DIM + epsilon)
     normed = (hidden * inv_rms[:, None] * decoder_gain[None, :]).astype(bf16)
     d_hidden = (
         inv_rms[:, None] * weighted - hidden * (inv_rms**3 * cross_sum / MODEL_DIM)[:, None]
     ).astype(bf16)
-    grads_all = exchange(d_hidden, "section", 4, False, 6, "gather_grads").reshape(
-        total_slots, -1
-    )
+    grads_all, normed = gather_grads(d_hidden, normed, 6)
+    grads_all = grads_all.reshape(total_slots, -1)
     d_part = contract(grads_all, output_weight, 1, 1).astype(bf16)
     d_attended = seq_scatter(
-        d_part.reshape(seq_size, slot_dev, -1), bf16, 7, "scatter_attended"
+        d_part.reshape(seq_size, slot_dev, -1), PAIRED, bf16, 7, "scatter_attended"
     )
     d_queries, dv_part = attend_backward(
-        span, rows, queries, d_attended, kv, ot, top, mass, tok_dev
-    )
-    d_values = seq_scatter(dv_part, bf16, 8, "scatter_values")
+        span, rows, queries_here, d_attended, kv, ot, top, mass, tok_dev
+    )
+    d_values, d_queries = scatter_values(dv_part, d_queries, 8)
     query_up_part = adapter_scale * contract(query_low, d_queries, 0, 0)
     value_up_part = adapter_scale * contract(value_low, d_values, 0, 0)
     query_part = adapter_scale * contract(d_queries, query_up_map, 1, 1)
     value_part = adapter_scale * contract(d_values, value_up_map, 1, 1)
     backs = jnp.sum(
         exchange(
-            jnp.concatenate([query_part, value_part], axis=0), "section", 4, False, 9, "sum_backs"
-        ),
+            jnp.concatenate([query_part, value_part], axis=0).astype(bf16),
+            "section", False, 9, "sum_backs",
+        ).astype(f32),
         axis=0,
     ).astype(bf16)
     width = memory.shape[1] // section_extent
@@ -527,10 +935,10 @@
         + [jnp.pad(ups.astype(bf16), ((0, 0), (0, -up_rows % 16), (0, 0)))],
         axis=1,
     )
-    final = seq_scatter(final_parts, f32, 10, "scatter_final")
     down_rows = MODEL_DIM // section_extent // seq_size
-    grad_qa, grad_va = final[:down_rows], final[down_rows : 2 * down_rows]
-    ups = exchange(final[2 * down_rows :], "seq", 32, False, 11, "gather_ups")[:, :up_rows]
+    final, ups = scatter_final(final_parts, 2 * down_rows, 10)
+    grad_qa, grad_va = final[:down_rows], final[down_rows:]
+    ups = ups[:, :up_rows]
     ups = jnp.moveaxis(ups.reshape(lanes, 128, 128), 0, 1).reshape(128, lanes * 128)
     split = query_up_part.shape[1]
     return (normed, grad_qa, grad_va, ups[:, :split], ups[:, split:])

time: 361 us -> 304 us (0.84)
  Pallas kernels: 319 us -> 275 us
  matrix products: 21.6 us -> 12.3 us
    pallas_call x11 -> x10, Pallas kernels: 314 us -> 254 us  [the longest x1 49.4 us: opening(): pl.pallas_call(functools.partial(opening_kernel, pieces, half_pieces), ou...]
    pallas_call x1, Pallas kernels: 3.97 us -> 11.2 us  [attend_backward(): pl.pallas_call(functools.partial(backward_kernel, context_rows), out_shap...]
    pallas_call x1, Pallas kernels: 1.75 us -> 8.82 us  [attend(): pl.pallas_call(functools.partial(attend_kernel, context_rows), out_shape=...]
    dot_general x2, matrix products: 11.9 us -> 4.86 us  [the longest x1 3.26 us: body(): jnp.dot(every_row, down, preferred_element_type=f32).astype(bf16)]
where the time goes in v2:
time: 304 us
  Pallas kernels  275 us (90%)
  matrix products  12.3 us (4%)
  local copies, waits for them, and re-layouts  9 us (3%)
  between operations  4.49 us (1%)
  other arithmetic  3.21 us (1%)
    pallas_call x1, Pallas kernels, opening(): pl.pallas_call(functools.partial(opening_kernel, pieces, half_pieces), ou...  49.4 us
    pallas_call x1, Pallas kernels, scatter_final(): pl.pallas_call(functools.partial(final_kernel, pieces, spread, down_rows)...  36 us
    pallas_call x1, Pallas kernels, seq_scatter(): pl.pallas_call(functools.partial(scatter_kernel, axes, pieces), out_shape...  33.1 us
    pallas_call x1, Pallas kernels, gather_keys(): pl.pallas_call(functools.partial(keys_kernel, pieces), out_shape=(jax.Sha...  31.6 us
    pallas_call x1, Pallas kernels, seq_gather(): pl.pallas_call(functools.partial(gather_kernel, axes, pieces), out_shape=...  28.8 us
    pallas_call x2, Pallas kernels, exchange(): pl.pallas_call(functools.partial(exchange_kernel, group, count, apart), o...  28 us
    pallas_call x1, Pallas kernels, scatter_values(): pl.pallas_call(functools.partial(values_kernel, pieces), out_shape=(jax.S...  21.7 us
    pallas_call x1, Pallas kernels, gather_grads(): pl.pallas_call(grads_kernel, out_shape=(jax.ShapeDtypeStruct((4, *x.shape...  14.2 us

profile of v2, /device:TPU:0, one launch (start us, length us, event | category | flops | bytes accessed | tf_op | source)
XLA Modules:
  0.0 303.6 jit_solution(7168506701945052534)
XLA Ops:
  0.7 0.9 select_reduce_fusion
  1.7 0.6 multiply_bitcast_fusion
  3.0 0.6 reduce_min.18
  6.5 2.7 constant_dynamic-update-slice_fusion.1
  9.4 49.4 %opening.1 = (bf16[2,4,4,256,256]{4,3,2,1,0:T(8,128)(2,1)}, bf16[2,4,4,2,128,128]{5,4,3,2,1,0:T(8,128)(2,1)}, f32[64,1024]{1,0:T(8,128)S(1)}, bf16[1024,256]{1,0...) custom-call(bf16[256,256]{1,0:T(8,128)(2,1)S(1)} %pad_maximum_fusion.2.kv_ref, ...), custom_call_target="tpu_custom_call" | custom-call | tf_op jit(solution)/shard_map/opening/pallas_call | solution.py:264
  58.8 3.3 %convolution_convert_fusion.4 = bf16[320,128]{1,0:T(8,128)(2,1)S(1)} fusion(bf16[320,8192]{1,0:T(8,128)(2,1)S(1)} %constant_dynamic-update-slice_fusion, bf16[8192,128]{1,0:T(8,128)(2,1)} %bitcast.71), kind=kOutput, calls=%fused_computation.18 | convolution fusion | flops 671129600 | bytes 7421952 | tf_op jit(solution)/shard_map/dot_general | solution.py:872
  62.1 1.6 fusion.21
  64.0 0.5 convolution_convert_fusion.5
  64.9 31.6 %gather_keys.1 = (bf16[2,4,2,2,320,256]{5,4,3,2,1,0:T(8,128)(2,1)S(1)}, bf16[64,1024]{1,0:T(8,128)(2,1)S(1)}) custom-call(bf16[320,256]{1,0:T(8,128)(2,1)S(1)} %pad_maximum_fusion.1.x_ref, bf16[64,1024]{1,0:T(8,128)(2,1)S(1)} %fusion.5.q_ref), custom_call_target="tpu_custom_call" | custom-call | tf_op jit(solution)/shard_map/gather_keys/pallas_call | solution.py:317
  96.5 8.8 %attend.1 = (bf16[64,1024]{1,0:T(8,128)(2,1)S(1)}, f32[128,512]{1,0:T(8,128)S(1)}, f32[8,512]{1,0:T(8,128)S(1)}, f32[8,512]{1,0:T(8,128)S(1)}) custom-call(s32[2]{0:T(128)S(1)} %pad_add_fusion.span, s32[8,512]{1,0:T(8,128)S(1)} %tile.10.rows_ref, bf16[64,1024]{1,0:T(8,128)(2,1)S(1)} %get-tuple-element.28.q_ref, bf16[32,320,256]{2,1,0:T(8,128)(2,1)S(1)} %bitcast.57), custom_call_target="tpu_custom_call" | custom-call | tf_op jit(solution)/shard_map/attend/pallas_call | solution.py:791
  105.3 28.8 %gather_attended.1 = bf16[2,4,2,2,64,1024]{5,4,3,2,1,0:T(8,128)(2,1)S(1)} custom-call(bf16[64,1024]{1,0:T(8,128)(2,1)S(1)} %get-tuple-element.30.x_ref), custom_call_target="tpu_custom_call" | custom-call | tf_op jit(solution)/shard_map/gather_attended/pallas_call | solution.py:361
  134.2 1.3 convolution_convert_fusion.1
  135.4 17.9 %sum_hidden.1 = bf16[4,512,256]{2,1,0:T(8,128)(2,1)S(1)} custom-call(bf16[4,512,256]{2,1,0:T(8,128)(2,1)S(1)} %bitcast.63), custom_call_target="tpu_custom_call" | custom-call | tf_op jit(solution)/shard_map/sum_hidden/pallas_call | solution.py:662
  153.5 0.2 multiply_reduce_fusion.1
  153.7 11.7 %sum_stats.1 = f32[8,128]{1,0:T(8,128)S(1)} custom-call(f32[8,128]{1,0:T(8,128)S(1)} %reshape.121.x_ref), custom_call_target="tpu_custom_call" | custom-call | tf_op jit(solution)/shard_map/sum_stats/pallas_call | solution.py:586
  165.7 14.2 %gather_grads.1 = (bf16[4,512,256]{2,1,0:T(8,128)(2,1)S(1)}, bf16[512,256]{1,0:T(8,128)(2,1)S(1)}) custom-call(bf16[512,256]{1,0:T(8,128)(2,1)S(1)} %get-tuple-element.60.x_ref, bf16[512,256]{1,0:T(8,128)(2,1)S(1)} %get-tuple-element.59.normed_ref), custom_call_target="tpu_custom_call" | custom-call | tf_op jit(solution)/shard_map/gather_grads/pallas_call | solution.py:623
  179.9 1.3 convolution_convert_fusion
  181.2 33.1 %scatter_attended.1.g_ref = bf16[64,1024]{1,0:T(8,128)(2,1)S(1)} custom-call(bf16[2,4,2,2,64,1024]{5,4,3,2,1,0:T(8,128)(2,1)S(1)} %bitcast.56), custom_call_target="tpu_custom_call" | custom-call | tf_op jit(solution)/shard_map/scatter_attended/pallas_call | solution.py:475
  214.3 11.2 %attend_backward.1 = (bf16[64,1024]{1,0:T(8,128)(2,1)S(1)}, bf16[32,320,128]{2,1,0:T(8,128)(2,1)S(1)}) custom-call(s32[2]{0:T(128)S(1)} %pad_add_fusion.span, s32[8,512]{1,0:T(8,128)S(1)} %tile.10.rows_ref, bf16[64,1024]{1,0:T(8,128)(2,1)S(1)} %get-tuple-element.28.q_ref, bf16[64,1024]{1,0:T(8,128)(2,1)S(1)} %scatter_attended.1.g_ref, ...), custom_call_target="tpu_custom_call" | custom-call | tf_op jit(solution)/shard_map/attend_backward/pallas_call | solution.py:807
  225.6 21.7 %scatter_values.1 = (bf16[320,128]{1,0:T(8,128)(2,1)S(1)}, bf16[64,1024]{1,0:T(8,128)(2,1)S(1)}) custom-call(bf16[2,4,2,2,320,128]{5,4,3,2,1,0:T(8,128)(2,1)S(1)} %bitcast.62, bf16[64,1024]{1,0:T(8,128)(2,1)S(1)} %get-tuple-element.40.dq_ref), custom_call_target="tpu_custom_call" | custom-call | tf_op jit(solution)/shard_map/scatter_values/pallas_call | solution.py:505
  247.5 0.2 fusion.3
  248.0 0.2 copy.29
  248.7 10.1 %sum_backs.1 = bf16[4,384,128]{2,1,0:T(8,128)(2,1)S(1)} custom-call(bf16[384,128]{1,0:T(8,128)(2,1)S(1)} %pad_maximum_fusion.3.x_ref), custom_call_target="tpu_custom_call" | custom-call | tf_op jit(solution)/shard_map/sum_backs/pallas_call | solution.py:662
  258.9 2.0 convolution_convert_fusion.2
  260.9 1.3 convolution_convert_fusion.3
  262.3 36.0 %scatter_final.1 = (f32[176,128]{1,0:T(8,128)S(1)}, f32[2,4,4,48,128]{4,3,2,1,0:T(8,128)S(1)}) custom-call(bf16[2,4,4,176,128]{4,3,2,1,0:T(8,128)(2,1)S(1)} %bitcast.59), custom_call_target="tpu_custom_call" | custom-call | tf_op jit(solution)/shard_map/scatter_final/pallas_call | solution.py:542
  298.3 0.6 fusion.20
  298.9 0.9 reshape.126
  299.8 1.3 copy.30
  301.1 1.0 copy.31
  302.1 0.7 copy.32
  302.9 0.7 copy.36
  (60 shorter events, 2.6 us)
Async XLA Ops:
  0.6 63.3 %copy-start = (bf16[8192,128]{1,0:T(8,128)(2,1)S(1)}, bf16[8192,128]{1,0:T(8,128)(2,1)}, u32[]{:S(2)}) copy-start(bf16[8192,128]{1,0:T(8,128)(2,1)} %param.18) | copy-start | bytes 6291460
  6.5 2.8 copy-start.7
  6.5 2.9 copy-start.11
  6.5 2.9 copy-start.12
  6.5 2.9 copy-start.3
  6.5 2.9 copy-start.4
  6.5 2.9 copy-start.5
  9.3 52.7 %copy-start.6 = (bf16[320,8192]{1,0:T(8,128)(2,1)}, bf16[320,8192]{1,0:T(8,128)(2,1)S(1)}, u32[]{:S(2)}) copy-start(bf16[320,8192]{1,0:T(8,128)(2,1)S(1)} %constant_dynamic-update-slice_fusion) | copy-start | bytes 15728644
  58.8 3.3 %copy-start.13 = (bf16[2,4,4,256,256]{4,3,2,1,0:T(8,128)(2,1)S(1)}, bf16[2,4,4,256,256]{4,3,2,1,0:T(8,128)(2,1)}, u32[]{:S(2)}) copy-start(bf16[2,4,4,256,256]{4,3,2,1,0:T(8,128)(2,1)} %get-tuple-element.25) | copy-start | bytes 12582916
  62.1 1.6 copy-start.10
  62.1 1.9 copy-start.8
  63.7 1.0 copy-start.9
  96.5 37.7 %copy-start.2 = (bf16[2,4,2,2,320,256]{5,4,3,2,1,0:T(8,128)(2,1)}, bf16[2,4,2,2,320,256]{5,4,3,2,1,0:T(8,128)(2,1)S(1)}, u32[]{:S(2)}) copy-start(bf16[2,4,2,2,320,256]{5,4,3,2,1,0:T(8,128)(2,1)S(1)} %get-tuple-element.29) | copy-start | bytes 15728644
  262.2 41.4 %copy-start.1 = (bf16[8192,128]{1,0:T(8,128)(2,1)S(1)}, bf16[8192,128]{1,0:T(8,128)(2,1)}, u32[]{:S(2)}) copy-start(bf16[8192,128]{1,0:T(8,128)(2,1)} %param.18) | copy-start | bytes 6291460

commit v3 on v2

v3 whole, which is shorter than its diff:
```python
import functools

import jax
import jax.numpy as jnp
from jax import lax
from jax.experimental import pallas as pl
from jax.experimental.pallas import tpu as pltpu
from jax.sharding import PartitionSpec as P

MODEL_DIM = 8192
HEADS_HERE = 8
HD = 128
ROWS = 512
GROUP = 2

adapter_scale = 0.25
epsilon = 1e-05
mask_fill = -1e30
score_scale = HD ** (-0.5)
exp2_scale = score_scale * 1.4426950408889634

MESH = pl.DeviceIdType.MESH
ANY = pl.BlockSpec(memory_space=pl.ANY)
VMEM = pl.BlockSpec(memory_space=pltpu.VMEM)
HBM = pl.BlockSpec(memory_space=pltpu.HBM)

SIZES = {"y": 2, "z": 4, "x": 4, "h": 2, "c": 2}
PLAIN, PAIRED = "yzx", "yzhc"


def coords(axes):
    seq, section = lax.axis_index("seq"), lax.axis_index("section")
    here = {"y": seq // 16, "z": (seq // 4) % 4, "x": seq % 4, "m": section // 2, "c": section % 2}
    here["h"], here["l"] = here["x"] // 2, here["x"] % 2
    return here


def device_at(axes, here):
    x = here["x"] if "x" in axes else here["h"] * 2 + here["l"]
    return (here["m"] * 2 + here["c"], here["y"] * 16 + here["z"] * 4 + x)


def moved(here, axis, step):
    return {**here, axis: lax.rem(here[axis] + step, SIZES[axis])}


def greet(devices, here=None):
    barrier = pltpu.get_barrier_semaphore()
    for device in devices:
        pl.semaphore_signal(barrier, inc=1, device_id=device, device_id_type=MESH)
    if here is not None:

        @pl.when(here["c"] != here["l"])
        def _():
            pl.semaphore_signal(
                barrier, inc=1, device_id=swap_device(here), device_id_type=MESH
            )

    extra = 0 if here is None else lax.rem(here["c"] + here["l"], 2)
    pl.semaphore_wait(barrier, len(devices) + extra)


def swap_device(here):
    return device_at("h", {**here, "c": here["l"], "l": here["c"]})


class Swap:
    def __init__(self, here, source, target, send, recv, local):
        self.apart = here["c"] != here["l"]
        self.there = lambda: pltpu.make_async_remote_copy(
            src_ref=source,
            dst_ref=target,
            send_sem=send,
            recv_sem=recv,
            device_id=swap_device(here),
            device_id_type=MESH,
        )
        self.stays = lambda: pltpu.make_async_copy(source, target, local)

    def start(self):
        @pl.when(self.apart)
        def _():
            self.there().start()

        @pl.when(jnp.logical_not(self.apart))
        def _():
            self.stays().start()

    def wait(self):
        @pl.when(self.apart)
        def _():
            self.there().wait()

        @pl.when(jnp.logical_not(self.apart))
        def _():
            self.stays().wait()


def axis_peers(axes, here):
    return [device_at(axes, moved(here, a, d)) for a in axes for d in range(1, SIZES[a])]


def remote(source, target, send, recv, device):
    copy = pltpu.make_async_remote_copy(
        src_ref=source,
        dst_ref=target,
        send_sem=send,
        recv_sem=recv,
        device_id=device,
        device_id_type=MESH,
    )
    copy.start()
    return copy


class Gather:
    def __init__(self, here, axes, pieces, source, target, sems, base):
        self.here, self.axes, self.pieces, self.base = here, axes, pieces, base
        self.source, self.target = source, target
        self.send, self.recv, self.fore, self.back = sems
        self.place = tuple(here[a] for a in axes)
        self.paired = "c" in axes
        self.partner = device_at(axes, moved(here, "c", 1)) if self.paired else None
        self.copies, self.latest, self.passed = [], {}, []

    def at(self, phase, i, d):
        return self.base + (i * 3 + phase) * 3 + d

    def begin(self):
        if self.paired:
            own = self.target.at[self.place]
            sem = self.base + 9 * len(self.pieces)
            self.passed.append(
                remote(
                    own if self.source is None else self.source,
                    own,
                    self.fore.at[sem],
                    self.back.at[sem],
                    self.partner,
                )
            )

    def arrived(self, phase, i):
        part, order = self.pieces[i]
        axis = order[phase]
        for d, copy in enumerate(self.latest[i]):
            copy.wait_recv()
            if self.paired:
                came = {**self.here, axis: lax.rem(self.here[axis] + SIZES[axis] - d - 1, SIZES[axis])}
                region = self.target.at[
                    tuple(slice(None) if a in order[:phase] else came[a] for a in self.axes)
                    + part
                ]
                at = self.at(phase, i, d)
                self.passed.append(
                    remote(region, region, self.fore.at[at], self.back.at[at], self.partner)
                )

    def launch(self, phase, i):
        part, order = self.pieces[i]
        held = tuple(slice(None) if a in order[:phase] else self.here[a] for a in self.axes)
        region = self.target.at[held + part]
        source = region if phase or self.source is None else self.source.at[part]
        self.latest[i] = []
        for d in range(1, SIZES[order[phase]]):
            at = self.at(phase, i, d - 1)
            device = device_at(self.axes, moved(self.here, order[phase], d))
            self.latest[i].append(remote(source, region, self.send.at[at], self.recv.at[at], device))
        self.copies += self.latest[i]

    def finish(self):
        for i in range(len(self.pieces)):
            self.arrived(2, i)
        for copy in self.passed:
            copy.wait_recv()
        for copy in self.copies + self.passed:
            copy.wait_send()


def run_gathers(gathers, owns, between):
    for gather in gathers:
        gather.begin()
    for phase in range(3):
        for gather in gathers:
            for i in range(len(gather.pieces)):
                if phase:
                    gather.arrived(phase - 1, i)
                    if phase == 1:
                        while owns:
                            owns.pop().wait()
                gather.launch(phase, i)
        between(phase)
    for gather in gathers:
        gather.finish()


def semaphores(count):
    return [pltpu.SemaphoreType.DMA((count,)) for _ in range(4)]


def opening_kernel(
    pieces, half_pieces, kv_ref, down_ref, memory_ref, weight_ref, wo_ref,
    kv_all, down_all, acc_ref, wo_out,
    send, recv, fore, back, buffer, loads, local, swap_send, swap_recv, swap_local,
):
    here = coords(PLAIN)
    depth = buffer.shape[1]
    count = weight_ref.shape[0] // depth

    def load(k):
        return pltpu.make_async_copy(
            weight_ref.at[pl.ds(k * depth, depth)], buffer.at[k % 3], loads.at[k % 3]
        )

    for k in range(2):
        load(k).start()
    greet(axis_peers(PLAIN + "c", here), here)
    swap = Swap(here, wo_ref, wo_out, swap_send, swap_recv, swap_local)
    half = down_ref.shape[0] // 2
    own_half = down_ref.at[pl.ds(here["c"] * half, half)]
    sems = (send, recv, fore, back)
    plain = Gather(here, PLAIN, pieces, kv_ref, kv_all, sems, 0)
    shared = Gather(
        here, PLAIN + "c", half_pieces, own_half, down_all, sems, 9 * len(pieces) + 1
    )
    owns = [
        pltpu.make_async_copy(kv_ref, kv_all.at[plain.place], local.at[0]),
        pltpu.make_async_copy(own_half, down_all.at[shared.place], local.at[1]),
    ]
    for own in owns:
        own.start()
    acc_ref[...] = jnp.zeros_like(acc_ref)

    def between(phase):
        if phase < 2:
            return
        swap.start()
        for k in range(count):
            load(k).wait()
            if k + 2 < count:
                load(k + 2).start()
            acc_ref[...] += jnp.dot(
                memory_ref[:, k * depth : (k + 1) * depth],
                buffer[k % 3],
                preferred_element_type=jnp.float32,
            )

    run_gathers([plain, shared], owns, between)
    swap.wait()


def opening(kv_weight, down, memory, query_weight, output_weight, collective_id):
    rows, cols = kv_weight.shape
    half = down.shape[0] // 2
    pieces = cut(rows, cols, ORDERS[PLAIN])
    half_pieces = cut(half, down.shape[1], ORDERS[PLAIN])
    n = 9 * len(pieces) + 1 + 9 * len(half_pieces) + 1
    outs = pl.pallas_call(
        functools.partial(opening_kernel, pieces, half_pieces),
        out_shape=(
            jax.ShapeDtypeStruct((2, 4, 4, rows, cols), kv_weight.dtype),
            jax.ShapeDtypeStruct((2, 4, 4, 2, half, down.shape[1]), down.dtype),
            jax.ShapeDtypeStruct((memory.shape[0], query_weight.shape[1]), jnp.float32),
            jax.ShapeDtypeStruct(output_weight.shape, output_weight.dtype),
        ),
        in_specs=[ANY, ANY, VMEM, HBM, ANY],
        out_specs=(ANY, ANY, VMEM, ANY),
        scratch_shapes=semaphores(n)
        + [
            pltpu.VMEM((3, 1024, query_weight.shape[1]), jnp.bfloat16),
            pltpu.SemaphoreType.DMA((3,)),
            pltpu.SemaphoreType.DMA((2,)),
            pltpu.SemaphoreType.DMA,
            pltpu.SemaphoreType.DMA,
            pltpu.SemaphoreType.DMA,
        ],
        compiler_params=pltpu.CompilerParams(
            collective_id=collective_id, has_side_effects=True, vmem_limit_bytes=46 << 20
        ),
        name="opening",
    )(kv_weight, down, memory, query_weight, output_weight)
    return (
        outs[0].reshape(32 * rows, cols),
        outs[1].reshape(32 * 2 * half, down.shape[1]),
        *outs[2:],
    )


def keys_kernel(
    pieces, x_ref, q_ref, ng_ref, gain_ref, o_ref, q_out, ng_out, gain_out,
    send, recv, fore, back, swap_send, swap_recv, swap_local,
):
    here = coords(PAIRED)
    greet(axis_peers(PAIRED, here), here)
    home = o_ref.at[here["y"], here["z"], here["h"], here["l"]]
    ends = ((x_ref, home), (q_ref, q_out), (gain_ref, gain_out), (ng_ref, ng_out))
    swaps = [
        Swap(here, a, b, swap_send.at[i], swap_recv.at[i], swap_local.at[i])
        for i, (a, b) in enumerate(ends)
    ]
    swaps[0].start()
    swaps[0].wait()
    gather = Gather(here, PAIRED, pieces, None, o_ref, (send, recv, fore, back), 0)

    def between(phase):
        if phase == 2:
            for swap in swaps[1:]:
                swap.start()

    run_gathers([gather], [], between)
    for swap in swaps[1:]:
        swap.wait()


def gather_keys(x, q, normed_gradient, gain, collective_id):
    rows, cols = x.shape
    pieces = cut(rows, cols, ORDERS[PAIRED])
    n = 9 * len(pieces) + 1
    sizes = [SIZES[a] for a in PAIRED]
    swapped = [jax.ShapeDtypeStruct(a.shape, a.dtype) for a in (q, normed_gradient, gain)]
    kv, *rest = pl.pallas_call(
        functools.partial(keys_kernel, pieces),
        out_shape=(jax.ShapeDtypeStruct((*sizes, rows, cols), x.dtype), *swapped),
        in_specs=[ANY] * 4,
        out_specs=(ANY,) * 4,
        scratch_shapes=semaphores(n) + [pltpu.SemaphoreType.DMA((4,))] * 3,
        compiler_params=pltpu.CompilerParams(
            collective_id=collective_id, has_side_effects=True, vmem_limit_bytes=1 << 20
        ),
        name="gather_keys",
    )(x, q, normed_gradient, gain)
    return kv.reshape(32, rows, cols), *rest


ORDERS = {
    PLAIN: ("xzy", "zyx", "yxz", "zxy", "yzx", "xyz"),
    PAIRED: ("hzy", "zyh", "yhz", "zhy", "yzh", "hyz"),
}


def cut(rows, cols, orders):
    by_rows = rows // 16 >= 2 * len(orders) or cols == 128
    step = 16 if by_rows else 128
    units = (rows if by_rows else cols) // step
    base, extra = divmod(units, len(orders))
    pieces, at = [], 0
    for i, order in enumerate(orders):
        size = (base + (1 if i < extra else 0)) * step
        if size:
            part = (pl.ds(at, size), pl.ds(0, cols)) if by_rows else (pl.ds(0, rows), pl.ds(at, size))
            pieces.append((part, order))
        at += size
    return pieces


class Scatter:
    def __init__(self, here, axes, pieces, x_ref, o_ref, send, recv, bufs):
        self.here, self.axes, self.pieces, self.x, self.o = here, axes, pieces, x_ref, o_ref
        self.send, self.recv, self.depth = send, recv, len(axes)
        n, depth = len(pieces), len(axes)
        self.inbox = [bufs[depth * i : depth * (i + 1)] for i in range(n)]
        self.partial = [bufs[depth * n + (depth - 1) * i :][: depth - 1] for i in range(n)]
        self.copies, self.latest = [], {}

    def block(self, phase, i, coord):
        part, order = self.pieces[i]
        left = [a for a in self.axes if a not in order[:phase]]
        ref = self.partial[i][phase - 1] if phase else self.x
        tail = () if phase else part
        return ref.at[tuple(coord if a == order[phase] else slice(None) for a in left) + tail]

    def launch(self, phase, i):
        axis = self.pieces[i][1][phase]
        self.latest[i] = []
        for d in range(1, SIZES[axis]):
            at = (i * self.depth + phase) * 3 + d - 1
            self.latest[i].append(
                remote(
                    self.block(phase, i, lax.rem(self.here[axis] + d, SIZES[axis])),
                    self.inbox[i][phase].at[d - 1],
                    self.send.at[at],
                    self.recv.at[at],
                    device_at(self.axes, moved(self.here, axis, d)),
                )
            )
        self.copies.extend(self.latest[i])

    def total(self, phase, i):
        part, order = self.pieces[i]
        axis = order[phase]
        for copy in self.latest[i]:
            copy.wait_recv()
        mine, inbox = self.block(phase, i, self.here[axis]), self.inbox[i][phase]
        left = [SIZES[a] for a in self.axes if a not in order[: phase + 1]]
        count = 1
        for extent in left:
            count *= extent

        def add(k, carry):
            at = ()
            for extent in reversed(left):
                at, k = (k % extent,) + at, k // extent
            whole = mine[at].astype(jnp.float32) if at else mine[...].astype(jnp.float32)
            for d in range(SIZES[axis] - 1):
                whole = whole + inbox[(d,) + at].astype(jnp.float32)
            if phase == self.depth - 1:
                self.o[part] = whole.astype(self.o.dtype)
            else:
                self.partial[i][phase][at] = whole.astype(jnp.bfloat16)
            return carry

        if count == 1:
            add(0, 0)
        else:
            lax.fori_loop(0, count, add, 0)

    def run(self):
        for i in range(len(self.pieces)):
            self.launch(0, i)
        for phase in range(self.depth):
            for i in range(len(self.pieces)):
                self.total(phase, i)
                if phase < self.depth - 1:
                    self.launch(phase + 1, i)
        for copy in self.copies:
            copy.wait_send()


def scatter_plan(rows, cols, axes):
    first = "c" if axes == PAIRED else ""
    pieces = cut(rows, cols, [first + order[::-1] for order in ORDERS[axes]])
    depth = len(axes)
    n = 3 * depth * len(pieces)
    inboxes, partials = [], []
    for part, order in pieces:
        size = tuple(edge.size for edge in part)
        for phase in range(depth):
            left = [SIZES[a] for a in axes if a not in order[: phase + 1]]
            inboxes.append(pltpu.VMEM((SIZES[order[phase]] - 1, *left, *size), jnp.bfloat16))
            if phase < depth - 1:
                partials.append(pltpu.VMEM((*left, *size), jnp.bfloat16))
    sems = [pltpu.SemaphoreType.DMA((n,)), pltpu.SemaphoreType.DMA((n,))]
    return pieces, sems, inboxes + partials


def split_axes(x, axes):
    return x.reshape(*[SIZES[a] for a in axes], *x.shape[1:])


def values_kernel(
    pieces, x_ref, dq_ref, o_ref, dq_out, send, recv, swap_send, swap_recv, swap_local, own, *bufs
):
    here = coords(PAIRED)
    greet(axis_peers(PAIRED, here), here)
    first = Swap(here, dq_ref, dq_out, swap_send.at[0], swap_recv.at[0], swap_local.at[0])
    second = Swap(here, own, o_ref, swap_send.at[1], swap_recv.at[1], swap_local.at[1])
    first.start()
    Scatter(here, PAIRED, pieces, x_ref, own, send, recv, bufs).run()
    second.start()
    first.wait()
    second.wait()


def scatter_values(x, d_queries, collective_id):
    _, rows, cols = x.shape
    pieces, sems, bufs = scatter_plan(rows, cols, PAIRED)
    return pl.pallas_call(
        functools.partial(values_kernel, pieces),
        out_shape=(
            jax.ShapeDtypeStruct((rows, cols), jnp.bfloat16),
            jax.ShapeDtypeStruct(d_queries.shape, d_queries.dtype),
        ),
        in_specs=[VMEM, ANY],
        out_specs=(ANY, ANY),
        scratch_shapes=sems
        + [pltpu.SemaphoreType.DMA((2,))] * 3
        + [pltpu.VMEM((rows, cols), jnp.bfloat16)]
        + bufs,
        compiler_params=pltpu.CompilerParams(
            collective_id=collective_id, has_side_effects=True, vmem_limit_bytes=40 << 20
        ),
        name="scatter_values",
    )(split_axes(x, PAIRED), d_queries)


def final_kernel(
    pieces, up_pieces, spread, x_ref, up_ref, o_ref, all_ref,
    send, recv, up_send, up_recv, g_send, g_recv, g_fore, g_back, local, own, *bufs,
):
    here = coords(PLAIN)
    greet(axis_peers(PLAIN, here))
    cut_at = 5 * len(up_pieces)
    up = Scatter(here, PLAIN, up_pieces, up_ref, own, up_send, up_recv, bufs[:cut_at])
    down = Scatter(here, PLAIN, pieces, x_ref, o_ref, send, recv, bufs[cut_at:])
    gather = Gather(here, PLAIN, spread, own, all_ref, (g_send, g_recv, g_fore, g_back), 0)

    def stage(scatter, phase):
        for i in range(len(scatter.pieces)):
            if phase:
                scatter.total(phase - 1, i)
            if phase < 3:
                scatter.launch(phase, i)

    def spread_on(phase):
        for i in range(len(spread)):
            if phase:
                gather.arrived(phase - 1, i)
            gather.launch(phase, i)

    stage(up, 0)
    stage(down, 0)
    stage(up, 1)
    stage(up, 2)
    stage(down, 1)
    stage(up, 3)
    copy = pltpu.make_async_copy(own, all_ref.at[gather.place], local)
    copy.start()
    spread_on(0)
    stage(down, 2)
    copy.wait()
    spread_on(1)
    spread_on(2)
    stage(down, 3)
    gather.finish()
    for one in up.copies + down.copies:
        one.wait_send()


def scatter_final(x, up, collective_id):
    _, rows, cols = x.shape
    up_rows = up.shape[1]
    pieces, sems, bufs = scatter_plan(rows, cols, PLAIN)
    up_pieces, up_sems, up_bufs = scatter_plan(up_rows, cols, PLAIN)
    spread = cut(up_rows, cols, ORDERS[PLAIN])
    out, ups = pl.pallas_call(
        functools.partial(final_kernel, pieces, up_pieces, spread),
        out_shape=(
            jax.ShapeDtypeStruct((rows, cols), jnp.float32),
            jax.ShapeDtypeStruct((2, 4, 4, up_rows, cols), jnp.float32),
        ),
        in_specs=[VMEM, VMEM],
        out_specs=(VMEM, VMEM),
        scratch_shapes=sems
        + up_sems
        + semaphores(9 * len(spread) + 1)
        + [pltpu.SemaphoreType.DMA, pltpu.VMEM((up_rows, cols), jnp.float32)]
        + up_bufs
        + bufs,
        compiler_params=pltpu.CompilerParams(
            collective_id=collective_id, has_side_effects=True, vmem_limit_bytes=40 << 20
        ),
        name="scatter_final",
    )(split_axes(x, PLAIN), split_axes(up, PLAIN))
    return out, ups.reshape(32, up_rows, cols)


def middle_kernel(
    pieces, scatter_pieces, total_slots, x_ref, wo_ref, ng_ref, gain_ref, o_ref, normed_out,
    everyone, part, inbox, hidden, grads, d_part, normed, stat, near_in, far_in,
    send, recv, fore, back, local, h_send, h_recv, s_send, s_recv, g_send, g_recv,
    swap_send, swap_recv, swap_local, r_send, r_recv, *bufs,
):
    f32, bf16 = jnp.float32, jnp.bfloat16
    here = coords(PAIRED)
    me, member = group_place("paired section", here)
    others = [lax.rem(me + d, 4) for d in range(1, 4)]
    near = [{**here, "h": lax.rem(here["h"] + a, 2), "c": lax.rem(here["c"] + b, 2)} for a, b in ((0, 1), (1, 0), (1, 1))]
    far = [
        {**here, "y": lax.rem(here["y"] + a, 2), "z": lax.rem(here["z"] + b, 4)}
        for a in range(2)
        for b in range(4)
        if a or b
    ]
    devices = [member(k) for k in others] + [device_at(PAIRED, place) for place in near + far]
    greet(devices, here)

    gather = Gather(here, PAIRED, pieces, x_ref, everyone, (send, recv, fore, back), 0)
    own = pltpu.make_async_copy(x_ref, everyone.at[gather.place], local)
    own.start()
    run_gathers([gather], [own], lambda phase: None)

    def slab(ref, k):
        return ref.at[k // 2, pl.ds(2 * (k % 2), 2)]

    copies = []
    for d in (2, 1, 3, 0):
        k = lax.rem(me + d, 4)
        rows = slab(everyone, k)[...].reshape(ROWS, x_ref.shape[1])
        part[k] = jnp.dot(rows, wo_ref[...], preferred_element_type=f32).astype(bf16)
        if d:
            copies.append(
                remote(part.at[k], inbox.at[d - 1], h_send.at[d - 1], h_recv.at[d - 1], member(k))
            )
    scaled = (total_slots ** (-0.5)) * ng_ref[...].astype(f32) * gain_ref[...]
    for copy in copies:
        copy.wait()
    summed = part[me].astype(f32)
    for d in range(3):
        summed = summed + inbox[d].astype(f32)
    hidden[...] = summed

    ones = jnp.ones((8, summed.shape[1]), f32)
    row_sums = lambda v: lax.dot_general(
        ones, v, (((1,), (1,)), ((), ())), preferred_element_type=f32, precision=lax.Precision.HIGHEST
    )
    first = lax.broadcasted_iota(jnp.int32, (8, ROWS), 0) == 0
    total = jnp.where(first, row_sums(summed * summed), row_sums(scaled * summed))
    stat[0] = total
    at = 0
    for step, (places, box) in enumerate(((near, near_in), (far, far_in))):
        copies = [
            remote(stat.at[step], box.at[k], s_send.at[at + k], s_recv.at[at + k], device_at(PAIRED, place))
            for k, place in enumerate(places)
        ]
        at += len(places)
        for copy in copies:
            copy.wait()
        for k in range(len(places)):
            total = total + box[k]
        if step == 0:
            stat[1] = total
    inv = lax.rsqrt(total[0:1, :] / MODEL_DIM + epsilon)
    pull = inv * inv * inv * total[1:2, :] / MODEL_DIM
    across = lambda v: jnp.transpose(v + jnp.zeros((HD, ROWS), f32))
    inv, pull = across(inv), across(pull)
    for j in range(summed.shape[1] // HD):
        cols = slice(j * HD, (j + 1) * HD)
        value = hidden[:, cols]
        normed[:, cols] = (value * inv * gain_ref[:, cols]).astype(bf16)
        weighted = (total_slots ** (-0.5)) * ng_ref[:, cols].astype(f32) * gain_ref[:, cols]
        grads[me, :, cols] = (inv * weighted - value * pull).astype(bf16)
    copies = [
        remote(grads.at[me], grads.at[me], g_send.at[d], g_recv.at[d], member(k))
        for d, k in enumerate(others)
    ]
    swap = Swap(here, normed, normed_out, swap_send, swap_recv, swap_local)
    swap.start()

    def back_through(k):
        rows = contract(grads[k], wo_ref[...], 1, 1).astype(bf16)
        slab(d_part, k)[...] = rows.reshape(2, 2, 2, x_ref.shape[0], x_ref.shape[1])

    back_through(me)
    for d in range(3):
        copies[2 - d].wait_recv()
        back_through(lax.rem(me + 4 - (3 - d), 4))
    for copy in copies:
        copy.wait_send()
    Scatter(here, PAIRED, scatter_pieces, d_part, o_ref, r_send, r_recv, bufs).run()
    swap.wait()


def middle(x, output_weight, normed_gradient, gain, total_slots, collective_id):
    bf16, f32 = jnp.bfloat16, jnp.float32
    rows, cols = x.shape
    width = output_weight.shape[1]
    pieces = cut(rows, cols, ORDERS[PAIRED])
    scatter_pieces, sems, bufs = scatter_plan(rows, cols, PAIRED)
    sizes = [SIZES[a] for a in PAIRED]
    dma = pltpu.SemaphoreType.DMA
    return pl.pallas_call(
        functools.partial(middle_kernel, pieces, scatter_pieces, total_slots),
        out_shape=(
            jax.ShapeDtypeStruct(x.shape, bf16),
            jax.ShapeDtypeStruct(normed_gradient.shape, bf16),
        ),
        in_specs=[VMEM] * 4,
        out_specs=(VMEM, ANY),
        scratch_shapes=[
            pltpu.VMEM((*sizes, rows, cols), bf16),
            pltpu.VMEM((4, ROWS, width), bf16),
            pltpu.VMEM((3, ROWS, width), bf16),
            pltpu.VMEM((ROWS, width), f32),
            pltpu.VMEM((4, ROWS, width), bf16),
            pltpu.VMEM((*sizes, rows, cols), bf16),
            pltpu.VMEM((ROWS, width), bf16),
            pltpu.VMEM((2, 8, ROWS), f32),
            pltpu.VMEM((3, 8, ROWS), f32),
            pltpu.VMEM((7, 8, ROWS), f32),
            *semaphores(9 * len(pieces) + 1),
            dma,
            dma((3,)),
            dma((3,)),
            dma((10,)),
            dma((10,)),
            dma((3,)),
            dma((3,)),
            dma,
            dma,
            dma,
            *sems,
            *bufs,
        ],
        compiler_params=pltpu.CompilerParams(
            collective_id=collective_id, has_side_effects=True, vmem_limit_bytes=32 << 20
        ),
        name="middle",
    )(x, output_weight, normed_gradient, gain)


def group_place(group, here):
    if group == "section":
        return here["m"] * 2 + here["c"], lambda k: device_at("x", {**here, "m": k // 2, "c": k % 2})
    return here["m"] * 2 + here["l"], lambda k: device_at("h", {**here, "m": k // 2, "l": k % 2})

def exchange_kernel(group, count, apart, x_ref, o_ref, send, recv, local):
    me, device = group_place(group, coords(PLAIN))
    others = [lax.rem(me + d, count) for d in range(1, count)]
    greet([device(k) for k in others])
    own = pltpu.make_async_copy(x_ref.at[me] if apart else x_ref, o_ref.at[me], local)
    own.start()
    copies = [
        remote(x_ref.at[k] if apart else x_ref, o_ref.at[me], send.at[d], recv.at[d], device(k))
        for d, k in enumerate(others)
    ]
    own.wait()
    for copy in copies:
        copy.wait()


def exchange(x, group, apart, collective_id, name):
    count = 4
    shape = x.shape[1:] if apart else x.shape
    return pl.pallas_call(
        functools.partial(exchange_kernel, group, count, apart),
        out_shape=jax.ShapeDtypeStruct((count, *shape), x.dtype),
        in_specs=[ANY],
        out_specs=ANY,
        scratch_shapes=[
            pltpu.SemaphoreType.DMA((count - 1,)),
            pltpu.SemaphoreType.DMA((count - 1,)),
            pltpu.SemaphoreType.DMA,
        ],
        compiler_params=pltpu.CompilerParams(
            collective_id=collective_id, has_side_effects=True, vmem_limit_bytes=1 << 20
        ),
        name=name,
    )(x)


def contract(left, right, l, r):
    return lax.dot_general(
        left, right, (((l,), (r,)), ((), ())), preferred_element_type=jnp.float32
    )


def head_rows(ref):
    return jnp.concatenate([ref[:, h * HD : (h + 1) * HD] for h in range(HEADS_HERE)], axis=0)


def key_block(kv_ref, g, cols, context_rows, slots):
    context = kv_ref[pl.ds(g * GROUP, GROUP), :context_rows, cols]
    context = context.reshape(GROUP * context_rows, HD)
    if not slots:
        return context
    memory = kv_ref[pl.ds(g * GROUP, GROUP), context_rows:, cols]
    return jnp.concatenate([context, memory.reshape(GROUP * slots, HD)], axis=0)


def key_docs(g, bounds_ref, context_rows, slots):
    edge = GROUP * context_rows
    token = g * edge + lax.broadcasted_iota(jnp.int32, (edge, HD), 0)
    docs = (token >= 4 * bounds_ref[0:1, :]) & (token < 4 * bounds_ref[1:2, :])
    if slots:
        slot = g * (GROUP * slots) + lax.broadcasted_iota(jnp.int32, (GROUP * slots, HD), 0)
        docs = jnp.concatenate(
            [
                docs.astype(jnp.float32),
                ((slot >= bounds_ref[0:1, :]) & (slot < bounds_ref[1:2, :])).astype(jnp.float32),
            ],
            axis=0,
        )
    return docs.astype(jnp.float32).astype(jnp.bfloat16)


def with_fill(q, rows_ref, bounds_ref):
    low = jnp.transpose(rows_ref[2:3, :].astype(jnp.float32) + jnp.zeros((HD, ROWS), jnp.float32))
    mine = low == bounds_ref[0:1, :].astype(jnp.float32)
    return jnp.concatenate([q, jnp.where(mine, 0.0, mask_fill).astype(jnp.bfloat16)], axis=1)


def group_scores(keys, g, q_wide, rows_ref, bounds_ref, context_rows, slots, causal):
    docs = key_docs(g, bounds_ref, context_rows, slots)
    scores = contract(jnp.concatenate([keys, docs], axis=1), q_wide, 1, 1)
    if not causal:
        return scores
    edge = GROUP * context_rows
    slot = g * (GROUP * slots) + lax.broadcasted_iota(jnp.int32, (GROUP * slots, ROWS), 0)
    return jnp.concatenate(
        [scores[:edge], jnp.where(slot <= rows_ref[3:4, :], scores[edge:], mask_fill)], axis=0
    )


def over_groups(span, step):
    first, own, last = span[0], span[1], span[2]

    def before(g, carry):
        step(g, False, True)
        return carry

    def after(g, carry):
        step(g, False, False)
        return carry

    step(own, True, True)
    lax.fori_loop(first, own, before, 0)
    lax.fori_loop(own + 1, last, after, 0)


def attend_kernel(
    context_rows, span, rows_ref, bounds_ref, q_ref, kv_ref, o_ref, ot_ref, top_ref, mass_ref
):
    slots = kv_ref.shape[1] - context_rows
    q = with_fill(head_rows(q_ref), rows_ref, bounds_ref)
    ot_ref[...] = jnp.zeros_like(ot_ref)
    top_ref[...] = jnp.full_like(top_ref, mask_fill)
    mass_ref[...] = jnp.zeros_like(mass_ref)

    def step(g, masked, with_memory):
        extra = slots if with_memory else 0
        keys = key_block(kv_ref, g, slice(0, HD), context_rows, extra)
        scores = group_scores(keys, g, q, rows_ref, bounds_ref, context_rows, extra, masked)
        before = top_ref[0:1, :]
        top = jnp.maximum(before, jnp.max(scores, axis=0, keepdims=True))
        keep = jnp.exp2((before - top) * exp2_scale)
        weight = jnp.exp2((scores - top) * exp2_scale)
        top_ref[0:1, :] = top
        mass_ref[0:1, :] = mass_ref[0:1, :] * keep + jnp.sum(weight, axis=0, keepdims=True)
        values = key_block(kv_ref, g, slice(HD, 2 * HD), context_rows, extra)
        ot_ref[...] = ot_ref[...] * keep + contract(values, weight.astype(jnp.bfloat16), 0, 0)

    over_groups(span, step)
    ot_ref[...] = ot_ref[...] / mass_ref[0:1, :]
    rows = jnp.transpose(ot_ref[...]).astype(jnp.bfloat16)
    here = q_ref.shape[0]
    for h in range(HEADS_HERE):
        o_ref[:, h * HD : (h + 1) * HD] = rows[h * here : (h + 1) * here]


def backward_kernel(
    context_rows, span, rows_ref, bounds_ref, q_ref, g_ref, kv_ref, ot_ref, top_ref, mass_ref,
    dq_ref, dv_ref, acc,
):
    slots = kv_ref.shape[1] - context_rows
    edge = GROUP * context_rows
    q = with_fill(head_rows(q_ref), rows_ref, bounds_ref)
    grad = head_rows(g_ref)
    center = jnp.sum(jnp.transpose(grad.astype(jnp.float32)) * ot_ref[...], axis=0, keepdims=True)
    top = top_ref[0:1, :]
    share = 1.0 / mass_ref[0:1, :]
    acc[...] = jnp.zeros_like(acc)
    dv_ref[...] = jnp.zeros_like(dv_ref)

    def step(g, masked, with_memory):
        extra = slots if with_memory else 0
        keys = key_block(kv_ref, g, slice(0, HD), context_rows, extra)
        scores = group_scores(keys, g, q, rows_ref, bounds_ref, context_rows, extra, masked)
        probs = jnp.exp2((scores - top) * exp2_scale) * share
        values = key_block(kv_ref, g, slice(HD, 2 * HD), context_rows, extra)
        d_probs = contract(values, grad, 1, 1)
        d_scores = (probs * (d_probs - center)).astype(jnp.bfloat16)
        d_values = contract(probs.astype(jnp.bfloat16), grad, 1, 0).astype(jnp.bfloat16)
        dv_ref[pl.ds(g * GROUP, GROUP), :context_rows, :] = d_values[:edge].reshape(
            GROUP, context_rows, HD
        )
        if with_memory:
            dv_ref[pl.ds(g * GROUP, GROUP), context_rows:, :] = d_values[edge:].reshape(
                GROUP, slots, HD
            )
        acc[...] += contract(keys, d_scores, 0, 0)

    over_groups(span, step)
    rows = jnp.transpose(acc[...] * score_scale).astype(jnp.bfloat16)
    here = q_ref.shape[0]
    for h in range(HEADS_HERE):
        dq_ref[:, h * HD : (h + 1) * HD] = rows[h * here : (h + 1) * here]


SMEM = pl.BlockSpec(memory_space=pltpu.SMEM)
BIG = pltpu.CompilerParams(vmem_limit_bytes=48 << 20)


def attend(span, rows, bounds, q, kv, context_rows):
    f32 = jnp.float32
    return pl.pallas_call(
        functools.partial(attend_kernel, context_rows),
        out_shape=(
            jax.ShapeDtypeStruct(q.shape, jnp.bfloat16),
            jax.ShapeDtypeStruct((HD, ROWS), f32),
            jax.ShapeDtypeStruct((8, ROWS), f32),
            jax.ShapeDtypeStruct((8, ROWS), f32),
        ),
        in_specs=[SMEM] + [VMEM] * 4,
        out_specs=(VMEM, VMEM, VMEM, VMEM),
        compiler_params=BIG,
        name="attend",
    )(span, rows, bounds, q, kv)


def attend_backward(span, rows, bounds, q, grad, kv, ot, top, mass, context_rows):
    return pl.pallas_call(
        functools.partial(backward_kernel, context_rows),
        out_shape=(
            jax.ShapeDtypeStruct(q.shape, jnp.bfloat16),
            jax.ShapeDtypeStruct((*kv.shape[:2], HD), jnp.bfloat16),
        ),
        in_specs=[SMEM] + [VMEM] * 8,
        out_specs=(VMEM, VMEM),
        scratch_shapes=[pltpu.VMEM((HD, ROWS), jnp.float32)],
        compiler_params=BIG,
        name="attend_backward",
    )(span, rows, bounds, q, grad, kv, ot, top, mass)


def row_bounds(document_slots, first, slot_dev, seq_size):
    docs = document_slots.shape[0]
    order = jnp.arange(docs, dtype=jnp.int32)
    ends = jnp.sum(jnp.where(order[None, :] <= order[:, None], document_slots[None, :], 0), axis=1)
    slot = first + jnp.arange(slot_dev, dtype=jnp.int32)
    passed = ends[None, :] <= slot[:, None]
    low = jnp.max(jnp.where(passed, ends[None, :], 0), axis=1)
    high = jnp.min(jnp.where(passed, slot_dev * seq_size, ends[None, :]), axis=1)
    one = jnp.stack([4 * low, 4 * high, low, slot] + [slot] * 4).astype(jnp.int32)
    unit = GROUP * slot_dev
    start, stop = jnp.min(low) // unit, (jnp.max(high) + unit - 1) // unit
    span = jnp.stack([start, first // unit, stop])
    starts = ends - document_slots
    bounds = jnp.stack([starts, ends] + [ends] * 6)
    bounds = jnp.pad(bounds, ((0, 0), (0, HD - docs)))
    return span.astype(jnp.int32), jnp.tile(one, (1, HEADS_HERE)), bounds.astype(jnp.int32)


def body(
    context,
    memory,
    query_weight,
    key_weight,
    value_weight,
    query_down_map,
    query_up_map,
    value_down_map,
    value_up_map,
    output_weight,
    decoder_gain,
    document_slots,
    normed_gradient,
):
    bf16, f32 = jnp.bfloat16, jnp.float32
    tok_dev = context.shape[0]
    slot_dev = memory.shape[0]
    seq_size = lax.axis_size("seq")
    here = coords(PLAIN)
    paired_index = here["y"] * 16 + here["z"] * 4 + here["h"] * 2 + here["c"]
    section_extent = lax.axis_size("section")
    section_index = lax.axis_index("section")
    kv_weight, down, query_sum, output_weight = opening(
        jnp.concatenate([key_weight, value_weight], axis=1),
        value_down_map,
        memory,
        query_weight,
        output_weight,
        1,
    )
    query_low = jnp.dot(memory, query_down_map, preferred_element_type=f32).astype(bf16)
    row_parts = (context, memory)
    value_low = jnp.concatenate(
        [jnp.dot(part, down, preferred_element_type=f32).astype(bf16) for part in row_parts], axis=0
    )
    projected = jnp.concatenate(
        [jnp.dot(part, kv_weight, preferred_element_type=f32) for part in row_parts], axis=0
    )
    queries = (
        query_sum + adapter_scale * jnp.dot(query_low, query_up_map, preferred_element_type=f32)
    ).astype(bf16)
    keys = projected[:, :HD].astype(bf16)
    values = (
        projected[:, HD : 2 * HD]
        + adapter_scale * jnp.dot(value_low, value_up_map, preferred_element_type=f32)
    ).astype(bf16)
    kv, queries_here, normed_gradient, decoder_gain = gather_keys(
        jnp.concatenate([keys, values], axis=1),
        queries,
        normed_gradient,
        decoder_gain.reshape(-1, 128),
        2,
    )
    decoder_gain = decoder_gain.reshape(1, -1)
    span, rows, bounds = row_bounds(document_slots, paired_index * slot_dev, slot_dev, seq_size)
    attended, ot, top, mass = attend(span, rows, bounds, queries_here, kv, tok_dev)
    total_slots = slot_dev * seq_size
    d_attended, normed = middle(
        attended, output_weight, normed_gradient, decoder_gain, total_slots, 3
    )
    d_queries, dv_part = attend_backward(
        span, rows, bounds, queries_here, d_attended, kv, ot, top, mass, tok_dev
    )
    d_values, d_queries = scatter_values(dv_part, d_queries, 8)
    query_up_part = adapter_scale * contract(query_low, d_queries, 0, 0)
    value_up_part = adapter_scale * contract(value_low, d_values, 0, 0)
    query_part = adapter_scale * contract(d_queries, query_up_map, 1, 1)
    value_part = adapter_scale * contract(d_values, value_up_map, 1, 1)
    backs = jnp.sum(
        exchange(
            jnp.concatenate([query_part, value_part], axis=0).astype(bf16),
            "section", False, 9, "sum_backs",
        ).astype(f32),
        axis=0,
    ).astype(bf16)
    width = memory.shape[1] // section_extent
    memory_cols = lax.dynamic_slice_in_dim(memory, section_index * width, width, 1)
    context_cols = lax.dynamic_slice_in_dim(context, section_index * width, width, 1)
    memory_backs = jnp.concatenate([backs[:slot_dev], backs[slot_dev + tok_dev :]], axis=1)
    memory_down = contract(memory_cols, memory_backs, 0, 0)
    down_parts = [
        memory_down[:, :HD],
        memory_down[:, HD:] + contract(context_cols, backs[slot_dev : slot_dev + tok_dev], 0, 0),
    ]
    ups = jnp.concatenate([query_up_part, value_up_part], axis=1)
    lanes = ups.shape[1] // 128
    ups = jnp.moveaxis(ups.reshape(128, lanes, 128), 1, 0).reshape(seq_size, -1, 128)
    up_rows = ups.shape[1]
    down_rows = MODEL_DIM // section_extent // seq_size
    final, ups = scatter_final(
        jnp.concatenate([part.reshape(seq_size, -1, 128).astype(bf16) for part in down_parts], axis=1),
        jnp.pad(ups.astype(bf16), ((0, 0), (0, -up_rows % 16), (0, 0))),
        10,
    )
    grad_qa, grad_va = final[:down_rows], final[down_rows:]
    ups = ups[:, :up_rows]
    ups = jnp.moveaxis(ups.reshape(lanes, 128, 128), 0, 1).reshape(128, lanes * 128)
    split = query_up_part.shape[1]
    return (normed, grad_qa, grad_va, ups[:, :split], ups[:, split:])


def solution(mesh):
    in_specs = (
        P("seq", None),
        P("seq", None),
        P(None, "section"),
        P("seq", "section"),
        P("seq", "section"),
        P(),
        P(None, "section"),
        P("seq", None),
        P(None, "section"),
        P("section", "seq"),
        P("seq"),
        P(),
        P("section", "seq"),
    )
    out_specs = (
        P("section", "seq"),
        P(("section", "seq"), None),
        P(("section", "seq"), None),
        P(None, "section"),
        P(None, "section"),
    )
    return jax.shard_map(body, mesh=mesh, in_specs=in_specs, out_specs=out_specs, check_vma=False)
```

time: 304 us -> 298 us (0.980)
  Pallas kernels: 275 us -> 242 us
  local copies, waits for them, and re-layouts: 9 us -> 27.6 us
  matrix products: 12.3 us -> 17.5 us
    pallas_call x2 -> x1, Pallas kernels: 28 us -> 8.15 us  [exchange(): pl.pallas_call(functools.partial(exchange_kernel, group, count, apart), o...]
    unnamed x32 -> x81, local copies, waits for them, and re-layouts: 5.44 us -> 15.8 us
    dot_general x3 -> x4, matrix products: 6.12 us -> 13.6 us  [the longest x2 8.1 us: body(): jnp.dot(part, kv_weight, preferred_element_type=f32)]
    pallas_call x1, Pallas kernels: 11.2 us -> 4.61 us  [attend_backward(): pl.pallas_call(functools.partial(backward_kernel, context_rows), out_shap...]
    pallas_call x1, Pallas kernels: 8.82 us -> 2.43 us  [attend(): pl.pallas_call(functools.partial(attend_kernel, context_rows), out_shape=...]
    pallas_call x1, Pallas kernels: 21.7 us -> 26.4 us  [scatter_values(): pl.pallas_call(functools.partial(values_kernel, pieces), out_shape=(jax.S...]
    pallas_call x1, Pallas kernels: 49.4 us -> 45.3 us  [opening(): pl.pallas_call(functools.partial(opening_kernel, pieces, half_pieces), ou...]
    convert_element_type x2, local copies, waits for them, and re-layouts: 0.28 us -> 3.58 us  [body(): ups.astype(bf16)]
where the time goes in v3:
time: 298 us
  Pallas kernels  242 us (81%)
  local copies, waits for them, and re-layouts  27.6 us (9%)
  matrix products  17.5 us (6%)
  other arithmetic  5.97 us (2%)
  between operations  4.48 us (2%)
    pallas_call x1, Pallas kernels, middle(): pl.pallas_call(functools.partial(middle_kernel, pieces, scatter_pieces, t...  95 us
    pallas_call x1, Pallas kernels, opening(): pl.pallas_call(functools.partial(opening_kernel, pieces, half_pieces), ou...  45.3 us
    pallas_call x1, Pallas kernels, scatter_final(): pl.pallas_call(functools.partial(final_kernel, pieces, up_pieces, spread)...  30.7 us
    pallas_call x1, Pallas kernels, gather_keys(): pl.pallas_call(functools.partial(keys_kernel, pieces), out_shape=(jax.Sha...  29.4 us
    pallas_call x1, Pallas kernels, scatter_values(): pl.pallas_call(functools.partial(values_kernel, pieces), out_shape=(jax.S...  26.4 us
    unnamed x81, local copies, waits for them, and re-layouts  15.8 us
    pallas_call x1, Pallas kernels, exchange(): pl.pallas_call(functools.partial(exchange_kernel, group, count, apart), o...  8.15 us
    dot_general x2, matrix products, body(): jnp.dot(part, kv_weight, preferred_element_type=f32)  8.1 us

profile of v3, /device:TPU:0, one launch (start us, length us, event | category | flops | bytes accessed | tf_op | source)
XLA Modules:
  0.0 297.7 jit_solution(2191601183505585457)
XLA Ops:
  0.7 0.9 select_reduce_fusion
  8.3 0.9 pad_maximum_fusion.4.kv_ref
  9.2 1.2 copy-done.2
  10.4 1.0 copy-done.5
  11.5 0.8 copy-done.17
  12.3 45.3 %opening.1 = (bf16[2,4,4,256,256]{4,3,2,1,0:T(8,128)(2,1)}, bf16[2,4,4,2,128,128]{5,4,3,2,1,0:T(8,128)(2,1)S(1)}, f32[64,1024]{1,0:T(8,128)S(1)}, bf16[1024,256]{1,0:T(8,128)(2,1)S(1)}) custom-call(bf16[256,256]{1,0:T(8,128)(2,1)S(1)} %pad_maximum_fusion.4.kv_ref, bf16[256,128]{1,0:T(8,128)(2,1)S(1)} %copy-done.17, bf16[64,8192]{1,0:T(8,128)(2,1)S(1)} %copy-done.2, ...), custom_call_target="tpu_custom_call" | custom-call | tf_op jit(solution)/shard_map/opening/pallas_call | solution.py:258
  57.6 4.0 %convolution_bitcast_fusion.1 = f32[64,256]{1,0:T(8,128)S(1)} fusion(bf16[64,8192]{1,0:T(8,128)(2,1)S(1)} %copy-done.2, bf16[8192,256]{1,0:T(8,128)(2,1)} %bitcast.62), kind=kOutput, calls=%fused_computation.14 | convolution fusion | flops 268435456 | bytes 5308416 | tf_op jit(solution)/shard_map/dot_general | solution.py:970
  62.0 4.1 %convolution_bitcast_fusion = f32[256,256]{1,0:T(8,128)} fusion(bf16[256,8192]{1,0:T(8,128)(2,1)S(1)} %copy-done.27, bf16[8192,256]{1,0:T(8,128)(2,1)} %bitcast.63), kind=kOutput, calls=%fused_computation.6 | convolution fusion | flops 1073741824 | bytes 8650752 | tf_op jit(solution)/shard_map/dot_general | solution.py:970
  66.1 1.1 fusion.10
  67.2 0.9 copy.36
  68.2 4.4 %fusion.7 = bf16[256,128]{0,1:T(8,128)(2,1)S(1)} fusion(bf16[8192,128]{1,0:T(8,128)(2,1)} %bitcast.56, bf16[256,8192]{1,0:T(8,128)(2,1)} %param.13), kind=kOutput, calls=%fused_computation.16 | convolution fusion | flops 536903680 | bytes 6356992 | tf_op jit(solution)/shard_map/dot_general | solution.py:967
  74.7 29.4 %gather_keys.1 = (bf16[2,4,2,2,320,256]{5,4,3,2,1,0:T(8,128)(2,1)S(1)}, bf16[64,1024]{1,0:T(8,128)(2,1)S(1)}, bf16[512,256]{1,0:T(8,128)(2,1)S(1)}, f32[2,128]{1,0:T(2,128)S(1)}) custom-call(bf16[320,256]{1,0:T(8,128)(2,1)S(1)} %pad_maximum_fusion.3.x_ref, bf16[64,1024]{1,0:T(8,128)(2,1)S(1)} %fusion.3.q_ref, bf16[512,256]{1,0:T(8,128)(2,1)S(1)} %copy-done.10, ...), custom_call_target="tpu_custom_call" | custom-call | tf_op jit(solution)/shard_map/gather_keys/pallas_call | solution.py:321
  104.2 2.4 attend.1
  106.6 2.3 copy-done.1
  110.2 95.0 %middle.1 = (bf16[64,1024]{1,0:T(8,128)(2,1)S(1)}, bf16[512,256]{1,0:T(8,128)(2,1)S(1)}) custom-call(bf16[64,1024]{1,0:T(8,128)(2,1)S(1)} %get-tuple-element.30.x_ref, bf16[1024,256]{1,0:T(8,128)(2,1)S(1)} %copy-done.9, bf16[512,256]{1,0:T(8,128)(2,1)S(1)} %get-tuple-element.32.ng_ref, f32[1,256]{1,0:T(1,128)S(1)} %bitcast.61), custom_call_target="tpu_custom_call" | custom-call | tf_op jit(solution)/shard_map/middle/pallas_call | solution.py:661
  206.5 0.9 copy-done.14
  208.8 0.7 copy-done.23
  210.2 4.6 %attend_backward.1 = (bf16[64,1024]{1,0:T(8,128)(2,1)S(1)}, bf16[32,320,128]{2,1,0:T(8,128)(2,1)S(1)}) custom-call(s32[3]{0:T(128)S(1)} %copy-done.25, s32[8,512]{1,0:T(8,128)S(1)} %tile.10.rows_ref, s32[8,128]{1,0:T(8,128)S(1)} %copy-done.19, bf16[64,1024]{1,0:T(8,128)(2,1)S(1)} %get-tuple-element.28.q_ref, bf16[64,1024]{1,0:T(8,128)(2,1)S(1)} %copy-done.14, ...), custom_call_target="tpu_custom_call" | custom-call | tf_op jit(solution)/shard_map/attend_backward/pallas_call | solution.py:901
  214.8 26.4 %scatter_values.1 = (bf16[320,128]{1,0:T(8,128)(2,1)S(1)}, bf16[64,1024]{1,0:T(8,128)(2,1)S(1)}) custom-call(bf16[2,4,2,2,320,128]{5,4,3,2,1,0:T(8,128)(2,1)S(1)} %bitcast.57, bf16[64,1024]{1,0:T(8,128)(2,1)S(1)} %get-tuple-element.40.dq_ref), custom_call_target="tpu_custom_call" | custom-call | tf_op jit(solution)/shard_map/scatter_values/pallas_call | solution.py:467
  241.9 8.2 %sum_backs.1 = bf16[4,384,128]{2,1,0:T(8,128)(2,1)S(1)} custom-call(bf16[384,128]{1,0:T(8,128)(2,1)S(1)} %pad_maximum_fusion.6.x_ref), custom_call_target="tpu_custom_call" | custom-call | tf_op jit(solution)/shard_map/sum_backs/pallas_call | solution.py:724
  250.7 0.8 fusion.27
  252.0 1.7 fusion
  254.4 0.7 pad_maximum_fusion.1
  255.1 1.8 copy.38
  257.0 1.8 copy.39
  258.8 1.7 convert_element_type.61
  260.5 1.1 pad.9
  261.6 30.7 %scatter_final.1 = (f32[128,128]{1,0:T(8,128)S(1)}, f32[2,4,4,48,128]{4,3,2,1,0:T(8,128)S(1)}) custom-call(bf16[2,4,4,128,128]{4,3,2,1,0:T(8,128)(2,1)S(1)} %pad_maximum_fusion.x_ref, bf16[2,4,4,48,128]{4,3,2,1,0:T(8,128)(2,1)S(1)} %bitcast.58), custom_call_target="tpu_custom_call" | custom-call | tf_op jit(solution)/shard_map/scatter_final/pallas_call | solution.py:535
  293.0 0.9 reshape.94
  293.9 1.3 copy.40
  295.2 1.0 copy.41
  296.2 0.7 copy.42
  (103 shorter events, 14.2 us)
Async XLA Ops:
  0.6 72.9 %copy-start = (bf16[8192,128]{1,0:T(8,128)(2,1)S(1)}, bf16[8192,128]{1,0:T(8,128)(2,1)}, u32[]{:S(2)}) copy-start(bf16[8192,128]{1,0:T(8,128)(2,1)} %param.18) | copy-start | bytes 6291460
  9.2 1.2 copy-start.2
  10.4 1.0 copy-start.5
  11.5 0.8 copy-start.17
  57.6 8.6 %copy-start.8 = (bf16[1024,256]{1,0:T(8,128)(2,1)}, bf16[1024,256]{1,0:T(8,128)(2,1)S(1)}, u32[]{:S(2)}) copy-start(bf16[1024,256]{1,0:T(8,128)(2,1)S(1)} %get-tuple-element.31.wo_ref) | copy-start | bytes 1572868
  57.6 8.5 %copy-start.4 = (bf16[2,4,4,2,128,128]{5,4,3,2,1,0:T(8,128)(2,1)}, bf16[2,4,4,2,128,128]{5,4,3,2,1,0:T(8,128)(2,1)S(1)}, u32[]{:S(2)}) copy-start(bf16[2,4,4,2,128,128]{5,4,3,2,1,0:T(8,128)(2,1)S(1)} %get-tuple-element.26) | copy-start | bytes 6291460
  57.6 4.4 %copy-start.27 = (bf16[256,8192]{1,0:T(8,128)(2,1)S(1)}, bf16[256,8192]{1,0:T(8,128)(2,1)}, u32[]{:S(2)}) copy-start(bf16[256,8192]{1,0:T(8,128)(2,1)} %param.13) | copy-start | bytes 12582916
  66.1 7.1 %copy-start.37 = (bf16[128,128]{1,0:T(8,128)(2,1)S(1)}, bf16[128,128]{1,0:T(8,128)(2,1)}, u32[]{:S(2)}) copy-start(bf16[128,128]{1,0:T(8,128)(2,1)} %param.21) | copy-start | bytes 98308
  67.2 6.3 %copy-start.3 = (bf16[64,8192]{1,0:T(8,128)(2,1)S(1)}, bf16[64,8192]{1,0:T(8,128)(2,1)}, u32[]{:S(2)}) copy-start(bf16[64,8192]{1,0:T(8,128)(2,1)} %memory_ref.1) | copy-start | bytes 3145732
  68.2 5.9 %copy-start.35 = (bf16[64,128]{0,1:T(8,128)(2,1)}, bf16[64,128]{0,1:T(8,128)(2,1)S(1)}, u32[]{:S(2)}) copy-start(bf16[64,128]{0,1:T(8,128)(2,1)S(1)} %copy.36) | copy-start | bytes 49156
  68.2 5.1 %copy-start.28 = (f32[256,256]{1,0:T(8,128)S(1)}, f32[256,256]{1,0:T(8,128)}, u32[]{:S(2)}) copy-start(f32[256,256]{1,0:T(8,128)} %convolution_bitcast_fusion) | copy-start | bytes 786436
  68.2 5.9 %copy-start.29 = (bf16[128,1024]{1,0:T(8,128)(2,1)S(1)}, bf16[128,1024]{1,0:T(8,128)(2,1)}, u32[]{:S(2)}) copy-start(bf16[128,1024]{1,0:T(8,128)(2,1)} %param.19) | copy-start | bytes 786436
  68.2 6.5 %copy-start.10 = (bf16[512,256]{1,0:T(8,128)(2,1)S(1)}, bf16[512,256]{1,0:T(8,128)(2,1)}, u32[]{:S(2)}) copy-start(bf16[512,256]{1,0:T(8,128)(2,1)} %ng_ref.1) | copy-start | bytes 786436
  68.2 6.5 %copy-start.26 = (f32[256]{0:T(256)S(1)}, f32[256]{0:T(256)}, u32[]{:S(2)}) copy-start(f32[256]{0:T(256)} %param.23) | copy-start | bytes 3076
  73.3 30.9 %copy-start.18 = (s32[8,128]{1,0:T(8,128)S(1)}, s32[8,128]{1,0:T(8,128)}, u32[]{:S(2)}) copy-start(s32[8,128]{1,0:T(8,128)} %pad.8.bounds_ref) | copy-start | bytes 12292
  73.3 30.9 %copy-start.24 = (s32[3]{0:T(128)S(1)}, s32[3]{0:T(128)}, u32[]{:S(2)}) copy-start(s32[3]{0:T(128)} %pad_add_fusion.span) | copy-start | bytes 40
  73.6 36.6 %copy-start.9 = (bf16[1024,256]{1,0:T(8,128)(2,1)S(1)}, bf16[1024,256]{1,0:T(8,128)(2,1)}, u32[]{:S(2)}) copy-start(bf16[1024,256]{1,0:T(8,128)(2,1)} %copy-done.8) | copy-start | bytes 1572868
  106.6 2.3 copy-start.1
  205.2 0.7 copy-start.11
  206.5 0.9 copy-start.14
  207.5 0.7 copy-start.19
  208.1 0.7 copy-start.21
  208.8 0.7 copy-start.23
  210.2 31.1 %copy-start.38 = (bf16[128,128]{1,0:T(8,128)(2,1)S(1)}, bf16[128,128]{1,0:T(8,128)(2,1)}, u32[]{:S(2)}) copy-start(bf16[128,128]{1,0:T(8,128)(2,1)} %param.21) | copy-start | bytes 98308
  210.2 31.3 %copy-start.30 = (bf16[128,1024]{1,0:T(8,128)(2,1)S(1)}, bf16[128,1024]{1,0:T(8,128)(2,1)}, u32[]{:S(2)}) copy-start(bf16[128,1024]{1,0:T(8,128)(2,1)} %param.19) | copy-start | bytes 786436
  241.2 0.7 copy-start.6
  250.7 3.2 %copy-start.16 = (bf16[320,128]{1,0:T(8,128)(2,1)S(1)}, bf16[320,128]{1,0:T(8,128)(2,1)}, u32[]{:S(2)}) copy-start(bf16[320,128]{1,0:T(8,128)(2,1)} %copy-done.15) | copy-start | bytes 245764
  250.7 3.2 %copy-start.32 = (bf16[256,128]{0,1:T(8,128)(2,1)S(1)}, bf16[256,128]{0,1:T(8,128)(2,1)}, u32[]{:S(2)}) copy-start(bf16[256,128]{0,1:T(8,128)(2,1)} %copy-done.31) | copy-start | bytes 196612
  250.7 3.2 %copy-start.36 = (bf16[64,128]{0,1:T(8,128)(2,1)S(1)}, bf16[64,128]{0,1:T(8,128)(2,1)}, u32[]{:S(2)}) copy-start(bf16[64,128]{0,1:T(8,128)(2,1)} %copy-done.35) | copy-start | bytes 49156
  251.5 2.6 copy-start.7
  251.5 2.6 copy-start.34
  260.5 36.4 %copy-start.12 = (bf16[512,256]{1,0:T(8,128)(2,1)S(1)}, bf16[512,256]{1,0:T(8,128)(2,1)}, u32[]{:S(2)}) copy-start(bf16[512,256]{1,0:T(8,128)(2,1)} %copy-done.11) | copy-start | bytes 786436
  (7 other events, 4.4 us)

commit v4 on v3

--- a/solution.py
+++ b/solution.py
@@ -198,138 +198,178 @@
     return [pltpu.SemaphoreType.DMA((count,)) for _ in range(4)]
 
 
-def opening_kernel(
-    pieces, half_pieces, kv_ref, down_ref, memory_ref, weight_ref, wo_ref,
-    kv_all, down_all, acc_ref, wo_out,
-    send, recv, fore, back, buffer, loads, local, swap_send, swap_recv, swap_local,
+def front_kernel(
+    pieces, half_pieces, kv_pieces,
+    key_ref, value_ref, down_ref, context_ref, memory_ref, weight_ref, query_down_ref, query_up_ref,
+    value_up_ref, wo_ref, ng_ref, gain_ref,
+    kv_all, q_out, query_low, value_low, wo_out, ng_out, gain_out,
+    shard, w_all, d_all, context, memory, query_down, buffer, acc, projected, kv_own, q_own,
+    send, recv, fore, back, k_send, k_recv, k_fore, k_back,
+    loads, inputs, local, swap_send, swap_recv, swap_local,
 ):
+    f32, bf16 = jnp.float32, jnp.bfloat16
     here = coords(PLAIN)
     depth = buffer.shape[1]
     count = weight_ref.shape[0] // depth
+    half = down_ref.shape[0] // 2
+    tok = context_ref.shape[0]
 
     def load(k):
         return pltpu.make_async_copy(
             weight_ref.at[pl.ds(k * depth, depth)], buffer.at[k % 3], loads.at[k % 3]
         )
 
+    own_half = down_ref.at[pl.ds(here["c"] * half, half)]
+    fetches = [
+        pltpu.make_async_copy(a, b, inputs.at[i])
+        for i, (a, b) in enumerate(
+            (
+                (key_ref, shard.at[:, pl.ds(0, HD)]),
+                (value_ref, shard.at[:, pl.ds(HD, HD)]),
+                (memory_ref, memory),
+                (query_down_ref, query_down),
+                (context_ref, context),
+            )
+        )
+    ]
+    for fetch in fetches:
+        fetch.start()
     for k in range(2):
         load(k).start()
     greet(axis_peers(PLAIN + "c", here), here)
-    swap = Swap(here, wo_ref, wo_out, swap_send, swap_recv, swap_local)
-    half = down_ref.shape[0] // 2
-    own_half = down_ref.at[pl.ds(here["c"] * half, half)]
+    swaps = [
+        Swap(here, a, b, swap_send.at[i], swap_recv.at[i], swap_local.at[i])
+        for i, (a, b) in enumerate(
+            (
+                (kv_own, kv_all.at[here["y"], here["z"], here["h"], here["l"]]),
+                (q_own, q_out),
+                (gain_ref, gain_out),
+                (ng_ref, ng_out),
+                (wo_ref, wo_out),
+            )
+        )
+    ]
+    fetches[0].wait()
+    fetches[1].wait()
     sems = (send, recv, fore, back)
-    plain = Gather(here, PLAIN, pieces, kv_ref, kv_all, sems, 0)
-    shared = Gather(
-        here, PLAIN + "c", half_pieces, own_half, down_all, sems, 9 * len(pieces) + 1
-    )
+    plain = Gather(here, PLAIN, pieces, shard, w_all, sems, 0)
+    shared = Gather(here, PLAIN + "c", half_pieces, own_half, d_all, sems, 9 * len(pieces) + 1)
     owns = [
-        pltpu.make_async_copy(kv_ref, kv_all.at[plain.place], local.at[0]),
-        pltpu.make_async_copy(own_half, down_all.at[shared.place], local.at[1]),
+        pltpu.make_async_copy(shard, w_all.at[plain.place], local.at[0]),
+        pltpu.make_async_copy(own_half, d_all.at[shared.place], local.at[1]),
     ]
     for own in owns:
         own.start()
-    acc_ref[...] = jnp.zeros_like(acc_ref)
 
     def between(phase):
         if phase < 2:
             return
-        swap.start()
+        swaps[4].start()
+        fetches[2].wait()
+        fetches[3].wait()
+        low = jnp.dot(memory[...], query_down[...], preferred_element_type=f32).astype(bf16)
+        query_low[...] = low
+        acc[...] = adapter_scale * jnp.dot(low, query_up_ref[...], preferred_element_type=f32)
         for k in range(count):
             load(k).wait()
             if k + 2 < count:
                 load(k + 2).start()
-            acc_ref[...] += jnp.dot(
-                memory_ref[:, k * depth : (k + 1) * depth],
-                buffer[k % 3],
-                preferred_element_type=jnp.float32,
+            acc[...] += jnp.dot(
+                memory[:, k * depth : (k + 1) * depth], buffer[k % 3], preferred_element_type=f32
             )
+        q_own[...] = acc[...].astype(bf16)
+        fetches[4].wait()
 
     run_gathers([plain, shared], owns, between)
-    swap.wait()
-
-
-def opening(kv_weight, down, memory, query_weight, output_weight, collective_id):
-    rows, cols = kv_weight.shape
-    half = down.shape[0] // 2
-    pieces = cut(rows, cols, ORDERS[PLAIN])
-    half_pieces = cut(half, down.shape[1], ORDERS[PLAIN])
+    wide = 4 * shard.shape[0]
+    for j in range(8):
+        at = (j // 4, j % 4)
+        kv_rows = w_all[at].reshape(wide, 2 * HD)
+        down_rows = d_all[at].reshape(wide, HD)
+        for rows, source in ((slice(0, tok), context), (slice(tok, None), memory)):
+            part = source[:, j * wide : (j + 1) * wide]
+            for cols, right in ((slice(0, 2 * HD), kv_rows), (slice(2 * HD, None), down_rows)):
+                step = jnp.dot(part, right, preferred_element_type=f32)
+                projected[rows, cols] = step if j == 0 else projected[rows, cols] + step
+    low = projected[:, 2 * HD :].astype(bf16)
+    value_low[...] = low
+    kv_own[:, :HD] = projected[:, :HD].astype(bf16)
+    kv_own[:, HD:] = (
+        projected[:, HD : 2 * HD]
+        + adapter_scale * jnp.dot(low, value_up_ref[...], preferred_element_type=f32)
+    ).astype(bf16)
+    swaps[0].start()
+    swaps[0].wait()
+    gather = Gather(here, PAIRED, kv_pieces, None, kv_all, (k_send, k_recv, k_fore, k_back), 0)
+
+    def rest(phase):
+        if phase == 2:
+            for swap in swaps[1:4]:
+                swap.start()
+
+    run_gathers([gather], [], rest)
+    for swap in swaps[1:]:
+        swap.wait()
+
+
+def front(
+    key_weight, value_weight, down, context, memory, query_weight, query_down, query_up, value_up,
+    output_weight, normed_gradient, gain, collective_id,
+):
+    f32, bf16 = jnp.float32, jnp.bfloat16
+    rows, half = key_weight.shape[0], down.shape[0] // 2
+    tok, slots, model = context.shape[0], memory.shape[0], memory.shape[1]
+    keys, wide = tok + slots, query_weight.shape[1]
+    pieces = cut(rows, 2 * HD, ORDERS[PLAIN])
+    half_pieces = cut(half, HD, ORDERS[PLAIN])
+    kv_pieces = cut(keys, 2 * HD, ORDERS[PAIRED])
     n = 9 * len(pieces) + 1 + 9 * len(half_pieces) + 1
-    outs = pl.pallas_call(
-        functools.partial(opening_kernel, pieces, half_pieces),
+    like = lambda a: jax.ShapeDtypeStruct(a.shape, a.dtype)
+    sizes = [SIZES[a] for a in PAIRED]
+    dma = pltpu.SemaphoreType.DMA
+    kv, *rest = pl.pallas_call(
+        functools.partial(front_kernel, pieces, half_pieces, kv_pieces),
         out_shape=(
-            jax.ShapeDtypeStruct((2, 4, 4, rows, cols), kv_weight.dtype),
-            jax.ShapeDtypeStruct((2, 4, 4, 2, half, down.shape[1]), down.dtype),
-            jax.ShapeDtypeStruct((memory.shape[0], query_weight.shape[1]), jnp.float32),
-            jax.ShapeDtypeStruct(output_weight.shape, output_weight.dtype),
+            jax.ShapeDtypeStruct((*sizes, keys, 2 * HD), bf16),
+            jax.ShapeDtypeStruct((slots, wide), bf16),
+            jax.ShapeDtypeStruct((slots, HD), bf16),
+            jax.ShapeDtypeStruct((keys, HD), bf16),
+            like(output_weight),
+            like(normed_gradient),
+            like(gain),
         ),
-        in_specs=[ANY, ANY, VMEM, HBM, ANY],
-        out_specs=(ANY, ANY, VMEM, ANY),
-        scratch_shapes=semaphores(n)
-        + [
-            pltpu.VMEM((3, 1024, query_weight.shape[1]), jnp.bfloat16),
-            pltpu.SemaphoreType.DMA((3,)),
-            pltpu.SemaphoreType.DMA((2,)),
-            pltpu.SemaphoreType.DMA,
-            pltpu.SemaphoreType.DMA,
-            pltpu.SemaphoreType.DMA,
+        in_specs=[ANY] * 7 + [VMEM] * 2 + [ANY] * 3,
+        out_specs=(ANY, ANY, VMEM, VMEM, ANY, ANY, ANY),
+        scratch_shapes=[
+            pltpu.VMEM((rows, 2 * HD), bf16),
+            pltpu.VMEM((2, 4, 4, rows, 2 * HD), bf16),
+            pltpu.VMEM((2, 4, 4, 2, half, HD), bf16),
+            pltpu.VMEM((tok, model), bf16),
+            pltpu.VMEM((slots, model), bf16),
+            pltpu.VMEM((model, HD), bf16),
+            pltpu.VMEM((3, 1024, wide), bf16),
+            pltpu.VMEM((slots, wide), f32),
+            pltpu.VMEM((keys, 3 * HD), f32),
+            pltpu.VMEM((keys, 2 * HD), bf16),
+            pltpu.VMEM((slots, wide), bf16),
+            *semaphores(n),
+            *semaphores(9 * len(kv_pieces) + 1),
+            dma((3,)),
+            dma((5,)),
+            dma((2,)),
+            dma((5,)),
+            dma((5,)),
+            dma((5,)),
         ],
         compiler_params=pltpu.CompilerParams(
-            collective_id=collective_id, has_side_effects=True, vmem_limit_bytes=46 << 20
+            collective_id=collective_id, has_side_effects=True, vmem_limit_bytes=61 << 20
         ),
-        name="opening",
-    )(kv_weight, down, memory, query_weight, output_weight)
-    return (
-        outs[0].reshape(32 * rows, cols),
-        outs[1].reshape(32 * 2 * half, down.shape[1]),
-        *outs[2:],
+        name="front",
+    )(
+        key_weight, value_weight, down, context, memory, query_weight, query_down, query_up, value_up,
+        output_weight, normed_gradient, gain,
     )
-
-
-def keys_kernel(
-    pieces, x_ref, q_ref, ng_ref, gain_ref, o_ref, q_out, ng_out, gain_out,
-    send, recv, fore, back, swap_send, swap_recv, swap_local,
-):
-    here = coords(PAIRED)
-    greet(axis_peers(PAIRED, here), here)
-    home = o_ref.at[here["y"], here["z"], here["h"], here["l"]]
-    ends = ((x_ref, home), (q_ref, q_out), (gain_ref, gain_out), (ng_ref, ng_out))
-    swaps = [
-        Swap(here, a, b, swap_send.at[i], swap_recv.at[i], swap_local.at[i])
-        for i, (a, b) in enumerate(ends)
-    ]
-    swaps[0].start()
-    swaps[0].wait()
-    gather = Gather(here, PAIRED, pieces, None, o_ref, (send, recv, fore, back), 0)
-
-    def between(phase):
-        if phase == 2:
-            for swap in swaps[1:]:
-                swap.start()
-
-    run_gathers([gather], [], between)
-    for swap in swaps[1:]:
-        swap.wait()
-
-
-def gather_keys(x, q, normed_gradient, gain, collective_id):
-    rows, cols = x.shape
-    pieces = cut(rows, cols, ORDERS[PAIRED])
-    n = 9 * len(pieces) + 1
-    sizes = [SIZES[a] for a in PAIRED]
-    swapped = [jax.ShapeDtypeStruct(a.shape, a.dtype) for a in (q, normed_gradient, gain)]
-    kv, *rest = pl.pallas_call(
-        functools.partial(keys_kernel, pieces),
-        out_shape=(jax.ShapeDtypeStruct((*sizes, rows, cols), x.dtype), *swapped),
-        in_specs=[ANY] * 4,
-        out_specs=(ANY,) * 4,
-        scratch_shapes=semaphores(n) + [pltpu.SemaphoreType.DMA((4,))] * 3,
-        compiler_params=pltpu.CompilerParams(
-            collective_id=collective_id, has_side_effects=True, vmem_limit_bytes=1 << 20
-        ),
-        name="gather_keys",
-    )(x, q, normed_gradient, gain)
-    return kv.reshape(32, rows, cols), *rest
+    return kv.reshape(32, keys, 2 * HD), *rest
 
 
 ORDERS = {
@@ -447,52 +487,62 @@
     return x.reshape(*[SIZES[a] for a in axes], *x.shape[1:])
 
 
-def values_kernel(
-    pieces, x_ref, dq_ref, o_ref, dq_out, send, recv, swap_send, swap_recv, swap_local, own, *bufs
+def tail_kernel(
+    dv_pieces, pieces, up_pieces, spread,
+    dv_ref, dq_ref, query_low, value_low, query_up_ref, value_up_ref, memory_ref, context_ref,
+    qa_ref, va_ref, query_up_out, value_up_out,
+    dv_own, dv_home, dq_home, context, memory, backs, backs_in, down_x, up_x, own, everyone, result,
+    v_send, v_recv, swap_send, swap_recv, swap_local, inputs, b_send, b_recv,
+    send, recv, up_send, up_recv, g_send, g_recv, g_fore, g_back, local, *bufs,
 ):
+    f32, bf16 = jnp.float32, jnp.bfloat16
     here = coords(PAIRED)
-    greet(axis_peers(PAIRED, here), here)
-    first = Swap(here, dq_ref, dq_out, swap_send.at[0], swap_recv.at[0], swap_local.at[0])
-    second = Swap(here, own, o_ref, swap_send.at[1], swap_recv.at[1], swap_local.at[1])
-    first.start()
-    Scatter(here, PAIRED, pieces, x_ref, own, send, recv, bufs).run()
-    second.start()
-    first.wait()
-    second.wait()
-
-
-def scatter_values(x, d_queries, collective_id):
-    _, rows, cols = x.shape
-    pieces, sems, bufs = scatter_plan(rows, cols, PAIRED)
-    return pl.pallas_call(
-        functools.partial(values_kernel, pieces),
-        out_shape=(
-            jax.ShapeDtypeStruct((rows, cols), jnp.bfloat16),
-            jax.ShapeDtypeStruct(d_queries.shape, d_queries.dtype),
-        ),
-        in_specs=[VMEM, ANY],
-        out_specs=(ANY, ANY),
-        scratch_shapes=sems
-        + [pltpu.SemaphoreType.DMA((2,))] * 3
-        + [pltpu.VMEM((rows, cols), jnp.bfloat16)]
-        + bufs,
-        compiler_params=pltpu.CompilerParams(
-            collective_id=collective_id, has_side_effects=True, vmem_limit_bytes=40 << 20
-        ),
-        name="scatter_values",
-    )(split_axes(x, PAIRED), d_queries)
-
-
-def final_kernel(
-    pieces, up_pieces, spread, x_ref, up_ref, o_ref, all_ref,
-    send, recv, up_send, up_recv, g_send, g_recv, g_fore, g_back, local, own, *bufs,
-):
-    here = coords(PLAIN)
-    greet(axis_peers(PLAIN, here))
-    cut_at = 5 * len(up_pieces)
-    up = Scatter(here, PLAIN, up_pieces, up_ref, own, up_send, up_recv, bufs[:cut_at])
-    down = Scatter(here, PLAIN, pieces, x_ref, o_ref, send, recv, bufs[cut_at:])
-    gather = Gather(here, PLAIN, spread, own, all_ref, (g_send, g_recv, g_fore, g_back), 0)
+    slots = memory.shape[0]
+    tok = context.shape[0]
+    columns = pl.ds(lax.axis_index("section") * memory.shape[1], memory.shape[1])
+    fetches = [
+        pltpu.make_async_copy(memory_ref.at[:, columns], memory, inputs.at[0]),
+        pltpu.make_async_copy(context_ref.at[:, columns], context, inputs.at[1]),
+    ]
+    for fetch in fetches:
+        fetch.start()
+    me, member = group_place("section", here)
+    others = [lax.rem(me + d, 4) for d in range(1, 4)]
+    across = [{**here, "m": 1 - here["m"], "c": lax.rem(here["c"] + d, 2)} for d in range(2)]
+    greet(axis_peers(PLAIN + "c", here) + [device_at(PLAIN, place) for place in across], here)
+
+    swaps = [
+        Swap(here, a, b, swap_send.at[i], swap_recv.at[i], swap_local.at[i])
+        for i, (a, b) in enumerate(((dq_ref, dq_home), (dv_own, dv_home)))
+    ]
+    at_v, at_up = 7 * len(dv_pieces), 5 * len(up_pieces)
+    swaps[0].start()
+    Scatter(here, PAIRED, dv_pieces, dv_ref, dv_own, v_send, v_recv, bufs[:at_v]).run()
+    swaps[1].start()
+
+    def up_rows(j, block):
+        block = (adapter_scale * block).astype(bf16)
+        for i in range(8):
+            slot, third = divmod(j * 8 + i, 3)
+            up_x[slot // 16, (slot // 4) % 4, slot % 4, 16 * third : 16 * third + 16, :] = block[
+                16 * i : 16 * i + 16
+            ]
+
+    swaps[0].wait()
+    for j in range(HEADS_HERE):
+        up_rows(j, contract(query_low[...], dq_home[:, j * HD : (j + 1) * HD], 0, 0))
+    up_x[1, 2:] = jnp.zeros_like(up_x[1, 2:])
+    backs[:slots, :] = (adapter_scale * contract(dq_home[...], query_up_ref[...], 1, 1)).astype(bf16)
+    swaps[1].wait()
+    up_rows(HEADS_HERE, contract(value_low[...], dv_home[...], 0, 0))
+    backs[slots:, :] = (adapter_scale * contract(dv_home[...], value_up_ref[...], 1, 1)).astype(bf16)
+    copies = [
+        remote(backs, backs_in.at[d], b_send.at[d], b_recv.at[d], member(k))
+        for d, k in enumerate(others)
+    ]
+    up = Scatter(here, PLAIN, up_pieces, up_x, own, up_send, up_recv, bufs[at_v : at_v + at_up])
+    down = Scatter(here, PLAIN, pieces, down_x, result, send, recv, bufs[at_v + at_up :])
+    gather = Gather(here, PLAIN, spread, own, everyone, (g_send, g_recv, g_fore, g_back), 0)
 
     def stage(scatter, phase):
         for i in range(len(scatter.pieces)):
@@ -508,12 +558,28 @@
             gather.launch(phase, i)
 
     stage(up, 0)
+    for copy in copies:
+        copy.wait()
+    whole = backs[...].astype(f32)
+    for d in range(3):
+        whole = whole + backs_in[d].astype(f32)
+    whole = whole.astype(bf16)
+    pair = jnp.concatenate([whole[:slots], whole[slots + tok :]], axis=1)
+    for fetch in fetches:
+        fetch.wait()
+    span = memory.shape[1] // 2
+    rows = span // 16
+    for y in range(2):
+        both = contract(memory[:, y * span : (y + 1) * span], pair, 0, 0)
+        more = contract(context[:, y * span : (y + 1) * span], whole[slots : slots + tok], 0, 0)
+        down_x[y, :, :, :rows, :] = both[:, :HD].astype(bf16).reshape(4, 4, rows, HD)
+        down_x[y, :, :, rows:, :] = (both[:, HD:] + more).astype(bf16).reshape(4, 4, rows, HD)
     stage(down, 0)
     stage(up, 1)
     stage(up, 2)
     stage(down, 1)
     stage(up, 3)
-    copy = pltpu.make_async_copy(own, all_ref.at[gather.place], local)
+    copy = pltpu.make_async_copy(own, everyone.at[gather.place], local)
     copy.start()
     spread_on(0)
     stage(down, 2)
@@ -521,37 +587,78 @@
     spread_on(1)
     spread_on(2)
     stage(down, 3)
+    qa_ref[...] = result[:rows, :]
+    va_ref[...] = result[rows:, :]
     gather.finish()
+    for j in range(HEADS_HERE + 1):
+        for i in range(8):
+            slot, third = divmod(j * 8 + i, 3)
+            tile = everyone[slot // 16, (slot // 4) % 4, slot % 4, 16 * third : 16 * third + 16, :]
+            if j < HEADS_HERE:
+                query_up_out[16 * i : 16 * i + 16, j * HD : (j + 1) * HD] = tile
+            else:
+                value_up_out[16 * i : 16 * i + 16, :] = tile
     for one in up.copies + down.copies:
         one.wait_send()
 
 
-def scatter_final(x, up, collective_id):
-    _, rows, cols = x.shape
-    up_rows = up.shape[1]
-    pieces, sems, bufs = scatter_plan(rows, cols, PLAIN)
-    up_pieces, up_sems, up_bufs = scatter_plan(up_rows, cols, PLAIN)
-    spread = cut(up_rows, cols, ORDERS[PLAIN])
-    out, ups = pl.pallas_call(
-        functools.partial(final_kernel, pieces, up_pieces, spread),
+def tail(dv_part, d_queries, query_low, value_low, query_up_map, value_up_map, memory, context, collective_id):
+    f32, bf16 = jnp.float32, jnp.bfloat16
+    _, keys, _ = dv_part.shape
+    slots, tok = memory.shape[0], context.shape[0]
+    width = memory.shape[1] // 4
+    rows = width // 32
+    dv_pieces, dv_sems, dv_bufs = scatter_plan(keys, HD, PAIRED)
+    pieces, sems, bufs = scatter_plan(2 * rows, HD, PLAIN)
+    up_pieces, up_sems, up_bufs = scatter_plan(48, HD, PLAIN)
+    spread = cut(48, HD, ORDERS[PLAIN])
+    dma = pltpu.SemaphoreType.DMA
+    return pl.pallas_call(
+        functools.partial(tail_kernel, dv_pieces, pieces, up_pieces, spread),
         out_shape=(
-            jax.ShapeDtypeStruct((rows, cols), jnp.float32),
-            jax.ShapeDtypeStruct((2, 4, 4, up_rows, cols), jnp.float32),
+            jax.ShapeDtypeStruct((rows, HD), f32),
+            jax.ShapeDtypeStruct((rows, HD), f32),
+            jax.ShapeDtypeStruct(query_up_map.shape, f32),
+            jax.ShapeDtypeStruct(value_up_map.shape, f32),
         ),
-        in_specs=[VMEM, VMEM],
-        out_specs=(VMEM, VMEM),
-        scratch_shapes=sems
-        + up_sems
-        + semaphores(9 * len(spread) + 1)
-        + [pltpu.SemaphoreType.DMA, pltpu.VMEM((up_rows, cols), jnp.float32)]
-        + up_bufs
-        + bufs,
+        in_specs=[VMEM, ANY, VMEM, VMEM, VMEM, VMEM, ANY, ANY],
+        out_specs=(VMEM,) * 4,
+        scratch_shapes=[
+            pltpu.VMEM((keys, HD), bf16),
+            pltpu.VMEM((keys, HD), bf16),
+            pltpu.VMEM(d_queries.shape, bf16),
+            pltpu.VMEM((tok, width), bf16),
+            pltpu.VMEM((slots, width), bf16),
+            pltpu.VMEM((slots + keys, HD), bf16),
+            pltpu.VMEM((3, slots + keys, HD), bf16),
+            pltpu.VMEM((2, 4, 4, 2 * rows, HD), bf16),
+            pltpu.VMEM((2, 4, 4, 48, HD), bf16),
+            pltpu.VMEM((48, HD), f32),
+            pltpu.VMEM((2, 4, 4, 48, HD), f32),
+            pltpu.VMEM((2 * rows, HD), f32),
+            *dv_sems,
+            dma((2,)),
+            dma((2,)),
+            dma((2,)),
+            dma((2,)),
+            dma((3,)),
+            dma((3,)),
+            *sems,
+            *up_sems,
+            *semaphores(9 * len(spread) + 1),
+            dma,
+            *dv_bufs,
+            *up_bufs,
+            *bufs,
+        ],
         compiler_params=pltpu.CompilerParams(
             collective_id=collective_id, has_side_effects=True, vmem_limit_bytes=40 << 20
         ),
-        name="scatter_final",
-    )(split_axes(x, PLAIN), split_axes(up, PLAIN))
-    return out, ups.reshape(32, up_rows, cols)
+        name="tail",
+    )(
+        split_axes(dv_part, PAIRED), d_queries, query_low, value_low, query_up_map, value_up_map,
+        memory, context,
+    )
 
 
 def middle_kernel(
@@ -703,41 +810,6 @@
         return here["m"] * 2 + here["c"], lambda k: device_at("x", {**here, "m": k // 2, "c": k % 2})
     return here["m"] * 2 + here["l"], lambda k: device_at("h", {**here, "m": k // 2, "l": k % 2})
 
-def exchange_kernel(group, count, apart, x_ref, o_ref, send, recv, local):
-    me, device = group_place(group, coords(PLAIN))
-    others = [lax.rem(me + d, count) for d in range(1, count)]
-    greet([device(k) for k in others])
-    own = pltpu.make_async_copy(x_ref.at[me] if apart else x_ref, o_ref.at[me], local)
-    own.start()
-    copies = [
-        remote(x_ref.at[k] if apart else x_ref, o_ref.at[me], send.at[d], recv.at[d], device(k))
-        for d, k in enumerate(others)
-    ]
-    own.wait()
-    for copy in copies:
-        copy.wait()
-
-
-def exchange(x, group, apart, collective_id, name):
-    count = 4
-    shape = x.shape[1:] if apart else x.shape
-    return pl.pallas_call(
-        functools.partial(exchange_kernel, group, count, apart),
-        out_shape=jax.ShapeDtypeStruct((count, *shape), x.dtype),
-        in_specs=[ANY],
-        out_specs=ANY,
-        scratch_shapes=[
-            pltpu.SemaphoreType.DMA((count - 1,)),
-            pltpu.SemaphoreType.DMA((count - 1,)),
-            pltpu.SemaphoreType.DMA,
-        ],
-        compiler_params=pltpu.CompilerParams(
-            collective_id=collective_id, has_side_effects=True, vmem_limit_bytes=1 << 20
-        ),
-        name=name,
-    )(x)
-
-
 def contract(left, right, l, r):
     return lax.dot_general(
         left, right, (((l,), (r,)), ((), ())), preferred_element_type=jnp.float32
@@ -757,37 +829,63 @@
     return jnp.concatenate([context, memory.reshape(GROUP * slots, HD)], axis=0)
 
 
-def key_docs(g, bounds_ref, context_rows, slots):
+def key_docs(g, bounds, context_rows, slots):
     edge = GROUP * context_rows
     token = g * edge + lax.broadcasted_iota(jnp.int32, (edge, HD), 0)
-    docs = (token >= 4 * bounds_ref[0:1, :]) & (token < 4 * bounds_ref[1:2, :])
+    docs = (token >= 4 * bounds[0][0:1, :]) & (token < 4 * bounds[1][0:1, :])
     if slots:
         slot = g * (GROUP * slots) + lax.broadcasted_iota(jnp.int32, (GROUP * slots, HD), 0)
         docs = jnp.concatenate(
             [
                 docs.astype(jnp.float32),
-                ((slot >= bounds_ref[0:1, :]) & (slot < bounds_ref[1:2, :])).astype(jnp.float32),
+                ((slot >= bounds[0][0:1, :]) & (slot < bounds[1][0:1, :])).astype(jnp.float32),
             ],
             axis=0,
         )
     return docs.astype(jnp.float32).astype(jnp.bfloat16)
 
 
-def with_fill(q, rows_ref, bounds_ref):
-    low = jnp.transpose(rows_ref[2:3, :].astype(jnp.float32) + jnp.zeros((HD, ROWS), jnp.float32))
-    mine = low == bounds_ref[0:1, :].astype(jnp.float32)
-    return jnp.concatenate([q, jnp.where(mine, 0.0, mask_fill).astype(jnp.bfloat16)], axis=1)
-
-
-def group_scores(keys, g, q_wide, rows_ref, bounds_ref, context_rows, slots, causal):
-    docs = key_docs(g, bounds_ref, context_rows, slots)
+def documents(docs_ref):
+    starts, ends, at = [], [], 0
+    for k in range(docs_ref.shape[0] - 1):
+        starts.append(at)
+        at = at + docs_ref[k]
+        ends.append(at)
+    return starts, ends
+
+
+def place_rows(docs_ref, here):
+    starts, ends = documents(docs_ref)
+    first = docs_ref[docs_ref.shape[0] - 1]
+    last = first + here - 1
+    lane = lax.broadcasted_iota(jnp.int32, (8, HD), 1)
+    low_lane, high_lane = jnp.zeros((8, HD), jnp.int32), jnp.zeros((8, HD), jnp.int32)
+    slot = first + lax.rem(lax.broadcasted_iota(jnp.int32, (ROWS, HD), 0), here)
+    low = jnp.zeros((ROWS, HD), jnp.int32)
+    start, stop = 0, ends[-1]
+    for k in range(len(starts)):
+        low_lane = jnp.where(lane == k, starts[k], low_lane)
+        high_lane = jnp.where(lane == k, ends[k], high_lane)
+        low = jnp.where(slot >= starts[k], starts[k], low)
+        start = jnp.where(first >= starts[k], starts[k], start)
+        stop = jnp.where((last >= starts[k]) & (last < ends[k]), ends[k], stop)
+    mine = low == low_lane[0:1, :]
+    fill = jnp.where(mine, 0.0, mask_fill).astype(jnp.bfloat16)
+    row_slot = first + lax.rem(lax.broadcasted_iota(jnp.int32, (8, ROWS), 1), here)
+    unit = GROUP * here
+    span = (start // unit, first // unit, (stop + unit - 1) // unit)
+    return span, row_slot, (low_lane, high_lane), fill
+
+
+def group_scores(keys, g, q_wide, row_slot, bounds, context_rows, slots, causal):
+    docs = key_docs(g, bounds, context_rows, slots)
     scores = contract(jnp.concatenate([keys, docs], axis=1), q_wide, 1, 1)
     if not causal:
         return scores
     edge = GROUP * context_rows
     slot = g * (GROUP * slots) + lax.broadcasted_iota(jnp.int32, (GROUP * slots, ROWS), 0)
     return jnp.concatenate(
-        [scores[:edge], jnp.where(slot <= rows_ref[3:4, :], scores[edge:], mask_fill)], axis=0
+        [scores[:edge], jnp.where(slot <= row_slot[0:1, :], scores[edge:], mask_fill)], axis=0
     )
 
 
@@ -808,10 +906,11 @@
 
 
 def attend_kernel(
-    context_rows, span, rows_ref, bounds_ref, q_ref, kv_ref, o_ref, ot_ref, top_ref, mass_ref
+    context_rows, docs_ref, q_ref, kv_ref, o_ref, ot_ref, top_ref, mass_ref
 ):
     slots = kv_ref.shape[1] - context_rows
-    q = with_fill(head_rows(q_ref), rows_ref, bounds_ref)
+    span, row_slot, bounds, fill = place_rows(docs_ref, q_ref.shape[0])
+    q = jnp.concatenate([head_rows(q_ref), fill], axis=1)
     ot_ref[...] = jnp.zeros_like(ot_ref)
     top_ref[...] = jnp.full_like(top_ref, mask_fill)
     mass_ref[...] = jnp.zeros_like(mass_ref)
@@ -819,7 +918,7 @@
     def step(g, masked, with_memory):
         extra = slots if with_memory else 0
         keys = key_block(kv_ref, g, slice(0, HD), context_rows, extra)
-        scores = group_scores(keys, g, q, rows_ref, bounds_ref, context_rows, extra, masked)
+        scores = group_scores(keys, g, q, row_slot, bounds, context_rows, extra, masked)
         before = top_ref[0:1, :]
         top = jnp.maximum(before, jnp.max(scores, axis=0, keepdims=True))
         keep = jnp.exp2((before - top) * exp2_scale)
@@ -838,12 +937,13 @@
 
 
 def backward_kernel(
-    context_rows, span, rows_ref, bounds_ref, q_ref, g_ref, kv_ref, ot_ref, top_ref, mass_ref,
+    context_rows, docs_ref, q_ref, g_ref, kv_ref, ot_ref, top_ref, mass_ref,
     dq_ref, dv_ref, acc,
 ):
     slots = kv_ref.shape[1] - context_rows
     edge = GROUP * context_rows
-    q = with_fill(head_rows(q_ref), rows_ref, bounds_ref)
+    span, row_slot, bounds, fill = place_rows(docs_ref, q_ref.shape[0])
+    q = jnp.concatenate([head_rows(q_ref), fill], axis=1)
     grad = head_rows(g_ref)
     center = jnp.sum(jnp.transpose(grad.astype(jnp.float32)) * ot_ref[...], axis=0, keepdims=True)
     top = top_ref[0:1, :]
@@ -854,7 +954,7 @@
     def step(g, masked, with_memory):
         extra = slots if with_memory else 0
         keys = key_block(kv_ref, g, slice(0, HD), context_rows, extra)
-        scores = group_scores(keys, g, q, rows_ref, bounds_ref, context_rows, extra, masked)
+        scores = group_scores(keys, g, q, row_slot, bounds, context_rows, extra, masked)
         probs = jnp.exp2((scores - top) * exp2_scale) * share
         values = key_block(kv_ref, g, slice(HD, 2 * HD), context_rows, extra)
         d_probs = contract(values, grad, 1, 1)
@@ -880,7 +980,7 @@
 BIG = pltpu.CompilerParams(vmem_limit_bytes=48 << 20)
 
 
-def attend(span, rows, bounds, q, kv, context_rows):
+def attend(docs, q, kv, context_rows):
     f32 = jnp.float32
     return pl.pallas_call(
         functools.partial(attend_kernel, context_rows),
@@ -890,44 +990,26 @@
             jax.ShapeDtypeStruct((8, ROWS), f32),
             jax.ShapeDtypeStruct((8, ROWS), f32),
         ),
-        in_specs=[SMEM] + [VMEM] * 4,
+        in_specs=[SMEM] + [VMEM] * 2,
         out_specs=(VMEM, VMEM, VMEM, VMEM),
         compiler_params=BIG,
         name="attend",
-    )(span, rows, bounds, q, kv)
-
-
-def attend_backward(span, rows, bounds, q, grad, kv, ot, top, mass, context_rows):
+    )(docs, q, kv)
+
+
+def attend_backward(docs, q, grad, kv, ot, top, mass, context_rows):
     return pl.pallas_call(
         functools.partial(backward_kernel, context_rows),
         out_shape=(
             jax.ShapeDtypeStruct(q.shape, jnp.bfloat16),
             jax.ShapeDtypeStruct((*kv.shape[:2], HD), jnp.bfloat16),
         ),
-        in_specs=[SMEM] + [VMEM] * 8,
+        in_specs=[SMEM] + [VMEM] * 6,
         out_specs=(VMEM, VMEM),
         scratch_shapes=[pltpu.VMEM((HD, ROWS), jnp.float32)],
         compiler_params=BIG,
         name="attend_backward",
-    )(span, rows, bounds, q, grad, kv, ot, top, mass)
-
-
-def row_bounds(document_slots, first, slot_dev, seq_size):
-    docs = document_slots.shape[0]
-    order = jnp.arange(docs, dtype=jnp.int32)
-    ends = jnp.sum(jnp.where(order[None, :] <= order[:, None], document_slots[None, :], 0), axis=1)
-    slot = first + jnp.arange(slot_dev, dtype=jnp.int32)
-    passed = ends[None, :] <= slot[:, None]
-    low = jnp.max(jnp.where(passed, ends[None, :], 0), axis=1)
-    high = jnp.min(jnp.where(passed, slot_dev * seq_size, ends[None, :]), axis=1)
-    one = jnp.stack([4 * low, 4 * high, low, slot] + [slot] * 4).astype(jnp.int32)
-    unit = GROUP * slot_dev
-    start, stop = jnp.min(low) // unit, (jnp.max(high) + unit - 1) // unit
-    span = jnp.stack([start, first // unit, stop])
-    starts = ends - document_slots
-    bounds = jnp.stack([starts, ends] + [ends] * 6)
-    bounds = jnp.pad(bounds, ((0, 0), (0, HD - docs)))
-    return span.astype(jnp.int32), jnp.tile(one, (1, HEADS_HERE)), bounds.astype(jnp.int32)
+    )(docs, q, grad, kv, ot, top, mass)
 
 
 def body(
@@ -945,91 +1027,25 @@
     document_slots,
     normed_gradient,
 ):
-    bf16, f32 = jnp.bfloat16, jnp.float32
     tok_dev = context.shape[0]
     slot_dev = memory.shape[0]
-    seq_size = lax.axis_size("seq")
     here = coords(PLAIN)
     paired_index = here["y"] * 16 + here["z"] * 4 + here["h"] * 2 + here["c"]
-    section_extent = lax.axis_size("section")
-    section_index = lax.axis_index("section")
-    kv_weight, down, query_sum, output_weight = opening(
-        jnp.concatenate([key_weight, value_weight], axis=1),
-        value_down_map,
-        memory,
-        query_weight,
-        output_weight,
-        1,
+    docs = jnp.concatenate([document_slots, (paired_index * slot_dev).reshape(1).astype(jnp.int32)])
+    kv, queries, query_low, value_low, output_weight, normed_gradient, decoder_gain = front(
+        key_weight, value_weight, value_down_map, context, memory, query_weight, query_down_map,
+        query_up_map, value_up_map, output_weight, normed_gradient, decoder_gain.reshape(-1, 128), 1,
     )
-    query_low = jnp.dot(memory, query_down_map, preferred_element_type=f32).astype(bf16)
-    row_parts = (context, memory)
-    value_low = jnp.concatenate(
-        [jnp.dot(part, down, preferred_element_type=f32).astype(bf16) for part in row_parts], axis=0
+    attended, ot, top, mass = attend(docs, queries, kv, tok_dev)
+    d_attended, normed = middle(
+        attended, output_weight, normed_gradient, decoder_gain.reshape(1, -1),
+        slot_dev * lax.axis_size("seq"), 2,
     )
-    projected = jnp.concatenate(
-        [jnp.dot(part, kv_weight, preferred_element_type=f32) for part in row_parts], axis=0
+    d_queries, dv_part = attend_backward(docs, queries, d_attended, kv, ot, top, mass, tok_dev)
+    grad_qa, grad_va, query_up_gradient, value_up_gradient = tail(
+        dv_part, d_queries, query_low, value_low, query_up_map, value_up_map, memory, context, 3
     )
-    queries = (
-        query_sum + adapter_scale * jnp.dot(query_low, query_up_map, preferred_element_type=f32)
-    ).astype(bf16)
-    keys = projected[:, :HD].astype(bf16)
-    values = (
-        projected[:, HD : 2 * HD]
-        + adapter_scale * jnp.dot(value_low, value_up_map, preferred_element_type=f32)
-    ).astype(bf16)
-    kv, queries_here, normed_gradient, decoder_gain = gather_keys(
-        jnp.concatenate([keys, values], axis=1),
-        queries,
-        normed_gradient,
-        decoder_gain.reshape(-1, 128),
-        2,
-    )
-    decoder_gain = decoder_gain.reshape(1, -1)
-    span, rows, bounds = row_bounds(document_slots, paired_index * slot_dev, slot_dev, seq_size)
-    attended, ot, top, mass = attend(span, rows, bounds, queries_here, kv, tok_dev)
-    total_slots = slot_dev * seq_size
-    d_attended, normed = middle(
-        attended, output_weight, normed_gradient, decoder_gain, total_slots, 3
-    )
-    d_queries, dv_part = attend_backward(
-        span, rows, bounds, queries_here, d_attended, kv, ot, top, mass, tok_dev
-    )
-    d_values, d_queries = scatter_values(dv_part, d_queries, 8)
-    query_up_part = adapter_scale * contract(query_low, d_queries, 0, 0)
-    value_up_part = adapter_scale * contract(value_low, d_values, 0, 0)
-    query_part = adapter_scale * contract(d_queries, query_up_map, 1, 1)
-    value_part = adapter_scale * contract(d_values, value_up_map, 1, 1)
-    backs = jnp.sum(
-        exchange(
-            jnp.concatenate([query_part, value_part], axis=0).astype(bf16),
-            "section", False, 9, "sum_backs",
-        ).astype(f32),
-        axis=0,
-    ).astype(bf16)
-    width = memory.shape[1] // section_extent
-    memory_cols = lax.dynamic_slice_in_dim(memory, section_index * width, width, 1)
-    context_cols = lax.dynamic_slice_in_dim(context, section_index * width, width, 1)
-    memory_backs = jnp.concatenate([backs[:slot_dev], backs[slot_dev + tok_dev :]], axis=1)
-    memory_down = contract(memory_cols, memory_backs, 0, 0)
-    down_parts = [
-        memory_down[:, :HD],
-        memory_down[:, HD:] + contract(context_cols, backs[slot_dev : slot_dev + tok_dev], 0, 0),
-    ]
-    ups = jnp.concatenate([query_up_part, value_up_part], axis=1)
-    lanes = ups.shape[1] // 128
-    ups = jnp.moveaxis(ups.reshape(128, lanes, 128), 1, 0).reshape(seq_size, -1, 128)
-    up_rows = ups.shape[1]
-    down_rows = MODEL_DIM // section_extent // seq_size
-    final, ups = scatter_final(
-        jnp.concatenate([part.reshape(seq_size, -1, 128).astype(bf16) for part in down_parts], axis=1),
-        jnp.pad(ups.astype(bf16), ((0, 0), (0, -up_rows % 16), (0, 0))),
-        10,
-    )
-    grad_qa, grad_va = final[:down_rows], final[down_rows:]
-    ups = ups[:, :up_rows]
-    ups = jnp.moveaxis(ups.reshape(lanes, 128, 128), 0, 1).reshape(128, lanes * 128)
-    split = query_up_part.shape[1]
-    return (normed, grad_qa, grad_va, ups[:, :split], ups[:, split:])
+    return (normed, grad_qa, grad_va, query_up_gradient, value_up_gradient)
 
 
 def solution(mesh):

time: 298 us -> 251 us (0.84)
  local copies, waits for them, and re-layouts: 27.6 us -> 6.79 us
  matrix products: 17.5 us -> 0 us
  other arithmetic: 5.97 us -> 0.73 us
  between operations: 4.48 us -> 0.89 us
    dot_general x13 -> x0, matrix products: 17.5 us -> none  [the longest x2 8.1 us: body(): jnp.dot(part, kv_weight, preferred_element_type=f32)]
    unnamed x81 -> x29, local copies, waits for them, and re-layouts: 15.8 us -> 6.79 us
    convert_element_type x3 -> x0, local copies, waits for them, and re-layouts: 4.49 us -> none  [the longest x2 3.58 us: body(): ups.astype(bf16)]
    pallas_call x5 -> x2, Pallas kernels: 140 us -> 139 us  [the longest x1 78.3 us: front(): pl.pallas_call(functools.partial(front_kernel, pieces, half_pieces, kv_pi...]
where the time goes in v4:
time: 251 us
  Pallas kernels  242 us (96%)
  local copies, waits for them, and re-layouts  6.79 us (3%)
    pallas_call x1, Pallas kernels, middle(): pl.pallas_call(functools.partial(middle_kernel, pieces, scatter_pieces, t...  96.5 us
    pallas_call x1, Pallas kernels, front(): pl.pallas_call(functools.partial(front_kernel, pieces, half_pieces, kv_pi...  78.3 us
    pallas_call x1, Pallas kernels, tail(): pl.pallas_call(functools.partial(tail_kernel, dv_pieces, pieces, up_piece...  60.6 us
    unnamed x29, local copies, waits for them, and re-layouts  6.79 us

profile of v4, /device:TPU:0, one launch (start us, length us, event | category | flops | bytes accessed | tf_op | source)
XLA Modules:
  0.0 250.7 jit_solution(12706638701758749103)
XLA Ops:
  0.7 0.7 pad_add_fusion.docs_ref
  1.4 78.3 %front.1 = (bf16[2,4,2,2,320,256]{5,4,3,2,1,0:T(8,128)(2,1)}, bf16[64,1024]{1,0:T(8,128)(2,1)}, bf16[64,128]{1,0:T(8,128)(2,1)}, bf16[320,128]{1,0:T(8,128)(2,1)...) custom-call(bf16[256,128]{1,0:T(8,128)(2,1)} %key_ref.1, bf16[256,128]{1,0:T(8,128)(2,1)} %value_ref.1, ...), custom_call_target="tpu_custom_call" | custom-call | tf_op jit(solution)/shard_map/front/pallas_call | solution.py:330
  79.8 0.0 copy-start.11
  79.8 0.0 copy-start
  79.8 2.5 copy-done
  82.2 0.0 copy-start.4
  82.3 0.9 copy-done.4
  83.2 2.3 attend.1
  85.4 0.0 copy-start.1
  85.5 0.0 copy-start.2
  85.5 0.0 copy-start.3
  85.5 0.0 copy-start.8
  85.5 0.0 copy-start.9
  85.5 0.0 copy-start.10
  85.5 0.0 copy-done.11
  85.5 0.0 copy-done.6
  85.5 0.0 copy-done.7
  85.5 96.5 %middle.1 = (bf16[64,1024]{1,0:T(8,128)(2,1)S(1)}, bf16[512,256]{1,0:T(8,128)(2,1)S(1)}) custom-call(bf16[64,1024]{1,0:T(8,128)(2,1)S(1)} %get-tuple-element.26.x_ref, bf16[1024,256]{1,0:T(8,128)(2,1)S(1)} %copy-done.6, bf16[512,256]{1,0:T(8,128)(2,1)S(1)} %copy-done.7, f32[1,256]{1,0:T(1,128)S(1)} %bitcast.8), custom_call_target="tpu_custom_call" | custom-call | tf_op jit(solution)/shard_map/middle/pallas_call | solution.py:768
  182.0 0.0 copy-done.5
  182.0 4.6 %attend_backward.1 = (bf16[64,1024]{1,0:T(8,128)(2,1)S(1)}, bf16[32,320,128]{2,1,0:T(8,128)(2,1)S(1)}) custom-call(s32[9]{0:T(128)S(1)} %pad_add_fusion.docs_ref, bf16[64,1024]{1,0:T(8,128)(2,1)S(1)} %copy-done.5, bf16[64,1024]{1,0:T(8,128)(2,1)S(1)} %get-tuple-element.31.g_ref, bf16[32,320,256]{2,1,0:T(8,128)(2,1)} %bitcast.5, ...), custom_call_target="tpu_custom_call" | custom-call | tf_op jit(solution)/shard_map/attend_backward/pallas_call | solution.py:1001
  186.7 0.0 copy-done.1
  186.7 0.0 copy-done.2
  186.7 0.0 copy-done.3
  186.7 0.0 copy-done.8
  186.7 0.0 copy-done.9
  186.7 0.0 copy-done.10
  186.7 60.6 %tail.1 = (f32[64,128]{1,0:T(8,128)S(1)}, f32[64,128]{1,0:T(8,128)S(1)}, f32[128,1024]{1,0:T(8,128)S(1)}, f32[128,128]{1,0:T(8,128)S(1)}) custom-call(bf16[2,4,2,2,320,128]{5,4,3,2,1,0:T(8,128)(2,1)S(1)} %bitcast.7, bf16[64,1024]{1,0:T(8,128)(2,1)S(1)} %get-tuple-element.36.dq_ref, bf16[64,128]{1,0:T(8,128)(2,1)S(1)} %copy-done.10, ...), custom_call_target="tpu_custom_call" | custom-call | tf_op jit(solution)/shard_map/tail/pallas_call | solution.py:616
  247.3 0.7 copy.23
  248.0 0.6 copy.24
  248.6 0.6 copy.25
  249.3 0.8 copy.26
  250.0 0.6 copy.27
  (3 shorter events, 0.0 us)
Async XLA Ops:
  79.8 5.8 %copy-start.11 = (f32[2,128]{1,0:T(2,128)S(1)}, f32[2,128]{1,0:T(2,128)}, u32[]{:S(2)}) copy-start(f32[2,128]{1,0:T(2,128)} %get-tuple-element.29) | copy-start | bytes 3076
  79.8 2.5 copy-start
  82.2 0.9 copy-start.4
  83.2 2.4 copy-start.6
  83.2 2.4 copy-start.7
  83.2 98.9 %copy-start.5 = (bf16[64,1024]{1,0:T(8,128)(2,1)S(1)}, bf16[64,1024]{1,0:T(8,128)(2,1)}, u32[]{:S(2)}) copy-start(bf16[64,1024]{1,0:T(8,128)(2,1)} %get-tuple-element.24.q_ref) | copy-start | bytes 393220
  85.4 101.2 %copy-start.1 = (bf16[256,8192]{1,0:T(8,128)(2,1)S(1)}, bf16[256,8192]{1,0:T(8,128)(2,1)}, u32[]{:S(2)}) copy-start(bf16[256,8192]{1,0:T(8,128)(2,1)} %context_ref.3) | copy-start | bytes 12582916
  85.5 101.2 %copy-start.2 = (bf16[64,8192]{1,0:T(8,128)(2,1)S(1)}, bf16[64,8192]{1,0:T(8,128)(2,1)}, u32[]{:S(2)}) copy-start(bf16[64,8192]{1,0:T(8,128)(2,1)} %memory_ref.3) | copy-start | bytes 3145732
  85.5 101.2 %copy-start.3 = (bf16[128,1024]{1,0:T(8,128)(2,1)S(1)}, bf16[128,1024]{1,0:T(8,128)(2,1)}, u32[]{:S(2)}) copy-start(bf16[128,1024]{1,0:T(8,128)(2,1)} %query_up_ref.3) | copy-start | bytes 786436
  85.5 101.2 %copy-start.8 = (bf16[128,128]{1,0:T(8,128)(2,1)S(1)}, bf16[128,128]{1,0:T(8,128)(2,1)}, u32[]{:S(2)}) copy-start(bf16[128,128]{1,0:T(8,128)(2,1)} %value_up_ref.3) | copy-start | bytes 98308
  85.5 101.2 %copy-start.9 = (bf16[320,128]{1,0:T(8,128)(2,1)S(1)}, bf16[320,128]{1,0:T(8,128)(2,1)}, u32[]{:S(2)}) copy-start(bf16[320,128]{1,0:T(8,128)(2,1)} %get-tuple-element.38.value_low) | copy-start | bytes 245764
  85.5 101.2 %copy-start.10 = (bf16[64,128]{1,0:T(8,128)(2,1)S(1)}, bf16[64,128]{1,0:T(8,128)(2,1)}, u32[]{:S(2)}) copy-start(bf16[64,128]{1,0:T(8,128)(2,1)} %get-tuple-element.37.query_low) | copy-start | bytes 49156

commit v5 on v4

--- a/solution.py
+++ b/solution.py
@@ -264,7 +264,6 @@
     def between(phase):
         if phase < 2:
             return
-        swaps[4].start()
         fetches[2].wait()
         fetches[3].wait()
         low = jnp.dot(memory[...], query_down[...], preferred_element_type=f32).astype(bf16)
@@ -281,6 +280,7 @@
         fetches[4].wait()
 
     run_gathers([plain, shared], owns, between)
+    swaps[4].start()
     wide = 4 * shard.shape[0]
     for j in range(8):
         at = (j // 4, j % 4)
@@ -321,7 +321,7 @@
     tok, slots, model = context.shape[0], memory.shape[0], memory.shape[1]
     keys, wide = tok + slots, query_weight.shape[1]
     pieces = cut(rows, 2 * HD, ORDERS[PLAIN])
-    half_pieces = cut(half, HD, ORDERS[PLAIN])
+    half_pieces = cut(half, HD, ORDERS[PLAIN][:3])
     kv_pieces = cut(keys, 2 * HD, ORDERS[PAIRED])
     n = 9 * len(pieces) + 1 + 9 * len(half_pieces) + 1
     like = lambda a: jax.ShapeDtypeStruct(a.shape, a.dtype)
@@ -877,36 +877,56 @@
     return span, row_slot, (low_lane, high_lane), fill
 
 
-def group_scores(keys, g, q_wide, row_slot, bounds, context_rows, slots, causal):
-    docs = key_docs(g, bounds, context_rows, slots)
+HALVES = (slice(0, ROWS // 2), slice(ROWS // 2, ROWS))
+
+
+def group_scores(keys, docs, g, q_wide, row_slot, context_rows, slots, causal):
     scores = contract(jnp.concatenate([keys, docs], axis=1), q_wide, 1, 1)
     if not causal:
         return scores
     edge = GROUP * context_rows
-    slot = g * (GROUP * slots) + lax.broadcasted_iota(jnp.int32, (GROUP * slots, ROWS), 0)
+    slot = g * (GROUP * slots) + lax.broadcasted_iota(
+        jnp.int32, (GROUP * slots, q_wide.shape[0]), 0
+    )
     return jnp.concatenate(
         [scores[:edge], jnp.where(slot <= row_slot[0:1, :], scores[edge:], mask_fill)], axis=0
     )
 
 
-def over_groups(span, step):
+def group_copy(kv_hbm, kv_ref, sems, g):
+    return pltpu.make_async_copy(
+        kv_hbm.at[pl.ds(g * GROUP, GROUP)], kv_ref.at[pl.ds(g * GROUP, GROUP)], sems.at[g]
+    )
+
+
+def over_groups(span, step, fetch):
     first, own, last = span[0], span[1], span[2]
 
+    def ask(g, carry):
+        fetch(g).start()
+        return carry
+
     def before(g, carry):
+        fetch(g).wait()
         step(g, False, True)
         return carry
 
     def after(g, carry):
+        fetch(g).wait()
         step(g, False, False)
         return carry
 
+    fetch(own).start()
+    lax.fori_loop(first, own, ask, 0)
+    lax.fori_loop(own + 1, last, ask, 0)
+    fetch(own).wait()
     step(own, True, True)
     lax.fori_loop(first, own, before, 0)
     lax.fori_loop(own + 1, last, after, 0)
 
 
 def attend_kernel(
-    context_rows, docs_ref, q_ref, kv_ref, o_ref, ot_ref, top_ref, mass_ref
+    context_rows, docs_ref, q_ref, kv_hbm, o_ref, ot_ref, top_ref, mass_ref, kv_ref, sems
 ):
     slots = kv_ref.shape[1] - context_rows
     span, row_slot, bounds, fill = place_rows(docs_ref, q_ref.shape[0])
@@ -918,17 +938,21 @@
     def step(g, masked, with_memory):
         extra = slots if with_memory else 0
         keys = key_block(kv_ref, g, slice(0, HD), context_rows, extra)
-        scores = group_scores(keys, g, q, row_slot, bounds, context_rows, extra, masked)
-        before = top_ref[0:1, :]
-        top = jnp.maximum(before, jnp.max(scores, axis=0, keepdims=True))
-        keep = jnp.exp2((before - top) * exp2_scale)
-        weight = jnp.exp2((scores - top) * exp2_scale)
-        top_ref[0:1, :] = top
-        mass_ref[0:1, :] = mass_ref[0:1, :] * keep + jnp.sum(weight, axis=0, keepdims=True)
         values = key_block(kv_ref, g, slice(HD, 2 * HD), context_rows, extra)
-        ot_ref[...] = ot_ref[...] * keep + contract(values, weight.astype(jnp.bfloat16), 0, 0)
-
-    over_groups(span, step)
+        docs = key_docs(g, bounds, context_rows, extra)
+        for cols in (slice(0, ROWS),):
+            scores = group_scores(keys, docs, g, q[cols], row_slot[:, cols], context_rows, extra, masked)
+            before = top_ref[0:1, cols]
+            top = jnp.maximum(before, jnp.max(scores, axis=0, keepdims=True))
+            keep = jnp.exp2((before - top) * exp2_scale)
+            weight = jnp.exp2((scores - top) * exp2_scale)
+            top_ref[0:1, cols] = top
+            mass_ref[0:1, cols] = mass_ref[0:1, cols] * keep + jnp.sum(weight, axis=0, keepdims=True)
+            ot_ref[:, cols] = ot_ref[:, cols] * keep + contract(
+                values, weight.astype(jnp.bfloat16), 0, 0
+            )
+
+    over_groups(span, step, functools.partial(group_copy, kv_hbm, kv_ref, sems))
     ot_ref[...] = ot_ref[...] / mass_ref[0:1, :]
     rows = jnp.transpose(ot_ref[...]).astype(jnp.bfloat16)
     here = q_ref.shape[0]
@@ -937,8 +961,8 @@
 
 
 def backward_kernel(
-    context_rows, docs_ref, q_ref, g_ref, kv_ref, ot_ref, top_ref, mass_ref,
-    dq_ref, dv_ref, acc,
+    context_rows, docs_ref, q_ref, g_ref, kv_hbm, ot_ref, top_ref, mass_ref,
+    dq_ref, dv_ref, acc, kv_ref, sems,
 ):
     slots = kv_ref.shape[1] - context_rows
     edge = GROUP * context_rows
@@ -954,12 +978,17 @@
     def step(g, masked, with_memory):
         extra = slots if with_memory else 0
         keys = key_block(kv_ref, g, slice(0, HD), context_rows, extra)
-        scores = group_scores(keys, g, q, row_slot, bounds, context_rows, extra, masked)
-        probs = jnp.exp2((scores - top) * exp2_scale) * share
         values = key_block(kv_ref, g, slice(HD, 2 * HD), context_rows, extra)
-        d_probs = contract(values, grad, 1, 1)
-        d_scores = (probs * (d_probs - center)).astype(jnp.bfloat16)
-        d_values = contract(probs.astype(jnp.bfloat16), grad, 1, 0).astype(jnp.bfloat16)
+        docs = key_docs(g, bounds, context_rows, extra)
+        d_values = 0.0
+        for cols in HALVES:
+            scores = group_scores(keys, docs, g, q[cols], row_slot[:, cols], context_rows, extra, masked)
+            probs = jnp.exp2((scores - top[:, cols]) * exp2_scale) * share[:, cols]
+            d_probs = contract(values, grad[cols], 1, 1)
+            d_scores = (probs * (d_probs - center[:, cols])).astype(jnp.bfloat16)
+            d_values = d_values + contract(probs.astype(jnp.bfloat16), grad[cols], 1, 0)
+            acc[:, cols] += contract(keys, d_scores, 0, 0)
+        d_values = d_values.astype(jnp.bfloat16)
         dv_ref[pl.ds(g * GROUP, GROUP), :context_rows, :] = d_values[:edge].reshape(
             GROUP, context_rows, HD
         )
@@ -967,9 +996,8 @@
             dv_ref[pl.ds(g * GROUP, GROUP), context_rows:, :] = d_values[edge:].reshape(
                 GROUP, slots, HD
             )
-        acc[...] += contract(keys, d_scores, 0, 0)
-
-    over_groups(span, step)
+
+    over_groups(span, step, functools.partial(group_copy, kv_hbm, kv_ref, sems))
     rows = jnp.transpose(acc[...] * score_scale).astype(jnp.bfloat16)
     here = q_ref.shape[0]
     for h in range(HEADS_HERE):
@@ -977,7 +1005,7 @@
 
 
 SMEM = pl.BlockSpec(memory_space=pltpu.SMEM)
-BIG = pltpu.CompilerParams(vmem_limit_bytes=48 << 20)
+BIG = pltpu.CompilerParams(vmem_limit_bytes=61 << 20)
 
 
 def attend(docs, q, kv, context_rows):
@@ -990,8 +1018,9 @@
             jax.ShapeDtypeStruct((8, ROWS), f32),
             jax.ShapeDtypeStruct((8, ROWS), f32),
         ),
-        in_specs=[SMEM] + [VMEM] * 2,
+        in_specs=[SMEM, VMEM, HBM],
         out_specs=(VMEM, VMEM, VMEM, VMEM),
+        scratch_shapes=[pltpu.VMEM(kv.shape, kv.dtype), pltpu.SemaphoreType.DMA((kv.shape[0] // GROUP,))],
         compiler_params=BIG,
         name="attend",
     )(docs, q, kv)
@@ -1004,9 +1033,13 @@
             jax.ShapeDtypeStruct(q.shape, jnp.bfloat16),
             jax.ShapeDtypeStruct((*kv.shape[:2], HD), jnp.bfloat16),
         ),
-        in_specs=[SMEM] + [VMEM] * 6,
+        in_specs=[SMEM, VMEM, VMEM, HBM, VMEM, VMEM, VMEM],
         out_specs=(VMEM, VMEM),
-        scratch_shapes=[pltpu.VMEM((HD, ROWS), jnp.float32)],
+        scratch_shapes=[
+            pltpu.VMEM((HD, ROWS), jnp.float32),
+            pltpu.VMEM(kv.shape, kv.dtype),
+            pltpu.SemaphoreType.DMA((kv.shape[0] // GROUP,)),
+        ],
         compiler_params=BIG,
         name="attend_backward",
     )(docs, q, grad, kv, ot, top, mass)

time: 251 us -> 261 us (1.040)
  Pallas kernels: 242 us -> 249 us
  local copies, waits for them, and re-layouts: 6.79 us -> 9.86 us
    pallas_call x1, Pallas kernels: 60.6 us -> 65.4 us  [tail(): pl.pallas_call(functools.partial(tail_kernel, dv_pieces, pieces, up_piece...]
    unnamed x29 -> x31, local copies, waits for them, and re-layouts: 6.79 us -> 9.86 us
where the time goes in v5:
time: 261 us
  Pallas kernels  249 us (95%)
  local copies, waits for them, and re-layouts  9.86 us (4%)
    pallas_call x1, Pallas kernels, middle(): pl.pallas_call(functools.partial(middle_kernel, pieces, scatter_pieces, t...  97.5 us
    pallas_call x1, Pallas kernels, front(): pl.pallas_call(functools.partial(front_kernel, pieces, half_pieces, kv_pi...  77.2 us
    pallas_call x1, Pallas kernels, tail(): pl.pallas_call(functools.partial(tail_kernel, dv_pieces, pieces, up_piece...  65.4 us
    unnamed x31, local copies, waits for them, and re-layouts  9.86 us

profile of v5, /device:TPU:0, one launch (start us, length us, event | category | flops | bytes accessed | tf_op | source)
XLA Modules:
  0.0 260.7 jit_solution(1693171830091093478)
XLA Ops:
  0.7 1.2 pad_add_fusion.docs_ref
  1.9 77.2 %front.1 = (bf16[2,4,2,2,320,256]{5,4,3,2,1,0:T(8,128)(2,1)}, bf16[64,1024]{1,0:T(8,128)(2,1)}, bf16[64,128]{1,0:T(8,128)(2,1)}, bf16[320,128]{1,0:T(8,128)(2,1)...) custom-call(bf16[256,128]{1,0:T(8,128)(2,1)} %key_ref.1, bf16[256,128]{1,0:T(8,128)(2,1)} %value_ref.1, ...), custom_call_target="tpu_custom_call" | custom-call | tf_op jit(solution)/shard_map/front/pallas_call | solution.py:330
  79.2 0.0 copy-start.4
  79.2 0.0 copy-start.5
  79.2 0.0 copy-start.12
  79.2 0.0 copy-start.10
  79.2 0.0 copy-start.11
  79.2 3.8 %attend.1 = (bf16[64,1024]{1,0:T(8,128)(2,1)}, f32[128,512]{1,0:T(8,128)}, f32[8,512]{1,0:T(8,128)}, f32[8,512]{1,0:T(8,128)}) custom-call(s32[9]{0:T(128)} %pad_add_fusion.docs_ref, bf16[64,1024]{1,0:T(8,128)(2,1)} %get-tuple-element.24.q_ref, bf16[32,320,256]{2,1,0:T(8,128)(2,1)} %bitcast.7), custom_call_target="tpu_custom_call" | custom-call | tf_op jit(solution)/shard_map/attend/pallas_call | solution.py:1013
  83.0 0.0 copy-start.1
  83.0 0.0 copy-start.3
  83.0 0.0 copy-start.7
  83.1 0.0 copy-done.4
  83.1 0.0 copy-done.5
  83.1 0.0 copy-done.12
  83.1 0.0 copy-start.9
  83.1 1.0 copy-done.9
  84.1 97.5 %middle.1 = (bf16[64,1024]{1,0:T(8,128)(2,1)S(1)}, bf16[512,256]{1,0:T(8,128)(2,1)S(1)}) custom-call(bf16[64,1024]{1,0:T(8,128)(2,1)S(1)} %copy-done.9, bf16[1024,256]{1,0:T(8,128)(2,1)S(1)} %copy-done.4, bf16[512,256]{1,0:T(8,128)(2,1)S(1)} %copy-done.5, f32[1,256]{1,0:T(1,128)S(1)} %bitcast.6), custom_call_target="tpu_custom_call" | custom-call | tf_op jit(solution)/shard_map/middle/pallas_call | solution.py:768
  181.6 0.0 copy-start.8
  181.7 0.6 copy-done.8
  182.3 4.8 %attend_backward.1 = (bf16[64,1024]{1,0:T(8,128)(2,1)}, bf16[32,320,128]{2,1,0:T(8,128)(2,1)}) custom-call(s32[9]{0:T(128)} %pad_add_fusion.docs_ref, bf16[64,1024]{1,0:T(8,128)(2,1)} %get-tuple-element.24.q_ref, bf16[64,1024]{1,0:T(8,128)(2,1)} %copy-done.8, bf16[32,320,256]{2,1,0:T(8,128)(2,1)} %bitcast.8, f32[128,512]{1,0:T(8,128)} %get-tuple-element.32.ot_ref, ...), custom_call_target="tpu_custom_call" | custom-call | tf_op jit(solution)/shard_map/attend_backward/pallas_call | solution.py:1030
  187.1 0.0 copy-done.10
  187.1 0.0 copy-done.11
  187.2 0.0 copy-start
  187.2 2.2 copy-done
  189.3 1.7 copy-done.2
  191.1 0.9 copy-done.6
  192.0 65.4 %tail.1 = (f32[64,128]{1,0:T(8,128)S(1)}, f32[64,128]{1,0:T(8,128)S(1)}, f32[128,1024]{1,0:T(8,128)S(1)}, f32[128,128]{1,0:T(8,128)S(1)}) custom-call(bf16[2,4,2,2,320,128]{5,4,3,2,1,0:T(8,128)(2,1)S(1)} %bitcast.5, bf16[64,1024]{1,0:T(8,128)(2,1)S(1)} %copy-done.6, bf16[64,128]{1,0:T(8,128)(2,1)S(1)} %copy-done.11, bf16[320,128]{1,0:T(8,128)(2,1)S(1)} %copy-done.10, ...), custom_call_target="tpu_custom_call" | custom-call | tf_op jit(solution)/shard_map/tail/pallas_call | solution.py:616
  257.4 0.7 copy.23
  258.1 0.6 copy.24
  258.7 0.6 copy.25
  259.3 0.8 copy.26
  260.1 0.6 copy.27
  (5 shorter events, 0.0 us)
Async XLA Ops:
  79.2 3.9 %copy-start.4 = (bf16[1024,256]{1,0:T(8,128)(2,1)S(1)}, bf16[1024,256]{1,0:T(8,128)(2,1)}, u32[]{:S(2)}) copy-start(bf16[1024,256]{1,0:T(8,128)(2,1)} %get-tuple-element.27.wo_ref) | copy-start | bytes 1572868
  79.2 3.9 %copy-start.5 = (bf16[512,256]{1,0:T(8,128)(2,1)S(1)}, bf16[512,256]{1,0:T(8,128)(2,1)}, u32[]{:S(2)}) copy-start(bf16[512,256]{1,0:T(8,128)(2,1)} %get-tuple-element.28.ng_ref) | copy-start | bytes 786436
  79.2 3.9 %copy-start.12 = (f32[2,128]{1,0:T(2,128)S(1)}, f32[2,128]{1,0:T(2,128)}, u32[]{:S(2)}) copy-start(f32[2,128]{1,0:T(2,128)} %get-tuple-element.29) | copy-start | bytes 3076
  79.2 107.9 %copy-start.10 = (bf16[320,128]{1,0:T(8,128)(2,1)S(1)}, bf16[320,128]{1,0:T(8,128)(2,1)}, u32[]{:S(2)}) copy-start(bf16[320,128]{1,0:T(8,128)(2,1)} %get-tuple-element.38.value_low) | copy-start | bytes 245764
  79.2 107.9 %copy-start.11 = (bf16[64,128]{1,0:T(8,128)(2,1)S(1)}, bf16[64,128]{1,0:T(8,128)(2,1)}, u32[]{:S(2)}) copy-start(bf16[64,128]{1,0:T(8,128)(2,1)} %get-tuple-element.37.query_low) | copy-start | bytes 49156
  83.0 104.1 %copy-start.1 = (bf16[64,8192]{1,0:T(8,128)(2,1)S(1)}, bf16[64,8192]{1,0:T(8,128)(2,1)}, u32[]{:S(2)}) copy-start(bf16[64,8192]{1,0:T(8,128)(2,1)} %memory_ref.3) | copy-start | bytes 3145732
  83.0 104.1 %copy-start.3 = (bf16[128,1024]{1,0:T(8,128)(2,1)S(1)}, bf16[128,1024]{1,0:T(8,128)(2,1)}, u32[]{:S(2)}) copy-start(bf16[128,1024]{1,0:T(8,128)(2,1)} %query_up_ref.3) | copy-start | bytes 786436
  83.0 104.1 %copy-start.7 = (bf16[128,128]{1,0:T(8,128)(2,1)S(1)}, bf16[128,128]{1,0:T(8,128)(2,1)}, u32[]{:S(2)}) copy-start(bf16[128,128]{1,0:T(8,128)(2,1)} %value_up_ref.3) | copy-start | bytes 98308
  83.1 1.0 copy-start.9
  181.6 0.7 copy-start.8
  187.2 2.2 copy-start
  189.3 1.7 copy-start.2
  191.1 0.9 copy-start.6

commit v6 on v5

--- a/solution.py
+++ b/solution.py
@@ -1005,7 +1005,7 @@
 
 
 SMEM = pl.BlockSpec(memory_space=pltpu.SMEM)
-BIG = pltpu.CompilerParams(vmem_limit_bytes=61 << 20)
+BIG = pltpu.CompilerParams(vmem_limit_bytes=48 << 20)
 
 
 def attend(docs, q, kv, context_rows):
@@ -1021,7 +1021,7 @@
         in_specs=[SMEM, VMEM, HBM],
         out_specs=(VMEM, VMEM, VMEM, VMEM),
         scratch_shapes=[pltpu.VMEM(kv.shape, kv.dtype), pltpu.SemaphoreType.DMA((kv.shape[0] // GROUP,))],
-        compiler_params=BIG,
+        compiler_params=pltpu.CompilerParams(vmem_limit_bytes=61 << 20),
         name="attend",
     )(docs, q, kv)
 

time: 261 us -> 253 us (0.969)
  Pallas kernels: 249 us -> 244 us
  local copies, waits for them, and re-layouts: 9.86 us -> 6.84 us
    unnamed x31 -> x35, local copies, waits for them, and re-layouts: 9.86 us -> 6.84 us
where the time goes in v6:
time: 253 us; the launch traced here: 254 us
  Pallas kernels  244 us (96%)
  local copies, waits for them, and re-layouts  6.84 us (3%)
    pallas_call x1, Pallas kernels, middle(): pl.pallas_call(functools.partial(middle_kernel, pieces, scatter_pieces, t...  97 us
    pallas_call x1, Pallas kernels, front(): pl.pallas_call(functools.partial(front_kernel, pieces, half_pieces, kv_pi...  77.2 us
    pallas_call x1, Pallas kernels, tail(): pl.pallas_call(functools.partial(tail_kernel, dv_pieces, pieces, up_piece...  63.6 us
    unnamed x35, local copies, waits for them, and re-layouts  6.84 us

profile of v6, /device:TPU:0, one launch (start us, length us, event | category | flops | bytes accessed | tf_op | source)
XLA Modules:
  0.0 253.5 jit_solution(5940362675187871144)
XLA Ops:
  0.7 1.2 pad_add_fusion.docs_ref
  1.9 77.2 %front.1 = (bf16[2,4,2,2,320,256]{5,4,3,2,1,0:T(8,128)(2,1)}, bf16[64,1024]{1,0:T(8,128)(2,1)}, bf16[64,128]{1,0:T(8,128)(2,1)}, bf16[320,128]{1,0:T(8,128)(2,1)...) custom-call(bf16[256,128]{1,0:T(8,128)(2,1)} %key_ref.1, bf16[256,128]{1,0:T(8,128)(2,1)} %value_ref.1, ...), custom_call_target="tpu_custom_call" | custom-call | tf_op jit(solution)/shard_map/front/pallas_call | solution.py:330
  79.2 0.0 copy-start.13
  79.2 0.0 copy-start.7
  79.2 0.0 copy-start.9
  79.2 0.0 copy-start.10
  79.3 3.8 %attend.1 = (bf16[64,1024]{1,0:T(8,128)(2,1)}, f32[128,512]{1,0:T(8,128)}, f32[8,512]{1,0:T(8,128)}, f32[8,512]{1,0:T(8,128)}) custom-call(s32[9]{0:T(128)} %pad_add_fusion.docs_ref, bf16[64,1024]{1,0:T(8,128)(2,1)} %get-tuple-element.24.q_ref, bf16[32,320,256]{2,1,0:T(8,128)(2,1)} %bitcast.7), custom_call_target="tpu_custom_call" | custom-call | tf_op jit(solution)/shard_map/attend/pallas_call | solution.py:1013
  83.1 0.0 copy-start
  83.1 0.0 copy-start.1
  83.1 0.0 copy-start.2
  83.1 0.0 copy-start.8
  83.1 1.0 copy-done.8
  84.2 97.0 %middle.1 = (bf16[64,1024]{1,0:T(8,128)(2,1)S(1)}, bf16[512,256]{1,0:T(8,128)(2,1)S(1)}) custom-call(bf16[64,1024]{1,0:T(8,128)(2,1)S(1)} %copy-done.8, bf16[1024,256]{1,0:T(8,128)(2,1)S(1)} %copy-done.4, bf16[512,256]{1,0:T(8,128)(2,1)S(1)} %copy-done.6, f32[1,256]{1,0:T(1,128)S(1)} %bitcast.6), custom_call_target="tpu_custom_call" | custom-call | tf_op jit(solution)/shard_map/middle/pallas_call | solution.py:768
  181.2 0.0 copy-done.3
  181.2 0.0 copy-done.13
  181.2 0.0 copy-start.5
  181.2 0.9 copy-done.5
  182.2 0.7 copy-done.11
  182.9 0.7 copy-done.12
  183.6 2.8 %attend_backward.1 = (bf16[64,1024]{1,0:T(8,128)(2,1)S(1)}, bf16[32,320,128]{2,1,0:T(8,128)(2,1)S(1)}) custom-call(s32[9]{0:T(128)S(1)} %copy-done.13, bf16[64,1024]{1,0:T(8,128)(2,1)S(1)} %copy-done.3, bf16[64,1024]{1,0:T(8,128)(2,1)S(1)} %get-tuple-element.31.g_ref, bf16[32,320,256]{2,1,0:T(8,128)(2,1)} %bitcast.8, f32[128,512]{1,0:T(8,128)S(1)} %copy-done.5, ...), custom_call_target="tpu_custom_call" | custom-call | tf_op jit(solution)/shard_map/attend_backward/pallas_call | solution.py:1030
  186.5 0.0 copy-done.7
  186.5 0.0 copy-done.9
  186.5 0.0 copy-done.10
  186.5 0.0 copy-done
  186.5 0.0 copy-done.1
  186.5 0.0 copy-done.2
  186.5 63.6 %tail.1 = (f32[64,128]{1,0:T(8,128)S(1)}, f32[64,128]{1,0:T(8,128)S(1)}, f32[128,1024]{1,0:T(8,128)S(1)}, f32[128,128]{1,0:T(8,128)S(1)}) custom-call(bf16[2,4,2,2,320,128]{5,4,3,2,1,0:T(8,128)(2,1)S(1)} %bitcast.5, bf16[64,1024]{1,0:T(8,128)(2,1)S(1)} %get-tuple-element.36.dq_ref, bf16[64,128]{1,0:T(8,128)(2,1)S(1)} %copy-done.10, ...), custom_call_target="tpu_custom_call" | custom-call | tf_op jit(solution)/shard_map/tail/pallas_call | solution.py:616
  250.2 0.7 copy.23
  250.9 0.6 copy.24
  251.5 0.6 copy.25
  252.1 0.8 copy.26
  252.9 0.6 copy.27
  (9 shorter events, 0.0 us)
Async XLA Ops:
  79.2 3.9 %copy-start.4 = (bf16[1024,256]{1,0:T(8,128)(2,1)S(1)}, bf16[1024,256]{1,0:T(8,128)(2,1)}, u32[]{:S(2)}) copy-start(bf16[1024,256]{1,0:T(8,128)(2,1)} %get-tuple-element.27.wo_ref) | copy-start | bytes 1572868
  79.2 3.9 %copy-start.6 = (bf16[512,256]{1,0:T(8,128)(2,1)S(1)}, bf16[512,256]{1,0:T(8,128)(2,1)}, u32[]{:S(2)}) copy-start(bf16[512,256]{1,0:T(8,128)(2,1)} %get-tuple-element.28.ng_ref) | copy-start | bytes 786436
  79.2 3.9 %copy-start.14 = (f32[2,128]{1,0:T(2,128)S(1)}, f32[2,128]{1,0:T(2,128)}, u32[]{:S(2)}) copy-start(f32[2,128]{1,0:T(2,128)} %get-tuple-element.29) | copy-start | bytes 3076
  79.2 102.0 %copy-start.3 = (bf16[64,1024]{1,0:T(8,128)(2,1)S(1)}, bf16[64,1024]{1,0:T(8,128)(2,1)}, u32[]{:S(2)}) copy-start(bf16[64,1024]{1,0:T(8,128)(2,1)} %get-tuple-element.24.q_ref) | copy-start | bytes 393220
  79.2 102.0 %copy-start.13 = (s32[9]{0:T(128)S(1)}, s32[9]{0:T(128)}, u32[]{:S(2)}) copy-start(s32[9]{0:T(128)} %pad_add_fusion.docs_ref) | copy-start | bytes 112
  79.2 107.2 %copy-start.7 = (bf16[128,128]{1,0:T(8,128)(2,1)S(1)}, bf16[128,128]{1,0:T(8,128)(2,1)}, u32[]{:S(2)}) copy-start(bf16[128,128]{1,0:T(8,128)(2,1)} %value_up_ref.3) | copy-start | bytes 98308
  79.2 107.2 %copy-start.9 = (bf16[320,128]{1,0:T(8,128)(2,1)S(1)}, bf16[320,128]{1,0:T(8,128)(2,1)}, u32[]{:S(2)}) copy-start(bf16[320,128]{1,0:T(8,128)(2,1)} %get-tuple-element.38.value_low) | copy-start | bytes 245764
  79.2 107.2 %copy-start.10 = (bf16[64,128]{1,0:T(8,128)(2,1)S(1)}, bf16[64,128]{1,0:T(8,128)(2,1)}, u32[]{:S(2)}) copy-start(bf16[64,128]{1,0:T(8,128)(2,1)} %get-tuple-element.37.query_low) | copy-start | bytes 49156
  83.1 103.4 %copy-start = (bf16[256,8192]{1,0:T(8,128)(2,1)S(1)}, bf16[256,8192]{1,0:T(8,128)(2,1)}, u32[]{:S(2)}) copy-start(bf16[256,8192]{1,0:T(8,128)(2,1)} %context_ref.3) | copy-start | bytes 12582916
  83.1 103.4 %copy-start.1 = (bf16[64,8192]{1,0:T(8,128)(2,1)S(1)}, bf16[64,8192]{1,0:T(8,128)(2,1)}, u32[]{:S(2)}) copy-start(bf16[64,8192]{1,0:T(8,128)(2,1)} %memory_ref.3) | copy-start | bytes 3145732
  83.1 103.4 %copy-start.2 = (bf16[128,1024]{1,0:T(8,128)(2,1)S(1)}, bf16[128,1024]{1,0:T(8,128)(2,1)}, u32[]{:S(2)}) copy-start(bf16[128,1024]{1,0:T(8,128)(2,1)} %query_up_ref.3) | copy-start | bytes 786436
  83.1 1.1 copy-start.8
  181.2 1.0 copy-start.5
  182.2 0.7 copy-start.11
  182.9 0.7 copy-start.12
